TPU v7x, 256 devices: a whole 4x4x8 slice. The times are simulated.
256 devices in a mesh: ctx: 8 (over z_hi, y), tp: 32 (over x, z_lo, core).
Axes of the slice: x: 4, y: 4, z: 8 (z_hi: 2, z_lo: 4; z = z_hi * 4 + z_lo), core: 2. Of those that a mesh axis runs over, the one named last changes fastest.
Arguments:
- tokens: bfloat16 [4096, 4096], P(('ctx', 'tp')), may hold values from -6 to 6
- gate_weight: bfloat16 [4096, 16384], P(None, 'tp'), may hold values from -0.09375 to 0.09375
- input_weight: bfloat16 [4096, 16384], P(None, 'tp'), may hold values from -0.09375 to 0.09375
- state_weight: bfloat16 [4096, 2048], P(None, 'tp'), may hold values from -0.09375 to 0.09375
- step_weight: bfloat16 [4096, 256], P(None, 'tp'), may hold values from -0.09375 to 0.09375
- input_conv: float32 [5, 16384], P(None, 'tp'), may hold values from -0.5 to 0.5
- state_conv: float32 [5, 2048], P(None, 'tp'), may hold values from -0.5 to 0.5
- log_rate: float32 [256], P('tp'), may hold values from -12 to 2.1
- step_bias: float32 [256], P('tp'), may hold values from -6 to -2
- skip_gain: float32 [256], P('tp'), may hold values from 0.5 to 2
- norm_gain: float32 [16384], P('tp'), may hold values from 0.25 to 1.75
- out_weight: bfloat16 [16384, 4096], P('tp'), may hold values from -0.046875 to 0.046875
Outputs:
- mixed_out: bfloat16 [4096, 4096], P(('ctx', 'tp'))
All inputs are finite; a program needn't handle non-finite values.
Results may differ from a plain program's by a relative error of at most 0.0035.
The roundings to bfloat16 on the way count: a program that leaves them out, or rounds other values in their place, can miss the bound.
Values may be sent and summed in bfloat16 or wider, within the bound.
No kernel may reach another device: no remote copies, remote signals or barrier semaphores. Data moves between devices by JAX's collectives and lax.ppermute only.
A program may use at most 128 MiB of HBM per device.

v0:
```python
import jax
import jax.numpy as jnp
from jax import lax
from jax.experimental import pallas as pl
from jax.experimental.pallas import tpu as pltpu
from jax.sharding import PartitionSpec as P


GROUPS = 4
CONV = 4
DINNER = 16384
F32 = jnp.float32
BF16 = jnp.bfloat16
F16 = jnp.float16
MIB = 1024 * 1024


VM = pl.BlockSpec(memory_space=pltpu.VMEM)
SM = pl.BlockSpec(memory_space=pltpu.SMEM)


def sds(shape, dtype):
    return jax.ShapeDtypeStruct(shape, dtype)


def cost(flops, nbytes):
    return pl.CostEstimate(flops=int(flops), bytes_accessed=int(nbytes), transcendentals=0)


def send(array, axis, to):
    size = lax.axis_size(axis)
    pairs = [(i, to(i)) for i in range(size) if to(i) is not None]
    return lax.ppermute(array, axis, pairs)


def hop(array, to):
    pairs = [(c * 32 + t, to(c, t)) for c in range(8) for t in range(32)]
    pairs = [(i, d[0] * 32 + d[1]) for i, d in pairs if d is not None]
    return lax.ppermute(array, ("ctx", "tp"), pairs)


def flip(array, axis, mask):
    return send(array, axis, lambda i: i ^ mask)


def along_x(array, by):
    return send(array, "tp", lambda i: (i + 8 * by) % 32)


def dot(a, b):
    return lax.dot_general(a, b, (((1,), (0,)), ((), ())), preferred_element_type=F32)


def dot_nt(a, b):
    return lax.dot_general(a, b, (((1,), (1,)), ((), ())), preferred_element_type=F32)


def dot_tn(a, b):
    return lax.dot_general(a, b, (((0,), (0,)), ((), ())), preferred_element_type=F32)


def silu(v):
    return v * jax.nn.sigmoid(v)


def pair_scale(cols, pair):
    rows = cols.shape[0]
    lane = lax.broadcasted_iota(jnp.int32, (rows, 128), 1)
    low = jnp.broadcast_to(cols[:, 2 * pair : 2 * pair + 1], (rows, 128))
    high = jnp.broadcast_to(cols[:, 2 * pair + 1 : 2 * pair + 2], (rows, 128))
    return jnp.where(lane < 64, low, high)


def split(value):
    high = value.astype(BF16)
    return high, (value - high.astype(F32)).astype(BF16)


def project(parts, slots, idx, gate_w, input_w, small_w, bufs):
    depth = parts[0].shape[1]
    steps = 4
    kb = depth // steps
    count = len(slots)
    rows = 128 * count
    weights, wspecs, outs, accs = [], [], [], []
    if gate_w is not None:
        weights.append(gate_w)
        wspecs.append(pl.BlockSpec((kb, 512), lambda k, i: (k, 0)))
        outs.append(sds((512, 512), BF16))
        accs.append(pltpu.VMEM((rows, 512), F32))
    if input_w is not None:
        weights += [input_w, small_w]
        wspecs += [
            pl.BlockSpec((kb, 512), lambda k, i: (k, 0)),
            pl.BlockSpec((256, kb), lambda k, i: (0, k)),
        ]
        outs += [sds((512, 512), BF16), sds((512, 128), BF16), sds((8, 512), F32)]
        accs += [pltpu.VMEM((rows, 512), F32), pltpu.VMEM((rows, 256), F32)]
    nw, no, na = len(weights), len(outs), len(accs)
    aliased = [] if bufs is None else list(bufs)
    ready = [pltpu.VMEM((rows, 512), BF16)] if gate_w is not None else []
    if input_w is not None:
        ready += [pltpu.VMEM((rows, 512), BF16), pltpu.VMEM((rows, 128), BF16), pltpu.VMEM((8, rows), F32)]
        ready += [pltpu.VMEM((rows, 128), F32)]
    nl = len(parts)

    def kernel(i, *refs):
        lrefs, refs = refs[:nl], refs[nl:]
        wrefs, refs = refs[:nw], refs[nw + len(aliased) :]
        orefs, refs = refs[:no], refs[no:]
        arefs, refs = refs[:na], refs[na:]
        rrefs, sem = refs[:-1], refs[-1]
        k = pl.program_id(0)
        lhs = jnp.concatenate([r[...] for r in lrefs], axis=0)
        for n, w in enumerate(wrefs):
            nt = input_w is not None and n == nw - 1
            part = dot_nt(lhs, w[...]) if nt else dot(lhs, w[...])

            @pl.when(k == 0)
            def _():
                arefs[n][...] = part

            @pl.when(k > 0)
            def _():
                arefs[n][...] += part

        @pl.when(k == steps - 1)
        def _():
            copies = []
            for s in range(count):
                for t in range(8):
                    at = slice(s * 128 + t * 16, s * 128 + t * 16 + 16)
                    dst = pl.ds(pl.multiple_of(i[4 + t] * 16, 16) + s * 128, 16)
                    n = 0
                    if gate_w is not None:
                        rrefs[n][dst, :] = arefs[n][at, :].astype(BF16)
                        n += 1
                    if input_w is not None:
                        rrefs[n][dst, :] = arefs[n][at, :].astype(BF16)
                        rrefs[n + 1][dst, :] = arefs[n + 1][at, 0:128].astype(BF16)
                        rrefs[n + 3][dst, :] = arefs[n + 1][at, 128:256]
                here = slice(s * 128, s * 128 + 128)
                if input_w is not None:
                    rrefs[n + 2][:, here] = jnp.transpose(rrefs[n + 3][here, :])[0:8, :]
                there = pl.ds(pl.multiple_of(i[slots[s]] * 128, 128), 128)
                for n in range(no):
                    if n == no - 1 and input_w is not None:
                        source, target = rrefs[n].at[:, here], orefs[n].at[:, there]
                    else:
                        source, target = rrefs[n].at[here, :], orefs[n].at[there, :]
                    copies.append(pltpu.make_async_copy(source, target, sem.at[len(copies)]))
            for copy in copies:
                copy.start()
            for copy in copies:
                copy.wait()

    cols = (512 if gate_w is not None else 0) + (768 if input_w is not None else 0)
    first = 1 + nl + nw
    lspecs = [pl.BlockSpec((p.shape[0], kb), lambda k, i: (0, k)) for p in parts]
    out = pl.pallas_call(
        kernel,
        out_shape=outs,
        grid_spec=pltpu.PrefetchScalarGridSpec(
            num_scalar_prefetch=1,
            grid=(steps,),
            in_specs=lspecs + wspecs + [pl.BlockSpec(memory_space=pl.ANY)] * len(aliased),
            out_specs=[pl.BlockSpec(memory_space=pl.ANY)] * no,
            scratch_shapes=accs + ready + [pltpu.SemaphoreType.DMA((no * count,))],
        ),
        input_output_aliases={first + n: n for n in range(len(aliased))},
        compiler_params=pltpu.CompilerParams(vmem_limit_bytes=14 * MIB),
        cost_estimate=cost(2 * rows * depth * cols, 2 * depth * cols),
    )(idx, *parts, *weights, *aliased)
    return list(out)


def project_resident(parts, halo, slots, idx, input_w, small_w, bufs):
    depth = parts[0].shape[1]
    kb = 1024
    count = len(slots)
    rows = 128 * count
    extra = 0 if halo is None else 16
    lefts = list(parts) + ([] if halo is None else [halo])
    nl = len(lefts)
    outs = [sds((512, 512), BF16), sds((512, 128), BF16), sds((8, 512), F32)]
    ospecs = [pl.BlockSpec(memory_space=pl.ANY)] * 3
    if extra:
        outs.append(sds((16, 640), BF16))
        ospecs.append(VM)
    no = len(outs)
    aliased = [] if bufs is None else list(bufs)

    def kernel(i, *refs):
        lrefs, refs = refs[:nl], refs[nl:]
        w_ref, s_ref = refs[:2]
        refs = refs[2 + len(aliased) :]
        orefs, refs = refs[:no], refs[no:]
        acc, acc_s, main, small, turned, steps, sem = refs

        acc[...] = jnp.zeros_like(acc)
        acc_s[...] = jnp.zeros_like(acc_s)

        def one(k, carry):
            here = pl.ds(pl.multiple_of(k * kb, kb), kb)
            lhs = jnp.concatenate([r[:, here] for r in lrefs], axis=0)
            acc[...] += dot(lhs, w_ref[here, :])
            acc_s[...] += dot_nt(lhs, s_ref[:, here])
            return carry

        lax.fori_loop(0, depth // kb, one, 0)
        copies = []
        for s in range(count):
            for t in range(8):
                at = slice(s * 128 + t * 16, s * 128 + t * 16 + 16)
                dst = pl.ds(pl.multiple_of(i[4 + t] * 16, 16) + s * 128, 16)
                main[dst, :] = acc[at, :].astype(BF16)
                small[dst, :] = acc_s[at, 0:128].astype(BF16)
                turned[dst, :] = acc_s[at, 128:256]
            here = slice(s * 128, s * 128 + 128)
            steps[:, here] = jnp.transpose(turned[here, :])[0:8, :]
            there = pl.ds(pl.multiple_of(i[slots[s]] * 128, 128), 128)
            for source, target in (
                (main.at[here, :], orefs[0].at[there, :]),
                (small.at[here, :], orefs[1].at[there, :]),
                (steps.at[:, here], orefs[2].at[:, there]),
            ):
                copies.append(pltpu.make_async_copy(source, target, sem.at[len(copies)]))
        for copy in copies:
            copy.start()
        if extra:
            orefs[3][:, 0:512] = acc[rows : rows + 16, :].astype(BF16)
            orefs[3][:, 512:640] = acc_s[rows : rows + 16, 0:128].astype(BF16)
        for copy in copies:
            copy.wait()

    first = 1 + nl + 2
    out = pl.pallas_call(
        kernel,
        out_shape=outs,
        in_specs=[SM] + [VM] * (nl + 2) + [pl.BlockSpec(memory_space=pl.ANY)] * len(aliased),
        out_specs=ospecs,
        scratch_shapes=[
            pltpu.VMEM((rows + extra, 512), F32),
            pltpu.VMEM((rows + extra, 256), F32),
            pltpu.VMEM((rows, 512), BF16),
            pltpu.VMEM((rows, 128), BF16),
            pltpu.VMEM((rows, 128), F32),
            pltpu.VMEM((8, rows), F32),
            pltpu.SemaphoreType.DMA((3 * count,)),
        ],
        input_output_aliases={first + n: n for n in range(len(aliased))},
        compiler_params=pltpu.CompilerParams(vmem_limit_bytes=14 * MIB),
        cost_estimate=cost(2 * rows * depth * 768, 2 * depth * 768),
    )(idx, *lefts, input_w, small_w, *aliased)
    return list(out)


def conv_rows(window, taps, rows):
    running = taps[CONV : CONV + 1, :] + taps[0:1, :] * window[13 : 13 + rows, :]
    for k in range(1, CONV):
        running = running + taps[k : k + 1, :] * window[13 + k : 13 + k + rows, :]
    return silu(running)


def conv_states_kernel(idx, rows_ref, halo_ref, taps_ref, out_ref, full):
    taps = taps_ref[...]
    for k in range(4):
        if k == 0:
            window = jnp.concatenate([halo_ref[:, 512:640], rows_ref[0:128, :]], axis=0).astype(F32)
        else:
            window = rows_ref[128 * k - 16 : 128 * k + 128, :].astype(F32)
        full[128 * k : 128 * k + 128, :] = conv_rows(window, taps, 128).astype(BF16)
    half = idx[13]
    out_ref[...] = full[pl.ds(pl.multiple_of(half * 256, 256), 256), :]


def conv_states(idx, rows, halo, taps):
    return pl.pallas_call(
        conv_states_kernel,
        out_shape=sds((256, 128), BF16),
        in_specs=[SM, VM, VM, VM],
        out_specs=VM,
        scratch_shapes=[pltpu.VMEM((512, 128), BF16)],
        compiler_params=pltpu.CompilerParams(vmem_limit_bytes=14 * MIB),
        cost_estimate=cost(2e6, 4e5),
        name="conv_states",
    )(idx, rows, halo, taps)


def columns_of(rows8):
    return jnp.transpose(rows8)


def column(par, start):
    row = lax.broadcasted_iota(jnp.int32, (8, 128), 0)
    out = jnp.zeros((8, 128), F32)
    for h in range(8):
        out = jnp.where(row == h, par[start + h], out)
    return out


def inputs_kernel(par_ref, rows_ref, halo_ref, taps_ref, step_ref, x_ref, hi_ref, lo_ref, dt_ref, cum_ref, weight_ref, longer):
    taps = taps_ref[...]
    rate = jnp.exp(column(par_ref, 0))
    bias = column(par_ref, 8)
    lane = lax.broadcasted_iota(jnp.int32, (8, 128), 1)
    dts, cums = [], []
    for k in range(4):
        raw = step_ref[:, 128 * k : 128 * k + 128] + bias
        dt = jnp.maximum(raw, 0.0) + jnp.log1p(jnp.exp(-jnp.abs(raw)))
        cum = -dt * rate
        for b in range(7):
            moved = pltpu.roll(cum, 1 << b, 1)
            cum = cum + jnp.where(lane >= (1 << b), moved, 0.0)
        dts.append(dt)
        cums.append(cum)
        dt_ref[:, 128 * k : 128 * k + 128] = dt
        cum_ref[:, 128 * k : 128 * k + 128] = cum
    after = jnp.zeros((8, 1), F32)
    for k in reversed(range(4)):
        total = cums[k][:, 127:128]
        weight_ref[:, 128 * k : 128 * k + 128] = jnp.exp(total - cums[k] + after) * dts[k]
        after = after + total
    longer[0:16, :] = halo_ref[:, 0:512]
    longer[16:528, :] = rows_ref[...]

    def one(k, carry):
        start = pl.multiple_of(k * 128, 128)
        here = pl.ds(start, 128)
        cols = columns_of(weight_ref[:, here])
        window = longer[pl.ds(start, 144), :]
        for p in range(4):
            ch = slice(128 * p, 128 * p + 128)
            x = conv_rows(window[:, ch].astype(F32), taps[:, ch], 128).astype(BF16)
            x_ref[here, ch] = x
            hi, lo = split(x.astype(F32) * pair_scale(cols, p))
            hi_ref[here, ch] = hi
            lo_ref[here, ch] = lo
        return carry

    lax.fori_loop(0, 4, one, 0)


def inputs_stage(rows, halo, taps, step, par):
    return pl.pallas_call(
        inputs_kernel,
        out_shape=[sds((512, 512), BF16)] * 3 + [sds((8, 512), F32)] * 2,
        in_specs=[SM] + [VM] * 4,
        out_specs=[VM] * 5,
        scratch_shapes=[pltpu.VMEM((8, 512), F32), pltpu.VMEM((528, 512), BF16)],
        compiler_params=pltpu.CompilerParams(vmem_limit_bytes=14 * MIB),
        cost_estimate=cost(1e7, 2e6),
        name="inputs_stage",
    )(par, rows, halo, taps, step)


def gathered_block(idx, own_ref, oth_ref, block, rows):
    place = lax.bitwise_xor(jnp.int32(block), idx[12])
    return jnp.where(idx[13] == rows, own_ref[place], oth_ref[place])


LOG2 = 0.6931471805599453


def scaled(value):
    most = jnp.max(jnp.abs(value), axis=0, keepdims=True)
    power = jnp.ceil(jnp.log(most) * (1.0 / LOG2))
    power = jnp.minimum(jnp.maximum(power, -100.0), 120.0)
    return value * jnp.exp(power * -LOG2), power


def unscaled(ref_value):
    return ref_value[0:256, :] * jnp.exp(ref_value[256:257, :] * LOG2)


def state_kernel(idx, own_ref, oth_ref, hi_ref, lo_ref, cum_ref, out_ref):
    halves = []
    for n in range(2):
        write = jnp.concatenate(
            [gathered_block(idx, own_ref, oth_ref, n, 0), gathered_block(idx, own_ref, oth_ref, n, 1)], axis=0
        )
        halves.append(write)
    write = jnp.concatenate(halves, axis=1)
    state = dot_tn(write, hi_ref[...]) + dot_tn(write, lo_ref[...])
    total = (
        cum_ref[:, 127:128] + cum_ref[:, 255:256] + cum_ref[:, 383:384] + cum_ref[:, 511:512]
    )
    damp = jnp.maximum(total, -110.0) * 256.0
    lane = lax.broadcasted_iota(jnp.int32, (16, 128), 1)
    row = lax.broadcasted_iota(jnp.int32, (16, 128), 0)
    for q in range(4):
        place = lax.bitwise_xor(jnp.int32(q), idx[14])
        mant, power = scaled(state[:, 128 * q : 128 * q + 128])
        out_ref[place, 0:256, :] = mant
        low = jnp.broadcast_to(damp[2 * q : 2 * q + 1, :], (16, 128))
        high = jnp.broadcast_to(damp[2 * q + 1 : 2 * q + 2, :], (16, 128))
        value = jnp.where(lane < 64, low, high)
        one = value.astype(BF16).astype(F32)
        two = (value - one).astype(BF16).astype(F32)
        three = value - one - two
        packed = jnp.where(row == 1, one, jnp.where(row == 2, two, jnp.where(row == 3, three, 0.0)))
        out_ref[place, 256:272, :] = jnp.where(row == 0, power, packed)


def state_stage(idx, own, oth, hi, lo, cum):
    return pl.pallas_call(
        state_kernel,
        out_shape=sds((4, 272, 128), F32),
        in_specs=[SM] + [VM] * 5,
        out_specs=VM,
        compiler_params=pltpu.CompilerParams(vmem_limit_bytes=14 * MIB),
        cost_estimate=cost(2.7e8, 2e6),
        name="state_stage",
    )(idx, own, oth, hi, lo, cum)


def prefix_kernel(idx, s0, s1, s2, s3, inc_ref, pre_ref, tot_ref):
    place = idx[14]
    odd = lax.bitwise_and(place, 1) == 1
    far = lax.bitwise_and(place, 2) == 2
    slots = [s0[...], s1[...], s2[...], s3[...]]
    a, b = jnp.where(odd, slots[1], slots[0]), jnp.where(odd, slots[0], slots[1])
    c, d = jnp.where(odd, slots[3], slots[2]), jnp.where(odd, slots[2], slots[3])
    ordered = [jnp.where(far, c, a), jnp.where(far, d, b), jnp.where(far, a, c), jnp.where(far, b, d)]
    running = jnp.zeros((256, 128), F32)
    carried = jnp.ones((1, 128), F32)
    for k in range(4):
        inc_ref[k] = running
        pre_ref[k] = jnp.broadcast_to(carried, (8, 128))
        tail = ordered[k][256:272, :]
        damp = jnp.exp((tail[1:2, :] + tail[2:3, :] + tail[3:4, :]) * (1.0 / 256.0))
        running = damp * running + unscaled(ordered[k])
        carried = carried * damp
    mant, power = scaled(running)
    tot_ref[0:256, :] = mant
    tot_ref[256:272, :] = jnp.broadcast_to(power, (16, 128))


def prefix_stage(idx, s0, s1, s2, s3):
    return pl.pallas_call(
        prefix_kernel,
        out_shape=[sds((4, 256, 128), F32), sds((4, 8, 128), F32), sds((272, 128), F32)],
        in_specs=[SM] + [VM] * 4,
        out_specs=[VM] * 3,
        compiler_params=pltpu.CompilerParams(vmem_limit_bytes=14 * MIB),
        cost_estimate=cost(1e6, 1e6),
        name="prefix_stage",
    )(idx, s0, s1, s2, s3)


def spread_kernel(idx, inc_ref, pre_ref, far_ref, out_ref):
    far = jnp.where(idx[15] > 0, unscaled(far_ref[...]), 0.0)
    for k in range(4):
        place = lax.bitwise_xor(jnp.int32(k), idx[14])
        mant, power = scaled(inc_ref[k] + pre_ref[k][0:1, :] * far)
        out_ref[place, 0:256, :] = mant
        out_ref[place, 256:272, :] = jnp.broadcast_to(power, (16, 128))


def spread_stage(idx, inc, pre, far):
    return pl.pallas_call(
        spread_kernel,
        out_shape=sds((4, 272, 128), F32),
        in_specs=[SM] + [VM] * 3,
        out_specs=VM,
        compiler_params=pltpu.CompilerParams(vmem_limit_bytes=14 * MIB),
        cost_estimate=cost(1e6, 1e6),
        name="spread_stage",
    )(idx, inc, pre, far)


def scan_kernel(idx, par_ref, own_ref, oth_ref, x_ref, dt_ref, cum_ref, y_ref, read_ref, state):
    row = lax.broadcasted_iota(jnp.int32, (128, 128), 0)
    col = lax.broadcasted_iota(jnp.int32, (128, 128), 1)
    causal = row >= col
    left = col < 64
    zero = jnp.zeros((128, 128), BF16)
    state[...] = jnp.zeros_like(state)

    def one(k, carry):
        here = pl.ds(pl.multiple_of(k * 128, 128), 128)
        half = lax.div(k, 2)
        sub = pl.ds(pl.multiple_of(lax.rem(k, 2) * 128, 128), 128)

        def part(block):
            place = lax.bitwise_xor(jnp.int32(block), idx[12])
            return jnp.where(idx[13] == half, own_ref[place, sub, :], oth_ref[place, sub, :])

        write = jnp.concatenate([part(0), part(1)], axis=1)
        read = jnp.concatenate([part(2), part(3)], axis=1)
        read_ref[here, :] = read
        scores = dot_nt(read, write)
        cum = cum_ref[:, here]
        dt = dt_ref[:, here]
        cols = columns_of(cum)
        exp_cols = columns_of(jnp.exp(cum))
        total = cum[:, 127:128]
        end_cols = columns_of(jnp.exp(total - cum) * dt)
        damp = jnp.exp(total)
        for p in range(4):
            ch = slice(128 * p, 128 * p + 128)
            x = x_ref[here, ch]
            xf = x.astype(F32)
            mixes = []
            for h in (2 * p, 2 * p + 1):
                gap = jnp.broadcast_to(cols[:, h : h + 1], (128, 128)) - cum[h : h + 1, :]
                damping = jnp.exp(jnp.where(causal, gap, -jnp.inf))
                mixes.append(scores * damping * dt[h : h + 1, :])
            mix = jnp.concatenate(mixes, axis=1)
            both = jnp.concatenate([jnp.where(left, x, zero), jnp.where(left, zero, x)], axis=0)
            mix_hi, mix_lo = split(mix)
            y = dot(mix_hi, both) + dot(mix_lo, both)
            y = y + jnp.where(left[0:1, :], par_ref[16 + 2 * p], par_ref[17 + 2 * p]) * xf
            before = state[:, ch]
            s_hi, s_lo = split(before)
            y_ref[here, ch] = y + pair_scale(exp_cols, p) * (dot(read, s_hi) + dot(read, s_lo))
            in_hi, in_lo = split(xf * pair_scale(end_cols, p))
            keep = jnp.where(
                left[0:1, :],
                jnp.broadcast_to(damp[2 * p : 2 * p + 1, :], (1, 128)),
                jnp.broadcast_to(damp[2 * p + 1 : 2 * p + 2, :], (1, 128)),
            )
            state[:, ch] = keep * before + dot_tn(write, in_hi) + dot_tn(write, in_lo)
        return carry

    lax.fori_loop(0, 4, one, 0)


def scan_stage(idx, own, oth, x, dt, cum, par):
    return pl.pallas_call(
        scan_kernel,
        out_shape=[sds((512, 512), F32), sds((512, 256), BF16)],
        in_specs=[SM] * 2 + [VM] * 5,
        out_specs=[VM] * 2,
        scratch_shapes=[pltpu.VMEM((256, 512), F32)],
        compiler_params=pltpu.CompilerParams(vmem_limit_bytes=14 * MIB),
        cost_estimate=cost(6e9, 3e6),
        name="scan_stage",
    )(idx, par, own, oth, x, dt, cum)


def gate_kernel(idx, y_ref, read_ref, q0, q1, q2, q3, cum_ref, gate_ref, u_ref, ss_ref):
    place = idx[14]
    odd = lax.bitwise_and(place, 1) == 1
    far = lax.bitwise_and(place, 2) == 2
    slots = [q0[...], q1[...], q2[...], q3[...]]
    a, b = jnp.where(odd, slots[1], slots[0]), jnp.where(odd, slots[0], slots[1])
    c, d = jnp.where(odd, slots[3], slots[2]), jnp.where(odd, slots[2], slots[3])
    ordered = [jnp.where(far, c, a), jnp.where(far, d, b), jnp.where(far, a, c), jnp.where(far, b, d)]
    halves = [split(unscaled(v)) for v in ordered]

    def one(k, before):
        here = pl.ds(pl.multiple_of(k * 128, 128), 128)
        cum = cum_ref[:, here]
        cols = columns_of(jnp.exp(cum + before))
        read = read_ref[here, :]
        squares = jnp.zeros((128, 128), F32)
        for p in range(4):
            ch = slice(128 * p, 128 * p + 128)
            carried = dot(read, halves[p][0]) + dot(read, halves[p][1])
            y = y_ref[here, ch] + pair_scale(cols, p) * carried
            u = y * silu(gate_ref[here, ch].astype(F32))
            u_ref[here, ch] = u
            squares = squares + u * u
        ss_ref[pl.ds(k, 1), :] = jnp.sum(jnp.transpose(squares), axis=0, keepdims=True)
        return before + cum[:, 127:128]

    lax.fori_loop(0, 4, one, jnp.zeros((8, 1), F32))


def gate_stage(idx, y, read, quarters, cum, gate):
    return pl.pallas_call(
        gate_kernel,
        out_shape=[sds((512, 512), F32), sds((4, 128), F32)],
        in_specs=[SM] + [VM] * 8,
        out_specs=[VM] * 2,
        compiler_params=pltpu.CompilerParams(vmem_limit_bytes=14 * MIB),
        cost_estimate=cost(2e8, 3e6),
        name="gate_stage",
    )(idx, y, read, *quarters, cum, gate)


def load_kernel(src_ref, dst_ref, sem):
    copy = pltpu.make_async_copy(src_ref, dst_ref, sem)
    copy.start()
    copy.wait()


def load(array):
    return pl.pallas_call(
        load_kernel,
        out_shape=sds(array.shape, array.dtype),
        in_specs=[pl.BlockSpec(memory_space=pltpu.HBM)],
        out_specs=VM,
        scratch_shapes=[pltpu.SemaphoreType.DMA],
        compiler_params=pltpu.CompilerParams(vmem_limit_bytes=8 * MIB),
        cost_estimate=cost(1, 8 * MIB),
        name="load",
    )(array)


def out_block(idx, slots, u, ss, gain, out_w):
    count = len(slots)
    rows = 64 * count

    def kernel(i, u_ref, ss_ref, gain_ref, w_ref, own_ref, oth_ref, lhs):
        for s in range(count):
            place = i[slots[s]]
            mean = ss_ref[pl.ds(place, 1), :] / (DINNER // GROUPS)
            scale = jnp.transpose(jnp.broadcast_to(lax.rsqrt(mean + 1e-05), (128, 128)))
            here = pl.ds(pl.multiple_of(place * 128, 128), 128)
            for p in range(4):
                ch = slice(128 * p, 128 * p + 128)
                normed = (u_ref[here, ch] * scale * gain_ref[:, ch]).astype(BF16)
                for t in range(8):
                    core, tile = t % 2, t // 2
                    at = lax.bitwise_xor(jnp.int32(core), i[13]) * rows + 64 * s + tile * 16
                    lhs[pl.ds(pl.multiple_of(at, 16), 16), ch] = normed[t * 16 : t * 16 + 16, :]

        def one(n, carry):
            here = pl.ds(pl.multiple_of(n * 1024, 1024), 1024)
            part = dot(lhs[...], w_ref[:, here])
            own_ref[:, here] = part[0:rows, :]
            oth_ref[:, here] = part[rows : 2 * rows, :]
            return carry

        lax.fori_loop(0, 4, one, 0)

    return pl.pallas_call(
        kernel,
        out_shape=[sds((rows, 4096), F32)] * 2,
        in_specs=[SM] + [VM] * 4,
        out_specs=[VM] * 2,
        scratch_shapes=[pltpu.VMEM((2 * rows, 512), BF16)],
        compiler_params=pltpu.CompilerParams(vmem_limit_bytes=20 * MIB),
        cost_estimate=cost(4 * rows * 512 * 4096, 6e6),
        name="out_block",
    )(idx, u, ss, gain, out_w)


def body(
    tokens,
    gate_weight,
    input_weight,
    state_weight,
    step_weight,
    input_conv,
    state_conv,
    log_rate,
    step_bias,
    skip_gain,
    norm_gain,
    out_weight,
):
    me = lax.axis_index("tp")
    x, zl, core = me // 8, (me // 2) % 4, me % 2
    y, later = lax.axis_index("ctx") % 4, lax.axis_index("ctx") // 4
    n = jnp.arange(16, dtype=jnp.int32)
    turn = jnp.where(n == 1, 3, jnp.where(n == 2, 1, jnp.where(n == 3, 2, 0)))
    tile = n - 4
    where = jnp.bitwise_xor(tile % 4, zl) * 2 + jnp.bitwise_xor(tile // 4, core)
    idx = jnp.where(n < 4, (x + turn) % 4, where)
    idx = jnp.where(n == 12, zl, jnp.where(n == 13, core, jnp.where(n == 14, y, jnp.where(n == 15, later, idx))))
    idx = idx.astype(jnp.int32)

    state_rows_w = state_weight.T
    state_pair = flip(state_rows_w, "tp", 1)
    taps_pair = flip(state_conv, "tp", 1)
    low = core == 0
    first = jnp.where(low, state_rows_w, state_pair)
    second = jnp.where(low, state_pair, state_rows_w)
    small_w = jnp.concatenate([first, second, step_weight.T, jnp.zeros((120, tokens.shape[1]), BF16)], axis=0)
    state_taps = jnp.concatenate(
        [jnp.where(low, state_conv, taps_pair), jnp.where(low, taps_pair, state_conv)], axis=1
    )
    par = jnp.concatenate([log_rate, step_bias, skip_gain])

    tiles = [tokens] + [flip(tokens, "tp", 2 * s) for s in (1, 2, 3)]
    mine = jnp.concatenate(tiles, axis=0)
    right = along_x(mine, 1)
    left = along_x(mine, -1)
    mine_other = flip(mine, "tp", 1)
    last = lax.dynamic_index_in_dim(mine.reshape(4, 16, mine.shape[1]), 3 - zl, 0, False)[8:]
    before_all = {"h0": lambda c, t: (c + 1, t) if c < 7 and t >= 24 and t % 2 else None}
    before_all["h1"] = lambda c, t: (c, t - 24) if t >= 24 and t % 2 else None
    before_all["h2"] = lambda c, t: (c, t - 8) if t >= 24 and t % 2 else ((c, t + 8) if t < 8 and t % 2 else None)
    before_all["h3"] = lambda c, t: (c, t - 1) if t % 2 else None
    rim = hop(last, before_all["h0"])
    bufs = project_resident([mine, mine_other], None, [0], idx, input_weight, small_w, None)
    rim = rim + hop(rim, before_all["h1"])
    far_a = along_x(right[:32], 1)
    far_b = along_x(left[32:], -1)
    right_other = flip(right, "tp", 1)
    left_other = flip(left, "tp", 1)
    rim = rim + hop(rim, before_all["h2"])
    bufs = project_resident(
        [right, right_other, left, left_other], None, [1, 2], idx, input_weight, small_w, bufs
    )
    rim = rim + hop(rim, before_all["h3"])
    rim = jnp.concatenate([jnp.zeros_like(rim), rim], axis=0)
    far_a_other = flip(far_a, "tp", 1)
    far_b_other = flip(far_b, "tp", 1)
    fars = [far_a, far_b, far_a_other, far_b_other]
    input_rows, state_rows, step_raw, halo = project_resident(
        fars, rim, [3], idx, input_weight, small_w, bufs
    )

    piece = conv_states(idx, state_rows, halo, state_taps)
    pieces = jnp.stack([piece] + [flip(piece, "tp", 2 * s) for s in (1, 2, 3)])
    pieces_other = flip(pieces, "tp", 1)

    xs, x_hi, x_lo, dt, cum = inputs_stage(input_rows, halo, input_conv, step_raw, par)
    payload = state_stage(idx, pieces, pieces_other, x_hi, x_lo, cum)
    ends = [payload[0]] + [half_flip(payload[s], s) for s in (1, 2, 3)]
    y_local, read_vec = scan_stage(idx, pieces, pieces_other, xs, dt, cum, par)
    inc, pre, total = prefix_stage(idx, *ends)
    before = half_flip(total, 4)
    everything = [mine, mine_other, right, right_other, left, left_other] + fars
    (gate_rows,) = project(everything, [0, 1, 2, 3], idx, gate_weight, None, None, None)
    spread = spread_stage(idx, inc, pre, before)
    quarters = [spread[0]] + [half_flip(spread[s], s) for s in (1, 2, 3)]
    u, squares = gate_stage(idx, y_local, read_vec, quarters, cum, gate_rows)

    squares = squares + flip(squares, "tp", 1)
    squares = squares + flip(squares, "tp", 2)
    squares = squares + flip(squares, "tp", 4)

    gain = norm_gain.reshape(1, 512)
    out_w = load(out_weight)
    far_own, far_oth = out_block(idx, [3], u, squares, gain, out_w)
    far_sum = swap_add(far_own, far_oth)
    got_a = along_x(narrow(far_sum[:32]), 1)
    got_b = along_x(narrow(far_sum[32:]), -1)
    rest_own, rest_oth = out_block(idx, [2, 1, 0], u, squares, gain, out_w)
    rest = swap_add(rest_own, rest_oth)
    ahead_sum, behind_sum, mine_sum = rest[:64], rest[64:128], rest[128:]
    to_right = narrow(jnp.concatenate([ahead_sum[:32] + widen(got_a), ahead_sum[32:]], axis=0))
    to_left = narrow(jnp.concatenate([behind_sum[:32], behind_sum[32:] + widen(got_b)], axis=0))
    from_left = along_x(to_right, 1)
    from_right = along_x(to_left, -1)
    both_sums = mine_sum + widen(from_left) + widen(from_right)
    block = both_sums.reshape(4, 16, 4096)
    out = lax.dynamic_index_in_dim(block, zl, 0, False)
    for s in (1, 2, 3):
        part = narrow(lax.dynamic_index_in_dim(block, jnp.bitwise_xor(zl, s), 0, False))
        part = flip(part, "tp", 2 * s)
        out = out + widen(part)
    return out.astype(BF16)


def half_flip(value, mask):
    return flip(value.astype(F16), "ctx", mask).astype(F32)


def narrow(value):
    return (value * 32.0).astype(F16)


def widen(value):
    return value.astype(F32) * 0.03125


def swap_add(own, other):
    return own + widen(flip(narrow(other), "tp", 1))


def solution(mesh):
    placed = (
        P(("ctx", "tp"), None),
        P(None, "tp"),
        P(None, "tp"),
        P(None, "tp"),
        P(None, "tp"),
        P(None, "tp"),
        P(None, "tp"),
        P("tp"),
        P("tp"),
        P("tp"),
        P("tp"),
        P("tp", None),
    )

    return jax.shard_map(
        body, mesh=mesh, in_specs=placed, out_specs=P(("ctx", "tp"), None), check_vma=False
    )
```

profile of v0, /device:TPU:38, one launch (start us, length us, event | category | flops | bytes accessed | tf_op | source)
XLA Modules:
  0.0 171.9 jit_solution(1580782176960925737)
XLA Ops:
  0.1 3.3 %collective-permute-start.1 = (bf16[16,4096]{1,0:T(8,128)(2,1)}, bf16[16,4096]{1,0:T(8,128)(2,1)S(1)}, u32[]{:S(2)}, u32[]{:S(2)}) collective-permute-start(bf16[16,4096]{1,0:T(8,128)(2,1)} %param.12), channel_id=1, source_target_pairs={{0,4},{1,5},{2,6},{3,7},{4,0},{5,1},{6,2},{7,3},{8,12},{9,13},{10,... | collective-permute-start | bytes 393224 | tf_op jit(solution)/shard_map/ppermute | solution.py:33
  5.5 7.7 %collective-permute-done.1 = bf16[16,4096]{1,0:T(8,128)(2,1)S(1)} collective-permute-done((bf16[16,4096]{1,0:T(8,128)(2,1)}, bf16[16,4096]{1,0:T(8,128)(2,1)S(1)}, u32[]{:S(2)}, u32[]{:S(2)}) %collective-permute-start.1) | collective-permute-done | bytes 131104 | tf_op jit(solution)/shard_map/ppermute | solution.py:33
  13.2 2.5 %collective-permute-done.2 = bf16[16,4096]{1,0:T(8,128)(2,1)S(1)} collective-permute-done((bf16[16,4096]{1,0:T(8,128)(2,1)}, bf16[16,4096]{1,0:T(8,128)(2,1)S(1)}, u32[]{:S(2)}, u32[]{:S(2)}) %collective-permute-start.2) | collective-permute-done | bytes 131104 | tf_op jit(solution)/shard_map/ppermute | solution.py:33
  23.1 7.2 %collective-permute-start.16 = (bf16[64,4096]{1,0:T(8,128)(2,1)S(1)}, bf16[64,4096]{1,0:T(8,128)(2,1)S(1)}, u32[]{:S(2)}, u32[]{:S(2)}) collective-permute-start(bf16[64,4096]{1,0:T(8,128)(2,1)S(1)} %constant_dynamic-update-slice_fusion.refs_0_), channel_id=1, source_target_pairs={{0,1},{1,0},{2,3},{3,2},{4,5},{5,4},{6,7},{7,6},{8,9},{9,8},{10,11... | collective-permute-start | bytes 1572872 | tf_op jit(solution)/shard_map/ppermute | solution.py:33
  31.0 3.8 %collective-permute-start.4 = (bf16[32,4096]{1,0:T(8,128)(2,1)S(1)}, bf16[32,4096]{1,0:T(8,128)(2,1)S(1)}, u32[]{:S(2)}, u32[]{:S(2)}) collective-permute-start(bf16[32,4096]{1,0:T(8,128)(2,1)S(1)} %slice.88), channel_id=1, source_target_pairs={{0,8},{1,9},{2,10},{3,11},{4,12},{5,13},{6,14},{7,15},{8,16},{9,17... | collective-permute-start | bytes 786440 | tf_op jit(solution)/shard_map/ppermute | solution.py:33
  35.6 5.1 %collective-permute-done.4.refs_0_.refs_6_ = bf16[32,4096]{1,0:T(8,128)(2,1)S(1)} collective-permute-done((bf16[32,4096]{1,0:T(8,128)(2,1)S(1)}, bf16[32,4096]{1,0:T(8,128)(2,1)S(1)}, u32[]{:S(2)}, u32[]{:S(2)}) %collective-permute-start.4) | collective-permute-done | bytes 262176 | tf_op jit(solution)/shard_map/ppermute | solution.py:33
  40.7 3.5 %collective-permute-done.6.refs_1_.refs_7_ = bf16[32,4096]{1,0:T(8,128)(2,1)S(1)} collective-permute-done((bf16[32,4096]{1,0:T(8,128)(2,1)S(1)}, bf16[32,4096]{1,0:T(8,128)(2,1)S(1)}, u32[]{:S(2)}, u32[]{:S(2)}) %collective-permute-start.6) | collective-permute-done | bytes 262176 | tf_op jit(solution)/shard_map/ppermute | solution.py:33
  44.6 2.8 %shard_map.118 = (bf16[512,512]{1,0:T(8,128)(2,1)S(1)}, bf16[512,128]{1,0:T(8,128)(2,1)S(1)}, f32[8,512]{1,0:T(8,128)S(1)}) custom-call(s32[16]{0:T(128)S(1)} %compare_select_fusion.9.i.idx, bf16[64,4096]{1,0:T(8,128)(2,1)S(1)} %constant_dynamic-update-slice_fusion.refs_0_, bf16[64,4096]{1,0:T(8,128)(2,1)S(1)} %collective-permute-done.16.refs_1_, ...), custom_call_target="tpu_custom_call" | custom-call | flops 805306368 | bytes 6291456 | tf_op jit(solution)/shard_map/pallas_call | solution.py:237
  47.4 3.5 %shard_map.119 = (bf16[512,512]{1,0:T(8,128)(2,1)S(1)}, bf16[512,128]{1,0:T(8,128)(2,1)S(1)}, f32[8,512]{1,0:T(8,128)S(1)}) custom-call(s32[16]{0:T(128)S(1)} %compare_select_fusion.9.i.idx, bf16[64,4096]{1,0:T(8,128)(2,1)S(1)} %collective-permute-done.3.refs_0_.refs_2_, ...), custom_call_target="tpu_custom_call", output_to_operand_aliasing={{0}: (7, {}), {1}: (8, {}), {2}: (9, {})} | custom-call | flops 1610612736 | bytes 6291456 | tf_op jit(solution)/shard_map/pallas_call | solution.py:237
  51.0 2.9 %shard_map.120 = (bf16[512,512]{1,0:T(8,128)(2,1)S(1)}, bf16[512,128]{1,0:T(8,128)(2,1)S(1)}, f32[8,512]{1,0:T(8,128)S(1)}, bf16[16,640]{1,0:T(8,128)(2,1)S(1)}) custom-call(s32[16]{0:T(128)S(1)} %compare_select_fusion.9.i.idx, ...), custom_call_target="tpu_custom_call", output_to_operand_aliasing={{0}: (8, {}), {1}: (9, {}), {2}: (10, {})} | custom-call | flops 805306368 | bytes 6291456 | tf_op jit(solution)/shard_map/pallas_call | solution.py:237
  54.7 3.0 %collective-permute-start.19 = (bf16[256,128]{1,0:T(8,128)(2,1)S(1)}, bf16[256,128]{1,0:T(8,128)(2,1)S(1)}, u32[]{:S(2)}, u32[]{:S(2)}) collective-permute-start(bf16[256,128]{1,0:T(8,128)(2,1)S(1)} %conv_states.1), channel_id=1, source_target_pairs={{0,4},{1,5},{2,6},{3,7},{4,0},{5,1},{6,2},{7,3},{8,12},{9,13},{10,... | collective-permute-start | bytes 196616 | tf_op jit(solution)/shard_map/ppermute | solution.py:33
  59.4 3.1 %collective-permute-done.19 = bf16[256,128]{1,0:T(8,128)(2,1)S(1)} collective-permute-done((bf16[256,128]{1,0:T(8,128)(2,1)S(1)}, bf16[256,128]{1,0:T(8,128)(2,1)S(1)}, u32[]{:S(2)}, u32[]{:S(2)}) %collective-permute-start.19) | collective-permute-done | bytes 65568 | tf_op jit(solution)/shard_map/ppermute | solution.py:33
  64.9 3.4 %inputs_stage.1 = (bf16[512,512]{1,0:T(8,128)(2,1)S(1)}, bf16[512,512]{1,0:T(8,128)(2,1)S(1)}, bf16[512,512]{1,0:T(8,128)(2,1)S(1)}, f32[8,512]{1,0:T(8,128)S(1)}, f32[8,512]{1,0:T(8,128)S(1)}) custom-call(f32[24]{0:T(128)S(1)} %pad_maximum_fusion.2.par_ref, bf16[512,512]{1,0:T(8,128)(2,1)S(1)} %get-tuple-element.39.rows_ref, ...), custom_call_target="tpu_custom_call" | custom-call | flops 10000000 | bytes 2000000 | tf_op jit(solution)/shard_map/inputs_stage/pallas_call | solution.py:345
  68.4 5.0 %shard_map.121.gate_ref = bf16[512,512]{1,0:T(8,128)(2,1)S(1)} custom-call(s32[16]{0:T(128)S(1)} %compare_select_fusion.9.i.idx, bf16[64,4096]{1,0:T(8,128)(2,1)S(1)} %constant_dynamic-update-slice_fusion.refs_0_, bf16[64,4096]{1,0:T(8,128)(2,1)S(1)} %collective-permute-done.16.refs_1_, bf16[64,4096]{1,0:T(8,128)(2,1)S(1)} %collective-permute-done.3.refs_0_.refs_2_, ...), custom_call_target="tpu_custom_call" | custom-call | flops 2147483648 | bytes 4194304 | tf_op jit(solution)/shard_map/pallas_call | solution.py:160
  76.1 3.9 %collective-permute-start.23 = (f16[272,128]{1,0:T(8,128)(2,1)S(1)}, f16[272,128]{1,0:T(8,128)(2,1)S(1)}, u32[]{:S(2)}, u32[]{:S(2)}) collective-permute-start(f16[272,128]{1,0:T(8,128)(2,1)S(1)} %get-tuple-element.72), channel_id=1, source_target_pairs={{0,64},{32,96},{64,0},{96,32},{128,192},{160,224},{192,128},{224,1... | collective-permute-start | bytes 208904 | tf_op jit(solution)/shard_map/ppermute | solution.py:33
  80.0 4.0 %collective-permute-done.23 = f16[272,128]{1,0:T(8,128)(2,1)S(1)} collective-permute-done((f16[272,128]{1,0:T(8,128)(2,1)S(1)}, f16[272,128]{1,0:T(8,128)(2,1)S(1)}, u32[]{:S(2)}, u32[]{:S(2)}) %collective-permute-start.23) | collective-permute-done | bytes 69664 | tf_op jit(solution)/shard_map/ppermute | solution.py:33
  86.3 5.6 %collective-permute-start.25 = (f16[272,128]{1,0:T(8,128)(2,1)S(1)}, f16[272,128]{1,0:T(8,128)(2,1)S(1)}, u32[]{:S(2)}, u32[]{:S(2)}) collective-permute-start(f16[272,128]{1,0:T(8,128)(2,1)S(1)} %convert_element_type.120), channel_id=1, source_target_pairs={{0,128},{32,160},{64,192},{96,224},{128,0},{160,32},{192,64},{224,... | collective-permute-start | bytes 208904 | tf_op jit(solution)/shard_map/ppermute | solution.py:33
  91.9 4.2 %scan_stage.1 = (f32[512,512]{1,0:T(8,128)S(1)}, bf16[512,256]{1,0:T(8,128)(2,1)S(1)}) custom-call(s32[16]{0:T(128)S(1)} %compare_select_fusion.9.i.idx, f32[24]{0:T(128)S(1)} %pad_maximum_fusion.2.par_ref, bf16[4,256,128]{2,1,0:T(8,128)(2,1)S(1)} %pad_maximum_fusion.own_ref, bf16[4,256,128]{2,1,0:T(8,128)(2,1)S(1)} %collective-permute-done.21.oth_ref, ...), custom_call_target="tpu_custom_call" | custom-call | flops 6000000000 | bytes 3000000 | tf_op jit(solution)/shard_map/scan_stage/pallas_call | solution.py:530
  97.2 3.8 %collective-permute-start.27 = (f16[272,128]{1,0:T(8,128)(2,1)S(1)}, f16[272,128]{1,0:T(8,128)(2,1)S(1)}, u32[]{:S(2)}, u32[]{:S(2)}) collective-permute-start(f16[272,128]{1,0:T(8,128)(2,1)S(1)} %get-tuple-element.69), channel_id=1, source_target_pairs={{0,64},{32,96},{64,0},{96,32},{128,192},{160,224},{192,128},{224,1... | collective-permute-start | bytes 208904 | tf_op jit(solution)/shard_map/ppermute | solution.py:33
  101.7 2.4 %collective-permute-done.27 = f16[272,128]{1,0:T(8,128)(2,1)S(1)} collective-permute-done((f16[272,128]{1,0:T(8,128)(2,1)S(1)}, f16[272,128]{1,0:T(8,128)(2,1)S(1)}, u32[]{:S(2)}, u32[]{:S(2)}) %collective-permute-start.27) | collective-permute-done | bytes 69664 | tf_op jit(solution)/shard_map/ppermute | solution.py:33
  104.1 2.4 %collective-permute-done.28 = f16[272,128]{1,0:T(8,128)(2,1)S(1)} collective-permute-done((f16[272,128]{1,0:T(8,128)(2,1)S(1)}, f16[272,128]{1,0:T(8,128)(2,1)S(1)}, u32[]{:S(2)}, u32[]{:S(2)}) %collective-permute-start.28) | collective-permute-done | bytes 69664 | tf_op jit(solution)/shard_map/ppermute | solution.py:33
  106.5 3.0 %gate_stage.1 = (f32[512,512]{1,0:T(8,128)S(1)}, f32[4,128]{1,0:T(4,128)S(1)}) custom-call(s32[16]{0:T(128)S(1)} %compare_select_fusion.9.i.idx, f32[512,512]{1,0:T(8,128)S(1)} %get-tuple-element.44.y_ref, bf16[512,256]{1,0:T(8,128)(2,1)S(1)} %get-tuple-element.45.read_ref, f32[272,128]{1,0:T(8,128)S(1)} %slice_bitcast_fusion.q0, ...), custom_call_target="tpu_custom_call" | custom-call | flops 200000000 | bytes 3000000 | tf_op jit(solution)/shard_map/gate_stage/pallas_call | solution.py:572
  111.4 3.1 %collective-permute-done.30 = f32[4,128]{1,0:T(4,128)S(1)} collective-permute-done((f32[4,128]{1,0:T(4,128)S(1)}, f32[4,128]{1,0:T(4,128)S(1)}, u32[]{:S(2)}, u32[]{:S(2)}) %collective-permute-start.30) | collective-permute-done | bytes 2080 | tf_op jit(solution)/shard_map/ppermute | solution.py:33
  115.7 3.2 %collective-permute-done.31 = f32[4,128]{1,0:T(4,128)S(1)} collective-permute-done((f32[4,128]{1,0:T(4,128)S(1)}, f32[4,128]{1,0:T(4,128)S(1)}, u32[]{:S(2)}, u32[]{:S(2)}) %collective-permute-start.31) | collective-permute-done | bytes 2080 | tf_op jit(solution)/shard_map/ppermute | solution.py:33
  120.9 3.0 %out_block.2 = (f32[192,4096]{1,0:T(8,128)S(1)}, f32[192,4096]{1,0:T(8,128)S(1)}) custom-call(s32[16]{0:T(128)S(1)} %compare_select_fusion.9.i.idx, f32[512,512]{1,0:T(8,128)S(1)} %get-tuple-element.51.u_ref, f32[4,128]{1,0:T(4,128)S(1)} %add.113.ss_ref, f32[1,512]{1,0:T(1,128)S(1)} %bitcast.46, bf16[512,4096]{1,0:T(8,128)(2,1)S(1)} %load.1.w_ref), custom_call_target="tpu_custom_call" | custom-call | flops 1610612736 | bytes 6000000 | tf_op jit(solution)/shard_map/out_block/pallas_call | solution.py:629
  129.1 5.8 %collective-permute-done.34 = f16[32,4096]{1,0:T(8,128)(2,1)S(1)} collective-permute-done((f16[32,4096]{1,0:T(8,128)(2,1)S(1)}, f16[32,4096]{1,0:T(8,128)(2,1)S(1)}, u32[]{:S(2)}, u32[]{:S(2)}) %collective-permute-start.34) | collective-permute-done | bytes 262176 | tf_op jit(solution)/shard_map/ppermute | solution.py:33
  140.7 10.2 %collective-permute-done.35 = f16[64,4096]{1,0:T(8,128)(2,1)} collective-permute-done((f16[64,4096]{1,0:T(8,128)(2,1)}, f16[64,4096]{1,0:T(8,128)(2,1)}, u32[]{:S(2)}, u32[]{:S(2)}) %collective-permute-start.35) | collective-permute-done | bytes 524320 | tf_op jit(solution)/shard_map/ppermute | solution.py:33
  151.0 2.4 %collective-permute-done.37 = f16[64,4096]{1,0:T(8,128)(2,1)} collective-permute-done((f16[64,4096]{1,0:T(8,128)(2,1)}, f16[64,4096]{1,0:T(8,128)(2,1)}, u32[]{:S(2)}, u32[]{:S(2)}) %collective-permute-start.37) | collective-permute-done | bytes 524320 | tf_op jit(solution)/shard_map/ppermute | solution.py:33
  153.4 2.4 %fusion = f32[64,4096]{1,0:T(8,128)} fusion(f32[192,4096]{1,0:T(8,128)S(1)} %multiply_add_fusion, f16[64,4096]{1,0:T(8,128)(2,1)} %collective-permute-done.37, f16[64,4096]{1,0:T(8,128)(2,1)} %collective-permute-done.35), kind=kLoop, calls=%fused_computation.4 | loop fusion | flops 1572864 | bytes 3145728 | tf_op jit(solution)/shard_map/add | solution.py:741
  160.5 2.9 %collective-permute-done.38 = f16[16,4096]{1,0:T(8,128)(2,1)S(1)} collective-permute-done((f16[16,4096]{1,0:T(8,128)(2,1)S(1)}, f16[16,4096]{1,0:T(8,128)(2,1)S(1)}, u32[]{:S(2)}, u32[]{:S(2)}) %collective-permute-start.38) | collective-permute-done | bytes 131104 | tf_op jit(solution)/shard_map/ppermute | solution.py:33
  163.4 3.7 %collective-permute-done.39 = f16[16,4096]{1,0:T(8,128)(2,1)S(1)} collective-permute-done((f16[16,4096]{1,0:T(8,128)(2,1)S(1)}, f16[16,4096]{1,0:T(8,128)(2,1)S(1)}, u32[]{:S(2)}, u32[]{:S(2)}) %collective-permute-start.39) | collective-permute-done | bytes 131104 | tf_op jit(solution)/shard_map/ppermute | solution.py:33
  167.1 3.1 %collective-permute-done.40 = f16[16,4096]{1,0:T(8,128)(2,1)S(1)} collective-permute-done((f16[16,4096]{1,0:T(8,128)(2,1)S(1)}, f16[16,4096]{1,0:T(8,128)(2,1)S(1)}, u32[]{:S(2)}, u32[]{:S(2)}) %collective-permute-start.40) | collective-permute-done | bytes 131104 | tf_op jit(solution)/shard_map/ppermute | solution.py:33
  (132 shorter events, 45.4 us)
Async XLA Ops:
  0.0 5.4 %collective-permute-start = (bf16[16,4096]{1,0:T(8,128)(2,1)}, bf16[16,4096]{1,0:T(8,128)(2,1)S(1)}, u32[]{:S(2)}, u32[]{:S(2)}) collective-permute-start(bf16[16,4096]{1,0:T(8,128)(2,1)} %param.12), channel_id=1, source_target_pairs={{0,2},{1,3},{2,0},{3,1},{4,6},{5,7},{6,4},{7,5},{8,10},{9,11},{10,... | collective-permute-start | bytes 393224 | tf_op jit(solution)/shard_map/ppermute | solution.py:33
  0.1 13.1 %collective-permute-start.1 = (bf16[16,4096]{1,0:T(8,128)(2,1)}, bf16[16,4096]{1,0:T(8,128)(2,1)S(1)}, u32[]{:S(2)}, u32[]{:S(2)}) collective-permute-start(bf16[16,4096]{1,0:T(8,128)(2,1)} %param.12), channel_id=1, source_target_pairs={{0,4},{1,5},{2,6},{3,7},{4,0},{5,1},{6,2},{7,3},{8,12},{9,13},{10,... | collective-permute-start | bytes 393224 | tf_op jit(solution)/shard_map/ppermute | solution.py:33
  3.4 12.3 %collective-permute-start.2 = (bf16[16,4096]{1,0:T(8,128)(2,1)}, bf16[16,4096]{1,0:T(8,128)(2,1)S(1)}, u32[]{:S(2)}, u32[]{:S(2)}) collective-permute-start(bf16[16,4096]{1,0:T(8,128)(2,1)} %param.12), channel_id=1, source_target_pairs={{0,6},{1,7},{2,4},{3,5},{4,2},{5,3},{6,0},{7,1},{8,14},{9,15},{10,... | collective-permute-start | bytes 393224 | tf_op jit(solution)/shard_map/ppermute | solution.py:33
  3.8 31.1 %collective-permute-start.13 = (bf16[64,4096]{1,0:T(8,128)(2,1)}, bf16[64,4096]{1,0:T(8,128)(2,1)S(1)}, u32[]{:S(2)}, u32[]{:S(2)}) collective-permute-start(bf16[64,4096]{1,0:T(8,128)(2,1)} %bitcast.47), channel_id=1, source_target_pairs={{0,1},{1,0},{2,3},{3,2},{4,5},{5,4},{6,7},{7,6},{8,9},{9,8},{10,11... | collective-permute-start | bytes 1572872 | tf_op jit(solution)/shard_map/ppermute | solution.py:33
  15.7 15.3 %collective-permute-start.3 = (bf16[64,4096]{1,0:T(8,128)(2,1)S(1)}, bf16[64,4096]{1,0:T(8,128)(2,1)S(1)}, u32[]{:S(2)}, u32[]{:S(2)}) collective-permute-start(bf16[64,4096]{1,0:T(8,128)(2,1)S(1)} %constant_dynamic-update-slice_fusion.refs_0_), channel_id=1, source_target_pairs={{0,8},{1,9},{2,10},{3,11},{4,12},{5,13},{6,14},{7,15},{8,16},{9,17... | collective-permute-start | bytes 1572872 | tf_op jit(solution)/shard_map/ppermute | solution.py:33
  16.3 18.5 %collective-permute-start.5 = (bf16[64,4096]{1,0:T(8,128)(2,1)S(1)}, bf16[64,4096]{1,0:T(8,128)(2,1)S(1)}, u32[]{:S(2)}, u32[]{:S(2)}) collective-permute-start(bf16[64,4096]{1,0:T(8,128)(2,1)S(1)} %constant_dynamic-update-slice_fusion.refs_0_), channel_id=1, source_target_pairs={{0,24},{1,25},{2,26},{3,27},{4,28},{5,29},{6,30},{7,31},{8,0},{9,1... | collective-permute-start | bytes 1572872 | tf_op jit(solution)/shard_map/ppermute | solution.py:33
  21.8 9.2 %collective-permute-start.12 = (bf16[8,4096]{1,0:T(8,128)(2,1)S(1)}, bf16[8,4096]{1,0:T(8,128)(2,1)S(1)}, u32[]{:S(2)}, u32[]{:S(2)}) collective-permute-start(bf16[8,4096]{1,0:T(8,128)(2,1)S(1)} %add.109), channel_id=1, source_target_pairs={{1,0},{3,2},{5,4},{7,6},{9,8},{11,10},{13,12},{15,14},{17,16},{19,... | collective-permute-start | bytes 196616 | tf_op jit(solution)/shard_map/ppermute | solution.py:39
  23.1 21.4 %collective-permute-start.16 = (bf16[64,4096]{1,0:T(8,128)(2,1)S(1)}, bf16[64,4096]{1,0:T(8,128)(2,1)S(1)}, u32[]{:S(2)}, u32[]{:S(2)}) collective-permute-start(bf16[64,4096]{1,0:T(8,128)(2,1)S(1)} %constant_dynamic-update-slice_fusion.refs_0_), channel_id=1, source_target_pairs={{0,1},{1,0},{2,3},{3,2},{4,5},{5,4},{6,7},{7,6},{8,9},{9,8},{10,11... | collective-permute-start | bytes 1572872 | tf_op jit(solution)/shard_map/ppermute | solution.py:33
  31.0 9.7 %collective-permute-start.4 = (bf16[32,4096]{1,0:T(8,128)(2,1)S(1)}, bf16[32,4096]{1,0:T(8,128)(2,1)S(1)}, u32[]{:S(2)}, u32[]{:S(2)}) collective-permute-start(bf16[32,4096]{1,0:T(8,128)(2,1)S(1)} %slice.88), channel_id=1, source_target_pairs={{0,8},{1,9},{2,10},{3,11},{4,12},{5,13},{6,14},{7,15},{8,16},{9,17... | collective-permute-start | bytes 786440 | tf_op jit(solution)/shard_map/ppermute | solution.py:33
  34.8 9.4 %collective-permute-start.6 = (bf16[32,4096]{1,0:T(8,128)(2,1)S(1)}, bf16[32,4096]{1,0:T(8,128)(2,1)S(1)}, u32[]{:S(2)}, u32[]{:S(2)}) collective-permute-start(bf16[32,4096]{1,0:T(8,128)(2,1)S(1)} %slice.89), channel_id=1, source_target_pairs={{0,24},{1,25},{2,26},{3,27},{4,28},{5,29},{6,30},{7,31},{8,0},{9,1... | collective-permute-start | bytes 786440 | tf_op jit(solution)/shard_map/ppermute | solution.py:33
  35.0 12.3 %collective-permute-start.14 = (bf16[64,4096]{1,0:T(8,128)(2,1)S(1)}, bf16[64,4096]{1,0:T(8,128)(2,1)S(1)}, u32[]{:S(2)}, u32[]{:S(2)}) collective-permute-start(bf16[64,4096]{1,0:T(8,128)(2,1)S(1)} %collective-permute-done.3.refs_0_.refs_2_), channel_id=1, source_target_pairs={{0,1},{1,0},{2,3},{3,2},{4,5},{5,4},{6,7},{7,6},{8,9},{9,8},{10,11... | collective-permute-start | bytes 1572872 | tf_op jit(solution)/shard_map/ppermute | solution.py:33
  35.1 12.2 %collective-permute-start.15 = (bf16[64,4096]{1,0:T(8,128)(2,1)S(1)}, bf16[64,4096]{1,0:T(8,128)(2,1)S(1)}, u32[]{:S(2)}, u32[]{:S(2)}) collective-permute-start(bf16[64,4096]{1,0:T(8,128)(2,1)S(1)} %collective-permute-done.5.refs_2_.refs_4_), channel_id=1, source_target_pairs={{0,1},{1,0},{2,3},{3,2},{4,5},{5,4},{6,7},{7,6},{8,9},{9,8},{10,11... | collective-permute-start | bytes 1572872 | tf_op jit(solution)/shard_map/ppermute | solution.py:33
  40.7 10.2 %collective-permute-start.7 = (bf16[32,4096]{1,0:T(8,128)(2,1)S(1)}, bf16[32,4096]{1,0:T(8,128)(2,1)S(1)}, u32[]{:S(2)}, u32[]{:S(2)}) collective-permute-start(bf16[32,4096]{1,0:T(8,128)(2,1)S(1)} %collective-permute-done.4.refs_0_.refs_6_), channel_id=1, source_target_pairs={{0,1},{1,0},{2,3},{3,2},{4,5},{5,4},{6,7},{7,6},{8,9},{9,8},{10,11... | collective-permute-start | bytes 786440 | tf_op jit(solution)/shard_map/ppermute | solution.py:33
  44.2 6.7 %collective-permute-start.8 = (bf16[32,4096]{1,0:T(8,128)(2,1)S(1)}, bf16[32,4096]{1,0:T(8,128)(2,1)S(1)}, u32[]{:S(2)}, u32[]{:S(2)}) collective-permute-start(bf16[32,4096]{1,0:T(8,128)(2,1)S(1)} %collective-permute-done.6.refs_1_.refs_7_), channel_id=1, source_target_pairs={{0,1},{1,0},{2,3},{3,2},{4,5},{5,4},{6,7},{7,6},{8,9},{9,8},{10,11... | collective-permute-start | bytes 786440 | tf_op jit(solution)/shard_map/ppermute | solution.py:33
  54.6 4.8 %collective-permute-start.18 = (bf16[256,128]{1,0:T(8,128)(2,1)S(1)}, bf16[256,128]{1,0:T(8,128)(2,1)S(1)}, u32[]{:S(2)}, u32[]{:S(2)}) collective-permute-start(bf16[256,128]{1,0:T(8,128)(2,1)S(1)} %conv_states.1), channel_id=1, source_target_pairs={{0,2},{1,3},{2,0},{3,1},{4,6},{5,7},{6,4},{7,5},{8,10},{9,11},{10,... | collective-permute-start | bytes 196616 | tf_op jit(solution)/shard_map/ppermute | solution.py:33
  54.7 7.8 %collective-permute-start.19 = (bf16[256,128]{1,0:T(8,128)(2,1)S(1)}, bf16[256,128]{1,0:T(8,128)(2,1)S(1)}, u32[]{:S(2)}, u32[]{:S(2)}) collective-permute-start(bf16[256,128]{1,0:T(8,128)(2,1)S(1)} %conv_states.1), channel_id=1, source_target_pairs={{0,4},{1,5},{2,6},{3,7},{4,0},{5,1},{6,2},{7,3},{8,12},{9,13},{10,... | collective-permute-start | bytes 196616 | tf_op jit(solution)/shard_map/ppermute | solution.py:33
  57.7 6.9 %collective-permute-start.20 = (bf16[256,128]{1,0:T(8,128)(2,1)S(1)}, bf16[256,128]{1,0:T(8,128)(2,1)S(1)}, u32[]{:S(2)}, u32[]{:S(2)}) collective-permute-start(bf16[256,128]{1,0:T(8,128)(2,1)S(1)} %conv_states.1), channel_id=1, source_target_pairs={{0,6},{1,7},{2,4},{3,5},{4,2},{5,3},{6,0},{7,1},{8,14},{9,15},{10,... | collective-permute-start | bytes 196616 | tf_op jit(solution)/shard_map/ppermute | solution.py:33
  64.7 8.6 %collective-permute-start.21 = (bf16[4,256,128]{2,1,0:T(8,128)(2,1)S(1)}, bf16[4,256,128]{2,1,0:T(8,128)(2,1)S(1)}, u32[]{:S(2)}, u32[]{:S(2)}) collective-permute-start(bf16[4,256,128]{2,1,0:T(8,128)(2,1)S(1)} %pad_maximum_fusion.own_ref), channel_id=1, source_target_pairs={{0,1},{1,0},{2,3},{3,2},{4,5},{5,4},{6,7},{7,6},{8,9},{9,8},{10,11... | collective-permute-start | bytes 786440 | tf_op jit(solution)/shard_map/ppermute | solution.py:33
  74.5 5.5 %collective-permute-start.22 = (f16[272,128]{1,0:T(8,128)(2,1)S(1)}, f16[272,128]{1,0:T(8,128)(2,1)S(1)}, u32[]{:S(2)}, u32[]{:S(2)}) collective-permute-start(f16[272,128]{1,0:T(8,128)(2,1)S(1)} %get-tuple-element.73), channel_id=1, source_target_pairs={{0,32},{32,0},{64,96},{96,64},{128,160},{160,128},{192,224},{224,1... | collective-permute-start | bytes 208904 | tf_op jit(solution)/shard_map/ppermute | solution.py:33
  76.1 8.0 %collective-permute-start.23 = (f16[272,128]{1,0:T(8,128)(2,1)S(1)}, f16[272,128]{1,0:T(8,128)(2,1)S(1)}, u32[]{:S(2)}, u32[]{:S(2)}) collective-permute-start(f16[272,128]{1,0:T(8,128)(2,1)S(1)} %get-tuple-element.72), channel_id=1, source_target_pairs={{0,64},{32,96},{64,0},{96,32},{128,192},{160,224},{192,128},{224,1... | collective-permute-start | bytes 208904 | tf_op jit(solution)/shard_map/ppermute | solution.py:33
  80.0 5.5 %collective-permute-start.24 = (f16[272,128]{1,0:T(8,128)(2,1)S(1)}, f16[272,128]{1,0:T(8,128)(2,1)S(1)}, u32[]{:S(2)}, u32[]{:S(2)}) collective-permute-start(f16[272,128]{1,0:T(8,128)(2,1)S(1)} %get-tuple-element.71), channel_id=1, source_target_pairs={{0,96},{32,64},{64,32},{96,0},{128,224},{160,192},{192,160},{224,1... | collective-permute-start | bytes 208904 | tf_op jit(solution)/shard_map/ppermute | solution.py:33
  86.3 9.8 %collective-permute-start.25 = (f16[272,128]{1,0:T(8,128)(2,1)S(1)}, f16[272,128]{1,0:T(8,128)(2,1)S(1)}, u32[]{:S(2)}, u32[]{:S(2)}) collective-permute-start(f16[272,128]{1,0:T(8,128)(2,1)S(1)} %convert_element_type.120), channel_id=1, source_target_pairs={{0,128},{32,160},{64,192},{96,224},{128,0},{160,32},{192,64},{224,... | collective-permute-start | bytes 208904 | tf_op jit(solution)/shard_map/ppermute | solution.py:33
  96.9 4.8 %collective-permute-start.26 = (f16[272,128]{1,0:T(8,128)(2,1)S(1)}, f16[272,128]{1,0:T(8,128)(2,1)S(1)}, u32[]{:S(2)}, u32[]{:S(2)}) collective-permute-start(f16[272,128]{1,0:T(8,128)(2,1)S(1)} %get-tuple-element.70), channel_id=1, source_target_pairs={{0,32},{32,0},{64,96},{96,64},{128,160},{160,128},{192,224},{224,1... | collective-permute-start | bytes 208904 | tf_op jit(solution)/shard_map/ppermute | solution.py:33
  97.2 6.9 %collective-permute-start.27 = (f16[272,128]{1,0:T(8,128)(2,1)S(1)}, f16[272,128]{1,0:T(8,128)(2,1)S(1)}, u32[]{:S(2)}, u32[]{:S(2)}) collective-permute-start(f16[272,128]{1,0:T(8,128)(2,1)S(1)} %get-tuple-element.69), channel_id=1, source_target_pairs={{0,64},{32,96},{64,0},{96,32},{128,192},{160,224},{192,128},{224,1... | collective-permute-start | bytes 208904 | tf_op jit(solution)/shard_map/ppermute | solution.py:33
  101.0 5.5 %collective-permute-start.28 = (f16[272,128]{1,0:T(8,128)(2,1)S(1)}, f16[272,128]{1,0:T(8,128)(2,1)S(1)}, u32[]{:S(2)}, u32[]{:S(2)}) collective-permute-start(f16[272,128]{1,0:T(8,128)(2,1)S(1)} %get-tuple-element.68), channel_id=1, source_target_pairs={{0,96},{32,64},{64,32},{96,0},{128,224},{160,192},{192,160},{224,1... | collective-permute-start | bytes 208904 | tf_op jit(solution)/shard_map/ppermute | solution.py:33
  126.5 8.4 %collective-permute-start.34 = (f16[32,4096]{1,0:T(8,128)(2,1)S(1)}, f16[32,4096]{1,0:T(8,128)(2,1)S(1)}, u32[]{:S(2)}, u32[]{:S(2)}) collective-permute-start(f16[32,4096]{1,0:T(8,128)(2,1)S(1)} %get-tuple-element.64), channel_id=1, source_target_pairs={{0,8},{1,9},{2,10},{3,11},{4,12},{5,13},{6,14},{7,15},{8,16},{9,17... | collective-permute-start | bytes 786440 | tf_op jit(solution)/shard_map/ppermute | solution.py:33
  127.4 9.3 %collective-permute-start.36 = (f16[32,4096]{1,0:T(8,128)(2,1)S(1)}, f16[32,4096]{1,0:T(8,128)(2,1)S(1)}, u32[]{:S(2)}, u32[]{:S(2)}) collective-permute-start(f16[32,4096]{1,0:T(8,128)(2,1)S(1)} %get-tuple-element.65), channel_id=1, source_target_pairs={{0,24},{1,25},{2,26},{3,27},{4,28},{5,29},{6,30},{7,31},{8,0},{9,1... | collective-permute-start | bytes 786440 | tf_op jit(solution)/shard_map/ppermute | solution.py:33
  137.8 13.1 %collective-permute-start.35 = (f16[64,4096]{1,0:T(8,128)(2,1)}, f16[64,4096]{1,0:T(8,128)(2,1)}, u32[]{:S(2)}, u32[]{:S(2)}) collective-permute-start(f16[64,4096]{1,0:T(8,128)(2,1)} %fusion.1), channel_id=1, source_target_pairs={{0,8},{1,9},{2,10},{3,11},{4,12},{5,13},{6,14},{7,15},{8,16},{9,17... | collective-permute-start | bytes 1572872 | tf_op jit(solution)/shard_map/ppermute | solution.py:33
  139.0 14.4 %collective-permute-start.37 = (f16[64,4096]{1,0:T(8,128)(2,1)}, f16[64,4096]{1,0:T(8,128)(2,1)}, u32[]{:S(2)}, u32[]{:S(2)}) collective-permute-start(f16[64,4096]{1,0:T(8,128)(2,1)} %fusion.2), channel_id=1, source_target_pairs={{0,24},{1,25},{2,26},{3,27},{4,28},{5,29},{6,30},{7,31},{8,0},{9,1... | collective-permute-start | bytes 1572872 | tf_op jit(solution)/shard_map/ppermute | solution.py:33
  157.0 6.5 %collective-permute-start.38 = (f16[16,4096]{1,0:T(8,128)(2,1)S(1)}, f16[16,4096]{1,0:T(8,128)(2,1)S(1)}, u32[]{:S(2)}, u32[]{:S(2)}) collective-permute-start(f16[16,4096]{1,0:T(8,128)(2,1)S(1)} %get-tuple-element.61), channel_id=1, source_target_pairs={{0,2},{1,3},{2,0},{3,1},{4,6},{5,7},{6,4},{7,5},{8,10},{9,11},{10,... | collective-permute-start | bytes 393224 | tf_op jit(solution)/shard_map/ppermute | solution.py:33
  157.6 9.6 %collective-permute-start.39 = (f16[16,4096]{1,0:T(8,128)(2,1)S(1)}, f16[16,4096]{1,0:T(8,128)(2,1)S(1)}, u32[]{:S(2)}, u32[]{:S(2)}) collective-permute-start(f16[16,4096]{1,0:T(8,128)(2,1)S(1)} %get-tuple-element.63), channel_id=1, source_target_pairs={{0,4},{1,5},{2,6},{3,7},{4,0},{5,1},{6,2},{7,3},{8,12},{9,13},{10,... | collective-permute-start | bytes 393224 | tf_op jit(solution)/shard_map/ppermute | solution.py:33
  159.5 10.7 %collective-permute-start.40 = (f16[16,4096]{1,0:T(8,128)(2,1)S(1)}, f16[16,4096]{1,0:T(8,128)(2,1)S(1)}, u32[]{:S(2)}, u32[]{:S(2)}) collective-permute-start(f16[16,4096]{1,0:T(8,128)(2,1)S(1)} %get-tuple-element.62), channel_id=1, source_target_pairs={{0,6},{1,7},{2,4},{3,5},{4,2},{5,3},{6,0},{7,1},{8,14},{9,15},{10,... | collective-permute-start | bytes 393224 | tf_op jit(solution)/shard_map/ppermute | solution.py:33
  (19 other events, 211.4 us)
where the time goes:
time: 172 us
  waiting for transfers between devices  75.1 us (44%)
  starting transfers between devices  51.6 us (30%)
  Pallas kernels  33.3 us (19%)
  other arithmetic  9.99 us (6%)
    ppermute x37, waiting for transfers between devices, send(): return lax.ppermute(array, axis, pairs)  74.4 us
    ppermute x37, starting transfers between devices, send(): return lax.ppermute(array, axis, pairs)  48.4 us
    pallas_call x3, Pallas kernels, project_resident(): pl.pallas_call(kernel, out_shape=outs, in_specs=[SM] + [VM] * (nl + 2) +...  9.13 us
    pallas_call x2, Pallas kernels, out_block(): pl.pallas_call(kernel, out_shape=[sds((rows, 4096), F32)] * 2, in_specs=[...  5.01 us
    pallas_call x1, Pallas kernels, project(): pl.pallas_call(kernel, out_shape=outs, grid_spec=pltpu.PrefetchScalarGrid...  4.96 us
    pallas_call x1, Pallas kernels, scan_stage(): pl.pallas_call(scan_kernel, out_shape=[sds((512, 512), F32), sds((512, 25...  4.16 us
    pallas_call x1, Pallas kernels, inputs_stage(): pl.pallas_call(inputs_kernel, out_shape=[sds((512, 512), BF16)] * 3 + [sd...  3.44 us
  transfers between devices with their start and end apart: 41, of which 24 were waited for; matrix products, arithmetic and copies ran while one was open for 3% of the time, Pallas kernels for 11%

commit v1 on v0

--- a/solution.py
+++ b/solution.py
@@ -682,11 +682,13 @@
     mine_other = flip(mine, "tp", 1)
     last = lax.dynamic_index_in_dim(mine.reshape(4, 16, mine.shape[1]), 3 - zl, 0, False)[8:]
     before_all = {"h0": lambda c, t: (c + 1, t) if c < 7 and t >= 24 and t % 2 else None}
-    before_all["h1"] = lambda c, t: (c, t - 24) if t >= 24 and t % 2 else None
-    before_all["h2"] = lambda c, t: (c, t - 8) if t >= 24 and t % 2 else ((c, t + 8) if t < 8 and t % 2 else None)
-    before_all["h3"] = lambda c, t: (c, t - 1) if t % 2 else None
+    before_all["hc"] = lambda c, t: (c, t - 1) if t >= 24 and t % 2 else None
+    before_all["h1"] = lambda c, t: (c, t - 24) if t >= 24 else None
+    before_all["h2"] = lambda c, t: (c, t - 8) if t >= 24 else ((c, t + 8) if t < 8 else None)
     rim = hop(last, before_all["h0"])
     bufs = project_resident([mine, mine_other], None, [0], idx, input_weight, small_w, None)
+    rim = rim + hop(rim, before_all["hc"])
+    right, left, rim = lax.optimization_barrier((right, left, rim))
     rim = rim + hop(rim, before_all["h1"])
     far_a = along_x(right[:32], 1)
     far_b = along_x(left[32:], -1)
@@ -696,7 +698,6 @@
     bufs = project_resident(
         [right, right_other, left, left_other], None, [1, 2], idx, input_weight, small_w, bufs
     )
-    rim = rim + hop(rim, before_all["h3"])
     rim = jnp.concatenate([jnp.zeros_like(rim), rim], axis=0)
     far_a_other = flip(far_a, "tp", 1)
     far_b_other = flip(far_b, "tp", 1)
@@ -734,18 +735,38 @@
     rest_own, rest_oth = out_block(idx, [2, 1, 0], u, squares, gain, out_w)
     rest = swap_add(rest_own, rest_oth)
     ahead_sum, behind_sum, mine_sum = rest[:64], rest[64:128], rest[128:]
-    to_right = narrow(jnp.concatenate([ahead_sum[:32] + widen(got_a), ahead_sum[32:]], axis=0))
-    to_left = narrow(jnp.concatenate([behind_sum[:32], behind_sum[32:] + widen(got_b)], axis=0))
-    from_left = along_x(to_right, 1)
-    from_right = along_x(to_left, -1)
-    both_sums = mine_sum + widen(from_left) + widen(from_right)
-    block = both_sums.reshape(4, 16, 4096)
-    out = lax.dynamic_index_in_dim(block, zl, 0, False)
-    for s in (1, 2, 3):
-        part = narrow(lax.dynamic_index_in_dim(block, jnp.bitwise_xor(zl, s), 0, False))
-        part = flip(part, "tp", 2 * s)
-        out = out + widen(part)
-    return out.astype(BF16)
+    half = out_w.shape[1] // 2
+    outs = []
+    moved = []
+    for n in range(2):
+        cols = slice(n * half, n * half + half)
+        to_right = narrow(
+            jnp.concatenate([ahead_sum[:32, cols] + widen(got_a[:, cols]), ahead_sum[32:, cols]], axis=0)
+        )
+        to_left = narrow(
+            jnp.concatenate([behind_sum[:32, cols], behind_sum[32:, cols] + widen(got_b[:, cols])], axis=0)
+        )
+        from_left = along_x(to_right, 1)
+        from_right = along_x(to_left, -1)
+        moved.append((mine_sum[:, cols], from_left, from_right))
+    for n in range(2):
+        own, from_left, from_right = moved[n]
+
+        def tile_sum(place):
+            at = place * 16
+            return (
+                lax.dynamic_slice_in_dim(own, at, 16, 0)
+                + widen(lax.dynamic_slice_in_dim(from_left, at, 16, 0))
+                + widen(lax.dynamic_slice_in_dim(from_right, at, 16, 0))
+            )
+
+        out = tile_sum(zl)
+        for p in (1, 2, 3):
+            part = narrow(tile_sum(jnp.bitwise_xor(zl, p)))
+            part = flip(part, "tp", 2 * p)
+            out = out + widen(part)
+        outs.append(out.astype(BF16))
+    return jnp.concatenate(outs, axis=1)
 
 
 def half_flip(value, mask):

time: 172 us -> 163 us (0.948)
  the two profiles are of different devices: /device:TPU:38 before, /device:TPU:24 now
where the time goes in v1:
time: 163 us; the launch traced here: 160 us
  starting transfers between devices  62.2 us (38%)
  waiting for transfers between devices  53 us (33%)
  Pallas kernels  33.2 us (20%)
  local copies, waits for them, and re-layouts  5.47 us (3%)
  other arithmetic  5.32 us (3%)
    ppermute x42, starting transfers between devices, send(): return lax.ppermute(array, axis, pairs)  58.3 us
    ppermute x42, waiting for transfers between devices, send(): return lax.ppermute(array, axis, pairs)  47.3 us
    pallas_call x3, Pallas kernels, project_resident(): pl.pallas_call(kernel, out_shape=outs, in_specs=[SM] + [VM] * (nl + 2) +...  9.12 us
    ppermute x4, waiting for transfers between devices, hop(): return lax.ppermute(array, ('ctx', 'tp'), pairs)  5.69 us
    unnamed x25, local copies, waits for them, and re-layouts  5.15 us
    pallas_call x2, Pallas kernels, out_block(): pl.pallas_call(kernel, out_shape=[sds((rows, 4096), F32)] * 2, in_specs=[...  5.01 us
    pallas_call x1, Pallas kernels, project(): pl.pallas_call(kernel, out_shape=outs, grid_spec=pltpu.PrefetchScalarGrid...  4.95 us
    pallas_call x1, Pallas kernels, scan_stage(): pl.pallas_call(scan_kernel, out_shape=[sds((512, 512), F32), sds((512, 25...  4.1 us
  transfers between devices with their start and end apart: 46, of which 19 were waited for; matrix products, arithmetic and copies ran while one was open for 3% of the time, Pallas kernels for 12%

profile of v1, /device:TPU:24, one launch (start us, length us, event | category | flops | bytes accessed | tf_op | source)
XLA Modules:
  0.0 160.0 jit_solution(7490340755459968960)
XLA Ops:
  0.0 1.9 %collective-permute-start = (bf16[16,4096]{1,0:T(8,128)(2,1)}, bf16[16,4096]{1,0:T(8,128)(2,1)S(1)}, u32[]{:S(2)}, u32[]{:S(2)}) collective-permute-start(bf16[16,4096]{1,0:T(8,128)(2,1)} %param.12), channel_id=1, source_target_pairs={{0,2},{1,3},{2,0},{3,1},{4,6},{5,7},{6,4},{7,5},{8,10},{9,11},{10,... | collective-permute-start | bytes 393224 | tf_op jit(solution)/shard_map/ppermute | solution.py:33
  1.9 3.3 %collective-permute-start.1 = (bf16[16,4096]{1,0:T(8,128)(2,1)}, bf16[16,4096]{1,0:T(8,128)(2,1)S(1)}, u32[]{:S(2)}, u32[]{:S(2)}) collective-permute-start(bf16[16,4096]{1,0:T(8,128)(2,1)} %param.12), channel_id=1, source_target_pairs={{0,4},{1,5},{2,6},{3,7},{4,0},{5,1},{6,2},{7,3},{8,12},{9,13},{10,... | collective-permute-start | bytes 393224 | tf_op jit(solution)/shard_map/ppermute | solution.py:33
  6.8 8.6 %collective-permute-done.1 = bf16[16,4096]{1,0:T(8,128)(2,1)S(1)} collective-permute-done((bf16[16,4096]{1,0:T(8,128)(2,1)}, bf16[16,4096]{1,0:T(8,128)(2,1)S(1)}, u32[]{:S(2)}, u32[]{:S(2)}) %collective-permute-start.1) | collective-permute-done | bytes 131104 | tf_op jit(solution)/shard_map/ppermute | solution.py:33
  20.9 7.3 %collective-permute-done.3.refs_0_.refs_2_ = bf16[64,4096]{1,0:T(8,128)(2,1)S(1)} collective-permute-done((bf16[64,4096]{1,0:T(8,128)(2,1)S(1)}, bf16[64,4096]{1,0:T(8,128)(2,1)S(1)}, u32[]{:S(2)}, u32[]{:S(2)}) %collective-permute-start.3) | collective-permute-done | bytes 524320 | tf_op jit(solution)/shard_map/ppermute | solution.py:33
  28.7 2.6 %collective-permute-start.8 = (bf16[32,4096]{1,0:T(8,128)(2,1)S(1)}, bf16[32,4096]{1,0:T(8,128)(2,1)S(1)}, u32[]{:S(2)}, u32[]{:S(2)}) collective-permute-start(bf16[32,4096]{1,0:T(8,128)(2,1)S(1)} %slice.106), channel_id=1, source_target_pairs={{0,24},{1,25},{2,26},{3,27},{4,28},{5,29},{6,30},{7,31},{8,0},{9,1... | collective-permute-start | bytes 786440 | tf_op jit(solution)/shard_map/ppermute | solution.py:33
  34.0 5.7 %collective-permute-done.11 = bf16[8,4096]{1,0:T(8,128)(2,1)S(1)} collective-permute-done((bf16[8,4096]{1,0:T(8,128)(2,1)S(1)}, bf16[8,4096]{1,0:T(8,128)(2,1)S(1)}, u32[]{:S(2)}, u32[]{:S(2)}) %collective-permute-start.11) | collective-permute-done | bytes 65568 | tf_op jit(solution)/shard_map/ppermute | solution.py:39
  42.0 2.7 %shard_map.118 = (bf16[512,512]{1,0:T(8,128)(2,1)S(1)}, bf16[512,128]{1,0:T(8,128)(2,1)S(1)}, f32[8,512]{1,0:T(8,128)S(1)}) custom-call(s32[16]{0:T(128)S(1)} %compare_select_fusion.9.i.idx, bf16[64,4096]{1,0:T(8,128)(2,1)S(1)} %constant_dynamic-update-slice_fusion.refs_0_, bf16[64,4096]{1,0:T(8,128)(2,1)S(1)} %collective-permute-done.16.refs_1_, ...), custom_call_target="tpu_custom_call" | custom-call | flops 805306368 | bytes 6291456 | tf_op jit(solution)/shard_map/pallas_call | solution.py:237
  44.8 3.5 %shard_map.119 = (bf16[512,512]{1,0:T(8,128)(2,1)S(1)}, bf16[512,128]{1,0:T(8,128)(2,1)S(1)}, f32[8,512]{1,0:T(8,128)S(1)}) custom-call(s32[16]{0:T(128)S(1)} %compare_select_fusion.9.i.idx, bf16[64,4096]{1,0:T(8,128)(2,1)S(1)} %collective-permute-done.3.refs_0_.refs_2_, ...), custom_call_target="tpu_custom_call", output_to_operand_aliasing={{0}: (7, {}), {1}: (8, {}), {2}: (9, {})} | custom-call | flops 1610612736 | bytes 6291456 | tf_op jit(solution)/shard_map/pallas_call | solution.py:237
  48.5 2.9 %shard_map.120 = (bf16[512,512]{1,0:T(8,128)(2,1)S(1)}, bf16[512,128]{1,0:T(8,128)(2,1)S(1)}, f32[8,512]{1,0:T(8,128)S(1)}, bf16[16,640]{1,0:T(8,128)(2,1)S(1)}) custom-call(s32[16]{0:T(128)S(1)} %compare_select_fusion.9.i.idx, ...), custom_call_target="tpu_custom_call", output_to_operand_aliasing={{0}: (8, {}), {1}: (9, {}), {2}: (10, {})} | custom-call | flops 805306368 | bytes 6291456 | tf_op jit(solution)/shard_map/pallas_call | solution.py:237
  52.1 3.7 %collective-permute-start.18 = (bf16[256,128]{1,0:T(8,128)(2,1)S(1)}, bf16[256,128]{1,0:T(8,128)(2,1)S(1)}, u32[]{:S(2)}, u32[]{:S(2)}) collective-permute-start(bf16[256,128]{1,0:T(8,128)(2,1)S(1)} %conv_states.1), channel_id=1, source_target_pairs={{0,2},{1,3},{2,0},{3,1},{4,6},{5,7},{6,4},{7,5},{8,10},{9,11},{10,... | collective-permute-start | bytes 196616 | tf_op jit(solution)/shard_map/ppermute | solution.py:33
  58.5 5.7 %collective-permute-done.19 = bf16[256,128]{1,0:T(8,128)(2,1)S(1)} collective-permute-done((bf16[256,128]{1,0:T(8,128)(2,1)S(1)}, bf16[256,128]{1,0:T(8,128)(2,1)S(1)}, u32[]{:S(2)}, u32[]{:S(2)}) %collective-permute-start.19) | collective-permute-done | bytes 65568 | tf_op jit(solution)/shard_map/ppermute | solution.py:33
  64.4 3.4 %inputs_stage.1 = (bf16[512,512]{1,0:T(8,128)(2,1)S(1)}, bf16[512,512]{1,0:T(8,128)(2,1)S(1)}, bf16[512,512]{1,0:T(8,128)(2,1)S(1)}, f32[8,512]{1,0:T(8,128)S(1)}, f32[8,512]{1,0:T(8,128)S(1)}) custom-call(f32[24]{0:T(128)S(1)} %pad_maximum_fusion.3.par_ref, bf16[512,512]{1,0:T(8,128)(2,1)S(1)} %get-tuple-element.45.rows_ref, ...), custom_call_target="tpu_custom_call" | custom-call | flops 10000000 | bytes 2000000 | tf_op jit(solution)/shard_map/inputs_stage/pallas_call | solution.py:345
  67.9 5.0 %shard_map.121.gate_ref = bf16[512,512]{1,0:T(8,128)(2,1)S(1)} custom-call(s32[16]{0:T(128)S(1)} %compare_select_fusion.9.i.idx, bf16[64,4096]{1,0:T(8,128)(2,1)S(1)} %constant_dynamic-update-slice_fusion.refs_0_, bf16[64,4096]{1,0:T(8,128)(2,1)S(1)} %collective-permute-done.16.refs_1_, bf16[64,4096]{1,0:T(8,128)(2,1)S(1)} %collective-permute-done.3.refs_0_.refs_2_, ...), custom_call_target="tpu_custom_call" | custom-call | flops 2147483648 | bytes 4194304 | tf_op jit(solution)/shard_map/pallas_call | solution.py:160
  75.9 2.9 %collective-permute-start.24 = (f16[272,128]{1,0:T(8,128)(2,1)S(1)}, f16[272,128]{1,0:T(8,128)(2,1)S(1)}, u32[]{:S(2)}, u32[]{:S(2)}) collective-permute-start(f16[272,128]{1,0:T(8,128)(2,1)S(1)} %get-tuple-element.88), channel_id=1, source_target_pairs={{0,96},{32,64},{64,32},{96,0},{128,224},{160,192},{192,160},{224,1... | collective-permute-start | bytes 208904 | tf_op jit(solution)/shard_map/ppermute | solution.py:33
  82.9 6.5 %collective-permute-start.25 = (f16[272,128]{1,0:T(8,128)(2,1)S(1)}, f16[272,128]{1,0:T(8,128)(2,1)S(1)}, u32[]{:S(2)}, u32[]{:S(2)}) collective-permute-start(f16[272,128]{1,0:T(8,128)(2,1)S(1)} %convert_element_type.186), channel_id=1, source_target_pairs={{0,128},{32,160},{64,192},{96,224},{128,0},{160,32},{192,64},{224,... | collective-permute-start | bytes 208904 | tf_op jit(solution)/shard_map/ppermute | solution.py:33
  89.4 4.1 %scan_stage.1 = (f32[512,512]{1,0:T(8,128)S(1)}, bf16[512,256]{1,0:T(8,128)(2,1)S(1)}) custom-call(s32[16]{0:T(128)S(1)} %compare_select_fusion.9.i.idx, f32[24]{0:T(128)S(1)} %pad_maximum_fusion.3.par_ref, bf16[4,256,128]{2,1,0:T(8,128)(2,1)S(1)} %pad_maximum_fusion.own_ref, bf16[4,256,128]{2,1,0:T(8,128)(2,1)S(1)} %collective-permute-done.21.oth_ref, ...), custom_call_target="tpu_custom_call" | custom-call | flops 6000000000 | bytes 3000000 | tf_op jit(solution)/shard_map/scan_stage/pallas_call | solution.py:530
  94.4 2.8 %collective-permute-start.27 = (f16[272,128]{1,0:T(8,128)(2,1)S(1)}, f16[272,128]{1,0:T(8,128)(2,1)S(1)}, u32[]{:S(2)}, u32[]{:S(2)}) collective-permute-start(f16[272,128]{1,0:T(8,128)(2,1)S(1)} %get-tuple-element.86), channel_id=1, source_target_pairs={{0,64},{32,96},{64,0},{96,32},{128,192},{160,224},{192,128},{224,1... | collective-permute-start | bytes 208904 | tf_op jit(solution)/shard_map/ppermute | solution.py:33
  100.4 2.3 %collective-permute-done.28 = f16[272,128]{1,0:T(8,128)(2,1)S(1)} collective-permute-done((f16[272,128]{1,0:T(8,128)(2,1)S(1)}, f16[272,128]{1,0:T(8,128)(2,1)S(1)}, u32[]{:S(2)}, u32[]{:S(2)}) %collective-permute-start.28) | collective-permute-done | bytes 69664 | tf_op jit(solution)/shard_map/ppermute | solution.py:33
  102.7 3.0 %gate_stage.1 = (f32[512,512]{1,0:T(8,128)S(1)}, f32[4,128]{1,0:T(4,128)S(1)}) custom-call(s32[16]{0:T(128)S(1)} %compare_select_fusion.9.i.idx, f32[512,512]{1,0:T(8,128)S(1)} %get-tuple-element.50.y_ref, bf16[512,256]{1,0:T(8,128)(2,1)S(1)} %get-tuple-element.51.read_ref, f32[272,128]{1,0:T(8,128)S(1)} %slice_bitcast_fusion.q0, ...), custom_call_target="tpu_custom_call" | custom-call | flops 200000000 | bytes 3000000 | tf_op jit(solution)/shard_map/gate_stage/pallas_call | solution.py:572
  108.5 2.1 %collective-permute-done.30 = f32[4,128]{1,0:T(4,128)S(1)} collective-permute-done((f32[4,128]{1,0:T(4,128)S(1)}, f32[4,128]{1,0:T(4,128)S(1)}, u32[]{:S(2)}, u32[]{:S(2)}) %collective-permute-start.30) | collective-permute-done | bytes 2080 | tf_op jit(solution)/shard_map/ppermute | solution.py:33
  110.6 1.9 %collective-permute-start.31 = (f32[4,128]{1,0:T(4,128)S(1)}, f32[4,128]{1,0:T(4,128)S(1)}, u32[]{:S(2)}, u32[]{:S(2)}) collective-permute-start(f32[4,128]{1,0:T(4,128)S(1)} %add.188), channel_id=1, source_target_pairs={{0,4},{1,5},{2,6},{3,7},{4,0},{5,1},{6,2},{7,3},{8,12},{9,13},{10,... | collective-permute-start | bytes 6152 | tf_op jit(solution)/shard_map/ppermute | solution.py:33
  112.9 2.0 %copy-done.1 = bf16[512,4096]{1,0:T(8,128)(2,1)} copy-done((bf16[512,4096]{1,0:T(8,128)(2,1)}, bf16[512,4096]{1,0:T(8,128)(2,1)S(1)}, u32[]{:S(2)}) %copy-start.1) | copy-done | bytes 4194328
  115.1 2.2 %copy-done.2 = bf16[512,4096]{1,0:T(8,128)(2,1)S(1)} copy-done((bf16[512,4096]{1,0:T(8,128)(2,1)S(1)}, bf16[512,4096]{1,0:T(8,128)(2,1)}, u32[]{:S(2)}) %copy-start.2) | copy-done | bytes 4194328
  117.3 2.0 %out_block.3 = (f32[64,4096]{1,0:T(8,128)S(1)}, f32[64,4096]{1,0:T(8,128)S(1)}) custom-call(s32[16]{0:T(128)S(1)} %compare_select_fusion.9.i.idx, f32[512,512]{1,0:T(8,128)S(1)} %get-tuple-element.57.u_ref, f32[4,128]{1,0:T(4,128)S(1)} %add.189.ss_ref, f32[1,512]{1,0:T(1,128)S(1)} %bitcast.30, bf16[512,4096]{1,0:T(8,128)(2,1)S(1)} %copy-done.2), custom_call_target="tpu_custom_call" | custom-call | flops 536870912 | bytes 6000000 | tf_op jit(solution)/shard_map/out_block/pallas_call | solution.py:629
  119.3 3.0 %out_block.2 = (f32[192,4096]{1,0:T(8,128)S(1)}, f32[192,4096]{1,0:T(8,128)S(1)}) custom-call(s32[16]{0:T(128)S(1)} %compare_select_fusion.9.i.idx, f32[512,512]{1,0:T(8,128)S(1)} %get-tuple-element.57.u_ref, f32[4,128]{1,0:T(4,128)S(1)} %add.189.ss_ref, f32[1,512]{1,0:T(1,128)S(1)} %bitcast.31, bf16[512,4096]{1,0:T(8,128)(2,1)S(1)} %copy-done.2), custom_call_target="tpu_custom_call" | custom-call | flops 1610612736 | bytes 6000000 | tf_op jit(solution)/shard_map/out_block/pallas_call | solution.py:629
  128.7 5.8 %collective-permute-done.34 = f16[32,4096]{1,0:T(8,128)(2,1)S(1)} collective-permute-done((f16[32,4096]{1,0:T(8,128)(2,1)S(1)}, f16[32,4096]{1,0:T(8,128)(2,1)S(1)}, u32[]{:S(2)}, u32[]{:S(2)}) %collective-permute-start.34) | collective-permute-done | bytes 262176 | tf_op jit(solution)/shard_map/ppermute | solution.py:33
  135.4 2.9 %collective-permute-start.37 = (f16[64,2048]{1,0:T(8,128)(2,1)S(1)}, f16[64,2048]{1,0:T(8,128)(2,1)S(1)}, u32[]{:S(2)}, u32[]{:S(2)}) collective-permute-start(f16[64,2048]{1,0:T(8,128)(2,1)S(1)} %fusion.3), channel_id=1, source_target_pairs={{0,24},{1,25},{2,26},{3,27},{4,28},{5,29},{6,30},{7,31},{8,0},{9,1... | collective-permute-start | bytes 786440 | tf_op jit(solution)/shard_map/ppermute | solution.py:33
  138.5 3.3 %collective-permute-start.42 = (f16[64,2048]{1,0:T(8,128)(2,1)S(1)}, f16[64,2048]{1,0:T(8,128)(2,1)S(1)}, u32[]{:S(2)}, u32[]{:S(2)}) collective-permute-start(f16[64,2048]{1,0:T(8,128)(2,1)S(1)} %fusion.5), channel_id=1, source_target_pairs={{0,24},{1,25},{2,26},{3,27},{4,28},{5,29},{6,30},{7,31},{8,0},{9,1... | collective-permute-start | bytes 786440 | tf_op jit(solution)/shard_map/ppermute | solution.py:33
  141.9 3.5 %collective-permute-done.35 = f16[64,2048]{1,0:T(8,128)(2,1)S(1)} collective-permute-done((f16[64,2048]{1,0:T(8,128)(2,1)S(1)}, f16[64,2048]{1,0:T(8,128)(2,1)S(1)}, u32[]{:S(2)}, u32[]{:S(2)}) %collective-permute-start.35) | collective-permute-done | bytes 262176 | tf_op jit(solution)/shard_map/ppermute | solution.py:33
  148.1 1.9 %collective-permute-start.40 = (f16[16,2048]{1,0:T(8,128)(2,1)S(1)}, f16[16,2048]{1,0:T(8,128)(2,1)S(1)}, u32[]{:S(2)}, u32[]{:S(2)}) collective-permute-start(f16[16,2048]{1,0:T(8,128)(2,1)S(1)} %get-tuple-element.76), channel_id=1, source_target_pairs={{0,6},{1,7},{2,4},{3,5},{4,2},{5,3},{6,0},{7,1},{8,14},{9,15},{10,... | collective-permute-start | bytes 196616 | tf_op jit(solution)/shard_map/ppermute | solution.py:33
  152.7 1.9 %collective-permute-start.45 = (f16[16,2048]{1,0:T(8,128)(2,1)S(1)}, f16[16,2048]{1,0:T(8,128)(2,1)S(1)}, u32[]{:S(2)}, u32[]{:S(2)}) collective-permute-start(f16[16,2048]{1,0:T(8,128)(2,1)S(1)} %get-tuple-element.79), channel_id=1, source_target_pairs={{0,6},{1,7},{2,4},{3,5},{4,2},{5,3},{6,0},{7,1},{8,14},{9,15},{10,... | collective-permute-start | bytes 196616 | tf_op jit(solution)/shard_map/ppermute | solution.py:33
  156.4 2.9 %collective-permute-done.44 = f16[16,2048]{1,0:T(8,128)(2,1)S(1)} collective-permute-done((f16[16,2048]{1,0:T(8,128)(2,1)S(1)}, f16[16,2048]{1,0:T(8,128)(2,1)S(1)}, u32[]{:S(2)}, u32[]{:S(2)}) %collective-permute-start.44) | collective-permute-done | bytes 65568 | tf_op jit(solution)/shard_map/ppermute | solution.py:33
  (149 shorter events, 46.1 us)
Async XLA Ops:
  0.0 6.8 %collective-permute-start = (bf16[16,4096]{1,0:T(8,128)(2,1)}, bf16[16,4096]{1,0:T(8,128)(2,1)S(1)}, u32[]{:S(2)}, u32[]{:S(2)}) collective-permute-start(bf16[16,4096]{1,0:T(8,128)(2,1)} %param.12), channel_id=1, source_target_pairs={{0,2},{1,3},{2,0},{3,1},{4,6},{5,7},{6,4},{7,5},{8,10},{9,11},{10,... | collective-permute-start | bytes 393224 | tf_op jit(solution)/shard_map/ppermute | solution.py:33
  1.9 13.5 %collective-permute-start.1 = (bf16[16,4096]{1,0:T(8,128)(2,1)}, bf16[16,4096]{1,0:T(8,128)(2,1)S(1)}, u32[]{:S(2)}, u32[]{:S(2)}) collective-permute-start(bf16[16,4096]{1,0:T(8,128)(2,1)} %param.12), channel_id=1, source_target_pairs={{0,4},{1,5},{2,6},{3,7},{4,0},{5,1},{6,2},{7,3},{8,12},{9,13},{10,... | collective-permute-start | bytes 393224 | tf_op jit(solution)/shard_map/ppermute | solution.py:33
  5.2 10.2 %collective-permute-start.2 = (bf16[16,4096]{1,0:T(8,128)(2,1)}, bf16[16,4096]{1,0:T(8,128)(2,1)S(1)}, u32[]{:S(2)}, u32[]{:S(2)}) collective-permute-start(bf16[16,4096]{1,0:T(8,128)(2,1)} %param.12), channel_id=1, source_target_pairs={{0,6},{1,7},{2,4},{3,5},{4,2},{5,3},{6,0},{7,1},{8,14},{9,15},{10,... | collective-permute-start | bytes 393224 | tf_op jit(solution)/shard_map/ppermute | solution.py:33
  5.2 27.6 %collective-permute-start.13 = (bf16[64,4096]{1,0:T(8,128)(2,1)}, bf16[64,4096]{1,0:T(8,128)(2,1)S(1)}, u32[]{:S(2)}, u32[]{:S(2)}) collective-permute-start(bf16[64,4096]{1,0:T(8,128)(2,1)} %bitcast.32), channel_id=1, source_target_pairs={{0,1},{1,0},{2,3},{3,2},{4,5},{5,4},{6,7},{7,6},{8,9},{9,8},{10,11... | collective-permute-start | bytes 1572872 | tf_op jit(solution)/shard_map/ppermute | solution.py:33
  5.2 14.2 %collective-permute-start.17 = (f32[5,64]{1,0:T(8,128)}, f32[5,64]{1,0:T(8,128)S(1)}, u32[]{:S(2)}, u32[]{:S(2)}) collective-permute-start(f32[5,64]{1,0:T(8,128)} %param.18), channel_id=1, source_target_pairs={{0,1},{1,0},{2,3},{3,2},{4,5},{5,4},{6,7},{7,6},{8,9},{9,8},{10,11... | collective-permute-start | bytes 3848 | tf_op jit(solution)/shard_map/ppermute | solution.py:33
  15.4 12.8 %collective-permute-start.3 = (bf16[64,4096]{1,0:T(8,128)(2,1)S(1)}, bf16[64,4096]{1,0:T(8,128)(2,1)S(1)}, u32[]{:S(2)}, u32[]{:S(2)}) collective-permute-start(bf16[64,4096]{1,0:T(8,128)(2,1)S(1)} %constant_dynamic-update-slice_fusion.refs_0_), channel_id=1, source_target_pairs={{0,8},{1,9},{2,10},{3,11},{4,12},{5,13},{6,14},{7,15},{8,16},{9,17... | collective-permute-start | bytes 1572872 | tf_op jit(solution)/shard_map/ppermute | solution.py:33
  17.0 11.7 %collective-permute-start.4 = (bf16[64,4096]{1,0:T(8,128)(2,1)S(1)}, bf16[64,4096]{1,0:T(8,128)(2,1)S(1)}, u32[]{:S(2)}, u32[]{:S(2)}) collective-permute-start(bf16[64,4096]{1,0:T(8,128)(2,1)S(1)} %constant_dynamic-update-slice_fusion.refs_0_), channel_id=1, source_target_pairs={{0,24},{1,25},{2,26},{3,27},{4,28},{5,29},{6,30},{7,31},{8,0},{9,1... | collective-permute-start | bytes 1572872 | tf_op jit(solution)/shard_map/ppermute | solution.py:33
  20.9 19.8 %collective-permute-start.16 = (bf16[64,4096]{1,0:T(8,128)(2,1)S(1)}, bf16[64,4096]{1,0:T(8,128)(2,1)S(1)}, u32[]{:S(2)}, u32[]{:S(2)}) collective-permute-start(bf16[64,4096]{1,0:T(8,128)(2,1)S(1)} %constant_dynamic-update-slice_fusion.refs_0_), channel_id=1, source_target_pairs={{0,1},{1,0},{2,3},{3,2},{4,5},{5,4},{6,7},{7,6},{8,9},{9,8},{10,11... | collective-permute-start | bytes 1572872 | tf_op jit(solution)/shard_map/ppermute | solution.py:33
  28.7 11.0 %collective-permute-start.8 = (bf16[32,4096]{1,0:T(8,128)(2,1)S(1)}, bf16[32,4096]{1,0:T(8,128)(2,1)S(1)}, u32[]{:S(2)}, u32[]{:S(2)}) collective-permute-start(bf16[32,4096]{1,0:T(8,128)(2,1)S(1)} %slice.106), channel_id=1, source_target_pairs={{0,24},{1,25},{2,26},{3,27},{4,28},{5,29},{6,30},{7,31},{8,0},{9,1... | collective-permute-start | bytes 786440 | tf_op jit(solution)/shard_map/ppermute | solution.py:33
  31.4 8.9 %collective-permute-start.7 = (bf16[32,4096]{1,0:T(8,128)(2,1)S(1)}, bf16[32,4096]{1,0:T(8,128)(2,1)S(1)}, u32[]{:S(2)}, u32[]{:S(2)}) collective-permute-start(bf16[32,4096]{1,0:T(8,128)(2,1)S(1)} %slice.105), channel_id=1, source_target_pairs={{0,8},{1,9},{2,10},{3,11},{4,12},{5,13},{6,14},{7,15},{8,16},{9,17... | collective-permute-start | bytes 786440 | tf_op jit(solution)/shard_map/ppermute | solution.py:33
  31.5 8.3 %collective-permute-start.11 = (bf16[8,4096]{1,0:T(8,128)(2,1)S(1)}, bf16[8,4096]{1,0:T(8,128)(2,1)S(1)}, u32[]{:S(2)}, u32[]{:S(2)}) collective-permute-start(bf16[8,4096]{1,0:T(8,128)(2,1)S(1)} %add.184), channel_id=1, source_target_pairs={{24,0},{25,1},{26,2},{27,3},{28,4},{29,5},{30,6},{31,7},{56,32},{5... | collective-permute-start | bytes 196616 | tf_op jit(solution)/shard_map/ppermute | solution.py:39
  34.0 10.9 %collective-permute-start.14 = (bf16[64,4096]{1,0:T(8,128)(2,1)S(1)}, bf16[64,4096]{1,0:T(8,128)(2,1)S(1)}, u32[]{:S(2)}, u32[]{:S(2)}) collective-permute-start(bf16[64,4096]{1,0:T(8,128)(2,1)S(1)} %collective-permute-done.3.refs_0_.refs_2_), channel_id=1, source_target_pairs={{0,1},{1,0},{2,3},{3,2},{4,5},{5,4},{6,7},{7,6},{8,9},{9,8},{10,11... | collective-permute-start | bytes 1572872 | tf_op jit(solution)/shard_map/ppermute | solution.py:33
  39.7 8.6 %collective-permute-start.10 = (bf16[32,4096]{1,0:T(8,128)(2,1)S(1)}, bf16[32,4096]{1,0:T(8,128)(2,1)S(1)}, u32[]{:S(2)}, u32[]{:S(2)}) collective-permute-start(bf16[32,4096]{1,0:T(8,128)(2,1)S(1)} %collective-permute-done.8.refs_1_.refs_7_), channel_id=1, source_target_pairs={{0,1},{1,0},{2,3},{3,2},{4,5},{5,4},{6,7},{7,6},{8,9},{9,8},{10,11... | collective-permute-start | bytes 786440 | tf_op jit(solution)/shard_map/ppermute | solution.py:33
  40.2 8.1 %collective-permute-start.9 = (bf16[32,4096]{1,0:T(8,128)(2,1)S(1)}, bf16[32,4096]{1,0:T(8,128)(2,1)S(1)}, u32[]{:S(2)}, u32[]{:S(2)}) collective-permute-start(bf16[32,4096]{1,0:T(8,128)(2,1)S(1)} %collective-permute-done.7.refs_0_.refs_6_), channel_id=1, source_target_pairs={{0,1},{1,0},{2,3},{3,2},{4,5},{5,4},{6,7},{7,6},{8,9},{9,8},{10,11... | collective-permute-start | bytes 786440 | tf_op jit(solution)/shard_map/ppermute | solution.py:33
  52.1 6.4 %collective-permute-start.18 = (bf16[256,128]{1,0:T(8,128)(2,1)S(1)}, bf16[256,128]{1,0:T(8,128)(2,1)S(1)}, u32[]{:S(2)}, u32[]{:S(2)}) collective-permute-start(bf16[256,128]{1,0:T(8,128)(2,1)S(1)} %conv_states.1), channel_id=1, source_target_pairs={{0,2},{1,3},{2,0},{3,1},{4,6},{5,7},{6,4},{7,5},{8,10},{9,11},{10,... | collective-permute-start | bytes 196616 | tf_op jit(solution)/shard_map/ppermute | solution.py:33
  55.8 8.4 %collective-permute-start.19 = (bf16[256,128]{1,0:T(8,128)(2,1)S(1)}, bf16[256,128]{1,0:T(8,128)(2,1)S(1)}, u32[]{:S(2)}, u32[]{:S(2)}) collective-permute-start(bf16[256,128]{1,0:T(8,128)(2,1)S(1)} %conv_states.1), channel_id=1, source_target_pairs={{0,4},{1,5},{2,6},{3,7},{4,0},{5,1},{6,2},{7,3},{8,12},{9,13},{10,... | collective-permute-start | bytes 196616 | tf_op jit(solution)/shard_map/ppermute | solution.py:33
  57.1 7.0 %collective-permute-start.20 = (bf16[256,128]{1,0:T(8,128)(2,1)S(1)}, bf16[256,128]{1,0:T(8,128)(2,1)S(1)}, u32[]{:S(2)}, u32[]{:S(2)}) collective-permute-start(bf16[256,128]{1,0:T(8,128)(2,1)S(1)} %conv_states.1), channel_id=1, source_target_pairs={{0,6},{1,7},{2,4},{3,5},{4,2},{5,3},{6,0},{7,1},{8,14},{9,15},{10,... | collective-permute-start | bytes 196616 | tf_op jit(solution)/shard_map/ppermute | solution.py:33
  64.2 8.6 %collective-permute-start.21 = (bf16[4,256,128]{2,1,0:T(8,128)(2,1)S(1)}, bf16[4,256,128]{2,1,0:T(8,128)(2,1)S(1)}, u32[]{:S(2)}, u32[]{:S(2)}) collective-permute-start(bf16[4,256,128]{2,1,0:T(8,128)(2,1)S(1)} %pad_maximum_fusion.own_ref), channel_id=1, source_target_pairs={{0,1},{1,0},{2,3},{3,2},{4,5},{5,4},{6,7},{7,6},{8,9},{9,8},{10,11... | collective-permute-start | bytes 786440 | tf_op jit(solution)/shard_map/ppermute | solution.py:33
  75.9 6.2 %collective-permute-start.24 = (f16[272,128]{1,0:T(8,128)(2,1)S(1)}, f16[272,128]{1,0:T(8,128)(2,1)S(1)}, u32[]{:S(2)}, u32[]{:S(2)}) collective-permute-start(f16[272,128]{1,0:T(8,128)(2,1)S(1)} %get-tuple-element.88), channel_id=1, source_target_pairs={{0,96},{32,64},{64,32},{96,0},{128,224},{160,192},{192,160},{224,1... | collective-permute-start | bytes 208904 | tf_op jit(solution)/shard_map/ppermute | solution.py:33
  82.9 10.6 %collective-permute-start.25 = (f16[272,128]{1,0:T(8,128)(2,1)S(1)}, f16[272,128]{1,0:T(8,128)(2,1)S(1)}, u32[]{:S(2)}, u32[]{:S(2)}) collective-permute-start(f16[272,128]{1,0:T(8,128)(2,1)S(1)} %convert_element_type.186), channel_id=1, source_target_pairs={{0,128},{32,160},{64,192},{96,224},{128,0},{160,32},{192,64},{224,... | collective-permute-start | bytes 208904 | tf_op jit(solution)/shard_map/ppermute | solution.py:33
  124.9 9.6 %collective-permute-start.34 = (f16[32,4096]{1,0:T(8,128)(2,1)S(1)}, f16[32,4096]{1,0:T(8,128)(2,1)S(1)}, u32[]{:S(2)}, u32[]{:S(2)}) collective-permute-start(f16[32,4096]{1,0:T(8,128)(2,1)S(1)} %get-tuple-element.81), channel_id=1, source_target_pairs={{0,8},{1,9},{2,10},{3,11},{4,12},{5,13},{6,14},{7,15},{8,16},{9,17... | collective-permute-start | bytes 786440 | tf_op jit(solution)/shard_map/ppermute | solution.py:33
  126.5 8.1 %collective-permute-start.36 = (f16[32,4096]{1,0:T(8,128)(2,1)S(1)}, f16[32,4096]{1,0:T(8,128)(2,1)S(1)}, u32[]{:S(2)}, u32[]{:S(2)}) collective-permute-start(f16[32,4096]{1,0:T(8,128)(2,1)S(1)} %get-tuple-element.82), channel_id=1, source_target_pairs={{0,24},{1,25},{2,26},{3,27},{4,28},{5,29},{6,30},{7,31},{8,0},{9,1... | collective-permute-start | bytes 786440 | tf_op jit(solution)/shard_map/ppermute | solution.py:33
  134.9 10.5 %collective-permute-start.35 = (f16[64,2048]{1,0:T(8,128)(2,1)S(1)}, f16[64,2048]{1,0:T(8,128)(2,1)S(1)}, u32[]{:S(2)}, u32[]{:S(2)}) collective-permute-start(f16[64,2048]{1,0:T(8,128)(2,1)S(1)} %fusion.2), channel_id=1, source_target_pairs={{0,8},{1,9},{2,10},{3,11},{4,12},{5,13},{6,14},{7,15},{8,16},{9,17... | collective-permute-start | bytes 786440 | tf_op jit(solution)/shard_map/ppermute | solution.py:33
  135.4 10.0 %collective-permute-start.37 = (f16[64,2048]{1,0:T(8,128)(2,1)S(1)}, f16[64,2048]{1,0:T(8,128)(2,1)S(1)}, u32[]{:S(2)}, u32[]{:S(2)}) collective-permute-start(f16[64,2048]{1,0:T(8,128)(2,1)S(1)} %fusion.3), channel_id=1, source_target_pairs={{0,24},{1,25},{2,26},{3,27},{4,28},{5,29},{6,30},{7,31},{8,0},{9,1... | collective-permute-start | bytes 786440 | tf_op jit(solution)/shard_map/ppermute | solution.py:33
  138.4 11.6 %collective-permute-start.41 = (f16[64,2048]{1,0:T(8,128)(2,1)S(1)}, f16[64,2048]{1,0:T(8,128)(2,1)S(1)}, u32[]{:S(2)}, u32[]{:S(2)}) collective-permute-start(f16[64,2048]{1,0:T(8,128)(2,1)S(1)} %fusion.4), channel_id=1, source_target_pairs={{0,8},{1,9},{2,10},{3,11},{4,12},{5,13},{6,14},{7,15},{8,16},{9,17... | collective-permute-start | bytes 786440 | tf_op jit(solution)/shard_map/ppermute | solution.py:33
  138.5 11.4 %collective-permute-start.42 = (f16[64,2048]{1,0:T(8,128)(2,1)S(1)}, f16[64,2048]{1,0:T(8,128)(2,1)S(1)}, u32[]{:S(2)}, u32[]{:S(2)}) collective-permute-start(f16[64,2048]{1,0:T(8,128)(2,1)S(1)} %fusion.5), channel_id=1, source_target_pairs={{0,24},{1,25},{2,26},{3,27},{4,28},{5,29},{6,30},{7,31},{8,0},{9,1... | collective-permute-start | bytes 786440 | tf_op jit(solution)/shard_map/ppermute | solution.py:33
  145.5 7.2 %collective-permute-start.38 = (f16[16,2048]{1,0:T(8,128)(2,1)S(1)}, f16[16,2048]{1,0:T(8,128)(2,1)S(1)}, u32[]{:S(2)}, u32[]{:S(2)}) collective-permute-start(f16[16,2048]{1,0:T(8,128)(2,1)S(1)} %get-tuple-element.75), channel_id=1, source_target_pairs={{0,2},{1,3},{2,0},{3,1},{4,6},{5,7},{6,4},{7,5},{8,10},{9,11},{10,... | collective-permute-start | bytes 196616 | tf_op jit(solution)/shard_map/ppermute | solution.py:33
  147.1 8.1 %collective-permute-start.39 = (f16[16,2048]{1,0:T(8,128)(2,1)S(1)}, f16[16,2048]{1,0:T(8,128)(2,1)S(1)}, u32[]{:S(2)}, u32[]{:S(2)}) collective-permute-start(f16[16,2048]{1,0:T(8,128)(2,1)S(1)} %get-tuple-element.77), channel_id=1, source_target_pairs={{0,4},{1,5},{2,6},{3,7},{4,0},{5,1},{6,2},{7,3},{8,12},{9,13},{10,... | collective-permute-start | bytes 196616 | tf_op jit(solution)/shard_map/ppermute | solution.py:33
  148.1 7.1 %collective-permute-start.40 = (f16[16,2048]{1,0:T(8,128)(2,1)S(1)}, f16[16,2048]{1,0:T(8,128)(2,1)S(1)}, u32[]{:S(2)}, u32[]{:S(2)}) collective-permute-start(f16[16,2048]{1,0:T(8,128)(2,1)S(1)} %get-tuple-element.76), channel_id=1, source_target_pairs={{0,6},{1,7},{2,4},{3,5},{4,2},{5,3},{6,0},{7,1},{8,14},{9,15},{10,... | collective-permute-start | bytes 196616 | tf_op jit(solution)/shard_map/ppermute | solution.py:33
  150.1 6.3 %collective-permute-start.43 = (f16[16,2048]{1,0:T(8,128)(2,1)S(1)}, f16[16,2048]{1,0:T(8,128)(2,1)S(1)}, u32[]{:S(2)}, u32[]{:S(2)}) collective-permute-start(f16[16,2048]{1,0:T(8,128)(2,1)S(1)} %get-tuple-element.78), channel_id=1, source_target_pairs={{0,2},{1,3},{2,0},{3,1},{4,6},{5,7},{6,4},{7,5},{8,10},{9,11},{10,... | collective-permute-start | bytes 196616 | tf_op jit(solution)/shard_map/ppermute | solution.py:33
  151.0 8.3 %collective-permute-start.44 = (f16[16,2048]{1,0:T(8,128)(2,1)S(1)}, f16[16,2048]{1,0:T(8,128)(2,1)S(1)}, u32[]{:S(2)}, u32[]{:S(2)}) collective-permute-start(f16[16,2048]{1,0:T(8,128)(2,1)S(1)} %get-tuple-element.80), channel_id=1, source_target_pairs={{0,4},{1,5},{2,6},{3,7},{4,0},{5,1},{6,2},{7,3},{8,12},{9,13},{10,... | collective-permute-start | bytes 196616 | tf_op jit(solution)/shard_map/ppermute | solution.py:33
  152.7 6.6 %collective-permute-start.45 = (f16[16,2048]{1,0:T(8,128)(2,1)S(1)}, f16[16,2048]{1,0:T(8,128)(2,1)S(1)}, u32[]{:S(2)}, u32[]{:S(2)}) collective-permute-start(f16[16,2048]{1,0:T(8,128)(2,1)S(1)} %get-tuple-element.79), channel_id=1, source_target_pairs={{0,6},{1,7},{2,4},{3,5},{4,2},{5,3},{6,0},{7,1},{8,14},{9,15},{10,... | collective-permute-start | bytes 196616 | tf_op jit(solution)/shard_map/ppermute | solution.py:33
  (25 other events, 219.8 us)

commit v2 on v1

--- a/solution.py
+++ b/solution.py
@@ -77,7 +77,7 @@
 
 
 def project(parts, slots, idx, gate_w, input_w, small_w, bufs):
-    depth = parts[0].shape[1]
+    depth = parts[0][0].shape[1]
     steps = 4
     kb = depth // steps
     count = len(slots)
@@ -156,7 +156,7 @@
 
     cols = (512 if gate_w is not None else 0) + (768 if input_w is not None else 0)
     first = 1 + nl + nw
-    lspecs = [pl.BlockSpec((p.shape[0], kb), lambda k, i: (0, k)) for p in parts]
+    lspecs = [pl.BlockSpec((32, kb), lambda k, i, b=b: (b, k)) for _, b in parts]
     out = pl.pallas_call(
         kernel,
         out_shape=outs,
@@ -170,17 +170,25 @@
         input_output_aliases={first + n: n for n in range(len(aliased))},
         compiler_params=pltpu.CompilerParams(vmem_limit_bytes=14 * MIB),
         cost_estimate=cost(2 * rows * depth * cols, 2 * depth * cols),
-    )(idx, *parts, *weights, *aliased)
+    )(idx, *[p for p, _ in parts], *weights, *aliased)
     return list(out)
 
 
 def project_resident(parts, halo, slots, idx, input_w, small_w, bufs):
-    depth = parts[0].shape[1]
-    kb = 1024
+    depth = parts[0][0].shape[1]
+    kb = 512
     count = len(slots)
     rows = 128 * count
     extra = 0 if halo is None else 16
-    lefts = list(parts) + ([] if halo is None else [halo])
+    lefts, pieces = [], []
+    for array, block in list(parts):
+        known = [n for n, seen in enumerate(lefts) if seen is array]
+        if not known:
+            lefts.append(array)
+        pieces.append((known[0] if known else len(lefts) - 1, slice(block * 32, block * 32 + 32)))
+    if halo is not None:
+        lefts.append(halo)
+        pieces.append((len(lefts) - 1, slice(0, 16)))
     nl = len(lefts)
     outs = [sds((512, 512), BF16), sds((512, 128), BF16), sds((8, 512), F32)]
     ospecs = [pl.BlockSpec(memory_space=pl.ANY)] * 3
@@ -202,7 +210,7 @@
 
         def one(k, carry):
             here = pl.ds(pl.multiple_of(k * kb, kb), kb)
-            lhs = jnp.concatenate([r[:, here] for r in lrefs], axis=0)
+            lhs = jnp.concatenate([lrefs[n][rows_of, here] for n, rows_of in pieces], axis=0)
             acc[...] += dot(lhs, w_ref[here, :])
             acc_s[...] += dot_nt(lhs, s_ref[:, here])
             return carry
@@ -565,7 +573,7 @@
         ss_ref[pl.ds(k, 1), :] = jnp.sum(jnp.transpose(squares), axis=0, keepdims=True)
         return before + cum[:, 127:128]
 
-    lax.fori_loop(0, 4, one, jnp.zeros((8, 1), F32))
+    lax.fori_loop(0, 4, one, jnp.zeros((8, 1), F32), unroll=1)
 
 
 def gate_stage(idx, y, read, quarters, cum, gate):
@@ -618,17 +626,17 @@
                     lhs[pl.ds(pl.multiple_of(at, 16), 16), ch] = normed[t * 16 : t * 16 + 16, :]
 
         def one(n, carry):
-            here = pl.ds(pl.multiple_of(n * 1024, 1024), 1024)
+            here = pl.ds(pl.multiple_of(n * 512, 512), 512)
             part = dot(lhs[...], w_ref[:, here])
             own_ref[:, here] = part[0:rows, :]
-            oth_ref[:, here] = part[rows : 2 * rows, :]
+            oth_ref[:, here] = part[rows : 2 * rows, :].astype(BF16)
             return carry
 
-        lax.fori_loop(0, 4, one, 0)
+        lax.fori_loop(0, 8, one, 0)
 
     return pl.pallas_call(
         kernel,
-        out_shape=[sds((rows, 4096), F32)] * 2,
+        out_shape=[sds((rows, 4096), F32), sds((rows, 4096), BF16)],
         in_specs=[SM] + [VM] * 4,
         out_specs=[VM] * 2,
         scratch_shapes=[pltpu.VMEM((2 * rows, 512), BF16)],
@@ -675,33 +683,45 @@
     )
     par = jnp.concatenate([log_rate, step_bias, skip_gain])
 
-    tiles = [tokens] + [flip(tokens, "tp", 2 * s) for s in (1, 2, 3)]
-    mine = jnp.concatenate(tiles, axis=0)
-    right = along_x(mine, 1)
-    left = along_x(mine, -1)
-    mine_other = flip(mine, "tp", 1)
-    last = lax.dynamic_index_in_dim(mine.reshape(4, 16, mine.shape[1]), 3 - zl, 0, False)[8:]
-    before_all = {"h0": lambda c, t: (c + 1, t) if c < 7 and t >= 24 and t % 2 else None}
-    before_all["hc"] = lambda c, t: (c, t - 1) if t >= 24 and t % 2 else None
-    before_all["h1"] = lambda c, t: (c, t - 24) if t >= 24 else None
-    before_all["h2"] = lambda c, t: (c, t - 8) if t >= 24 else ((c, t + 8) if t < 8 else None)
-    rim = hop(last, before_all["h0"])
-    bufs = project_resident([mine, mine_other], None, [0], idx, input_weight, small_w, None)
-    rim = rim + hop(rim, before_all["hc"])
-    right, left, rim = lax.optimization_barrier((right, left, rim))
-    rim = rim + hop(rim, before_all["h1"])
-    far_a = along_x(right[:32], 1)
-    far_b = along_x(left[32:], -1)
-    right_other = flip(right, "tp", 1)
-    left_other = flip(left, "tp", 1)
-    rim = rim + hop(rim, before_all["h2"])
-    bufs = project_resident(
-        [right, right_other, left, left_other], None, [1, 2], idx, input_weight, small_w, bufs
-    )
+    tiles = [tokens, flip(tokens, "tp", 2)]
+    tiles.append(flip(tokens, "tp", 4))
+    tiles.append(flip(tokens, "tp", 6))
+    part1 = jnp.concatenate(tiles[:2], axis=0)
+    right1 = along_x(part1, 1)
+    left1 = along_x(part1, -1)
+    other1 = flip(part1, "tp", 1)
+    late, other1 = lax.optimization_barrier((tiles[2:], other1))
+    part2 = jnp.concatenate(late, axis=0)
+    right2 = along_x(part2, 1)
+    left2 = along_x(part2, -1)
+    other2 = flip(part2, "tp", 1)
+    own_parts = [(part1, 0), (part2, 0), (other1, 0), (other2, 0)]
+    last = tiles[0][8:]
+    for s in (1, 2, 3):
+        last = jnp.where(zl == 3 - s, tiles[s][8:], last)
+    to = {
+        "h0": lambda c, t: (c + 1, t) if c < 7 and t >= 24 and t % 2 else None,
+        "hc": lambda c, t: (c, t - 1) if t >= 24 and t % 2 else None,
+        "h1": lambda c, t: (c, t - 24) if t >= 24 else None,
+        "h2": lambda c, t: (c, t - 8) if t >= 24 else ((c, t + 8) if t < 8 else None),
+    }
+    rim = hop(last, to["h0"])
+    bufs = project_resident(own_parts, None, [0], idx, input_weight, small_w, None)
+    far_a = along_x(right1, 1)
+    side1 = flip(jnp.concatenate([right1, left1], axis=0), "tp", 1)
+    rim = rim + hop(rim, to["hc"])
+    rim = rim + hop(rim, to["h1"])
+    left2, rim = lax.optimization_barrier((left2, rim))
+    far_b = along_x(left2, -1)
+    side2 = flip(jnp.concatenate([right2, left2], axis=0), "tp", 1)
+    rim = rim + hop(rim, to["h2"])
+    rights = [(right1, 0), (right2, 0), (side1, 0), (side2, 0)]
+    lefts = [(left1, 0), (left2, 0), (side1, 1), (side2, 1)]
+    bufs = project_resident(rights + lefts, None, [1, 2], idx, input_weight, small_w, bufs)
     rim = jnp.concatenate([jnp.zeros_like(rim), rim], axis=0)
     far_a_other = flip(far_a, "tp", 1)
     far_b_other = flip(far_b, "tp", 1)
-    fars = [far_a, far_b, far_a_other, far_b_other]
+    fars = [(far_a, 0), (far_b, 0), (far_a_other, 0), (far_b_other, 0)]
     input_rows, state_rows, step_raw, halo = project_resident(
         fars, rim, [3], idx, input_weight, small_w, bufs
     )
@@ -716,7 +736,7 @@
     y_local, read_vec = scan_stage(idx, pieces, pieces_other, xs, dt, cum, par)
     inc, pre, total = prefix_stage(idx, *ends)
     before = half_flip(total, 4)
-    everything = [mine, mine_other, right, right_other, left, left_other] + fars
+    everything = own_parts + rights + lefts + fars
     (gate_rows,) = project(everything, [0, 1, 2, 3], idx, gate_weight, None, None, None)
     spread = spread_stage(idx, inc, pre, before)
     quarters = [spread[0]] + [half_flip(spread[s], s) for s in (1, 2, 3)]
@@ -729,26 +749,25 @@
     gain = norm_gain.reshape(1, 512)
     out_w = load(out_weight)
     far_own, far_oth = out_block(idx, [3], u, squares, gain, out_w)
-    far_sum = swap_add(far_own, far_oth)
+    far_sum = far_own + flip(far_oth, "tp", 1).astype(F32)
     got_a = along_x(narrow(far_sum[:32]), 1)
     got_b = along_x(narrow(far_sum[32:]), -1)
     rest_own, rest_oth = out_block(idx, [2, 1, 0], u, squares, gain, out_w)
-    rest = swap_add(rest_own, rest_oth)
-    ahead_sum, behind_sum, mine_sum = rest[:64], rest[64:128], rest[128:]
+    rest_got = flip(rest_oth, "tp", 1)
     half = out_w.shape[1] // 2
     outs = []
     moved = []
     for n in range(2):
         cols = slice(n * half, n * half + half)
-        to_right = narrow(
-            jnp.concatenate([ahead_sum[:32, cols] + widen(got_a[:, cols]), ahead_sum[32:, cols]], axis=0)
-        )
-        to_left = narrow(
-            jnp.concatenate([behind_sum[:32, cols], behind_sum[32:, cols] + widen(got_b[:, cols])], axis=0)
-        )
+
+        def rest_sum(rows):
+            return rest_own[rows, cols] + rest_got[rows, cols].astype(F32)
+
+        to_right = narrow(rest_sum(slice(0, 64)) + jnp.pad(widen(got_a[:, cols]), ((0, 32), (0, 0))))
+        to_left = narrow(rest_sum(slice(64, 128)) + jnp.pad(widen(got_b[:, cols]), ((32, 0), (0, 0))))
         from_left = along_x(to_right, 1)
         from_right = along_x(to_left, -1)
-        moved.append((mine_sum[:, cols], from_left, from_right))
+        moved.append((rest_sum(slice(128, 192)), from_left, from_right))
     for n in range(2):
         own, from_left, from_right = moved[n]
 
@@ -779,10 +798,6 @@
 
 def widen(value):
     return value.astype(F32) * 0.03125
-
-
-def swap_add(own, other):
-    return own + widen(flip(narrow(other), "tp", 1))
 
 
 def solution(mesh):

time: 163 us -> 171 us (1.049); the launches traced: 160 us -> 170 us
  starting transfers between devices: 62.2 us -> 68.6 us
  local copies, waits for them, and re-layouts: 5.47 us -> 1.2 us
  waiting for transfers between devices: 53 us -> 56.7 us
  Pallas kernels: 33.2 us -> 36.7 us
    ppermute x42 -> x45, waiting for transfers between devices: 47.3 us -> 54 us  [send(): return lax.ppermute(array, axis, pairs)]
    ppermute x42 -> x45, starting transfers between devices: 58.3 us -> 63.2 us  [send(): return lax.ppermute(array, axis, pairs)]
    unnamed x25 -> x20, local copies, waits for them, and re-layouts: 5.15 us -> 0.97 us
    ppermute x4, waiting for transfers between devices: 5.69 us -> 2.74 us  [hop(): return lax.ppermute(array, ('ctx', 'tp'), pairs)]
    pallas_call x3, Pallas kernels: 9.12 us -> 11.1 us  [project_resident(): pl.pallas_call(kernel, out_shape=outs, in_specs=[SM] + [VM] * (nl + 2) +...]
  transfers between devices with their start and end apart: 46 -> 49, of which waited for: 19 -> 23; matrix products, arithmetic and copies ran while one was open for 3% -> 3% of each run, Pallas kernels for 12% -> 14%
where the time goes in v2:
time: 171 us; the launch traced here: 170 us
  starting transfers between devices  68.6 us (40%)
  waiting for transfers between devices  56.7 us (33%)
  Pallas kernels  36.7 us (21%)
  other arithmetic  5.84 us (3%)
    ppermute x45, starting transfers between devices, send(): return lax.ppermute(array, axis, pairs)  63.2 us
    ppermute x45, waiting for transfers between devices, send(): return lax.ppermute(array, axis, pairs)  54 us
    pallas_call x3, Pallas kernels, project_resident(): pl.pallas_call(kernel, out_shape=outs, in_specs=[SM] + [VM] * (nl + 2) +...  11.1 us
    pallas_call x2, Pallas kernels, out_block(): pl.pallas_call(kernel, out_shape=[sds((rows, 4096), F32), sds((rows, 4096...  6.31 us
    ppermute x4, starting transfers between devices, hop(): return lax.ppermute(array, ('ctx', 'tp'), pairs)  5.42 us
    pallas_call x1, Pallas kernels, project(): pl.pallas_call(kernel, out_shape=outs, grid_spec=pltpu.PrefetchScalarGrid...  5.1 us
    pallas_call x1, Pallas kernels, scan_stage(): pl.pallas_call(scan_kernel, out_shape=[sds((512, 512), F32), sds((512, 25...  4.15 us
    pallas_call x1, Pallas kernels, inputs_stage(): pl.pallas_call(inputs_kernel, out_shape=[sds((512, 512), BF16)] * 3 + [sd...  3.44 us
  transfers between devices with their start and end apart: 49, of which 23 were waited for; matrix products, arithmetic and copies ran while one was open for 3% of the time, Pallas kernels for 14%

profile of v2, /device:TPU:24, one launch (start us, length us, event | category | flops | bytes accessed | tf_op | source)
XLA Modules:
  0.0 169.9 jit_solution(6351195601051208497)
XLA Ops:
  1.9 3.3 %collective-permute-start.3 = (bf16[16,4096]{1,0:T(8,128)(2,1)}, bf16[16,4096]{1,0:T(8,128)(2,1)S(1)}, u32[]{:S(2)}, u32[]{:S(2)}) collective-permute-start(bf16[16,4096]{1,0:T(8,128)(2,1)} %param.12), channel_id=1, source_target_pairs={{0,4},{1,5},{2,6},{3,7},{4,0},{5,1},{6,2},{7,3},{8,12},{9,13},{10,... | collective-permute-start | bytes 393224 | tf_op jit(solution)/shard_map/ppermute | solution.py:33
  6.8 8.6 %collective-permute-done.3 = bf16[16,4096]{1,0:T(8,128)(2,1)S(1)} collective-permute-done((bf16[16,4096]{1,0:T(8,128)(2,1)}, bf16[16,4096]{1,0:T(8,128)(2,1)S(1)}, u32[]{:S(2)}, u32[]{:S(2)}) %collective-permute-start.3) | collective-permute-done | bytes 131104 | tf_op jit(solution)/shard_map/ppermute | solution.py:33
  21.2 6.7 %collective-permute-start.16 = (bf16[32,4096]{1,0:T(8,128)(2,1)S(1)}, bf16[32,4096]{1,0:T(8,128)(2,1)S(1)}, u32[]{:S(2)}, u32[]{:S(2)}) collective-permute-start(bf16[32,4096]{1,0:T(8,128)(2,1)S(1)} %constant_dynamic-update-slice_fusion.refs_0_), channel_id=1, source_target_pairs={{0,24},{1,25},{2,26},{3,27},{4,28},{5,29},{6,30},{7,31},{8,0},{9,1... | collective-permute-start | bytes 786440 | tf_op jit(solution)/shard_map/ppermute | solution.py:33
  27.9 2.7 %collective-permute-done.9 = bf16[8,4096]{1,0:T(8,128)(2,1)S(1)} collective-permute-done((bf16[8,4096]{1,0:T(8,128)(2,1)S(1)}, bf16[8,4096]{1,0:T(8,128)(2,1)S(1)}, u32[]{:S(2)}, u32[]{:S(2)}) %collective-permute-start.9) | collective-permute-done | bytes 65568 | tf_op jit(solution)/shard_map/ppermute | solution.py:39
  32.8 3.4 %collective-permute-done.1.refs_0_.refs_4_ = bf16[32,4096]{1,0:T(8,128)(2,1)S(1)} collective-permute-done((bf16[32,4096]{1,0:T(8,128)(2,1)S(1)}, bf16[32,4096]{1,0:T(8,128)(2,1)S(1)}, u32[]{:S(2)}, u32[]{:S(2)}) %collective-permute-start.1) | collective-permute-done | bytes 262176 | tf_op jit(solution)/shard_map/ppermute | solution.py:33
  39.4 3.7 %collective-permute-start.10 = (bf16[32,4096]{1,0:T(8,128)(2,1)S(1)}, bf16[32,4096]{1,0:T(8,128)(2,1)S(1)}, u32[]{:S(2)}, u32[]{:S(2)}) collective-permute-start(bf16[32,4096]{1,0:T(8,128)(2,1)S(1)} %collective-permute-done.6.refs_5_.refs_9_), channel_id=1, source_target_pairs={{0,24},{1,25},{2,26},{3,27},{4,28},{5,29},{6,30},{7,31},{8,0},{9,1... | collective-permute-start | bytes 786440 | tf_op jit(solution)/shard_map/ppermute | solution.py:33
  43.2 3.7 %collective-permute-done.2.refs_0_.refs_12_ = bf16[32,4096]{1,0:T(8,128)(2,1)S(1)} collective-permute-done((bf16[32,4096]{1,0:T(8,128)(2,1)S(1)}, bf16[32,4096]{1,0:T(8,128)(2,1)S(1)}, u32[]{:S(2)}, u32[]{:S(2)}) %collective-permute-start.2) | collective-permute-done | bytes 262176 | tf_op jit(solution)/shard_map/ppermute | solution.py:33
  48.5 2.7 %collective-permute-start.13 = (bf16[8,4096]{1,0:T(8,128)(2,1)S(1)}, bf16[8,4096]{1,0:T(8,128)(2,1)S(1)}, u32[]{:S(2)}, u32[]{:S(2)}) collective-permute-start(bf16[8,4096]{1,0:T(8,128)(2,1)S(1)} %add.202), channel_id=1, source_target_pairs={{0,8},{1,9},{2,10},{3,11},{4,12},{5,13},{6,14},{7,15},{24,16},{25,... | collective-permute-start | bytes 196616 | tf_op jit(solution)/shard_map/ppermute | solution.py:39
  51.1 3.4 %shard_map.118 = (bf16[512,512]{1,0:T(8,128)(2,1)S(1)}, bf16[512,128]{1,0:T(8,128)(2,1)S(1)}, f32[8,512]{1,0:T(8,128)S(1)}) custom-call(s32[16]{0:T(128)S(1)} %compare_select_fusion.9.i.idx, bf16[32,4096]{1,0:T(8,128)(2,1)S(1)} %constant_dynamic-update-slice_fusion.refs_0_, bf16[32,4096]{1,0:T(8,128)(2,1)S(1)} %constant_dynamic-update-slice_fusion.2.refs_1_, ...), custom_call_target="tpu_custom_call" | custom-call | flops 805306368 | bytes 6291456 | tf_op jit(solution)/shard_map/pallas_call | solution.py:245
  54.6 4.2 %shard_map.119 = (bf16[512,512]{1,0:T(8,128)(2,1)S(1)}, bf16[512,128]{1,0:T(8,128)(2,1)S(1)}, f32[8,512]{1,0:T(8,128)S(1)}) custom-call(s32[16]{0:T(128)S(1)} %compare_select_fusion.9.i.idx, bf16[32,4096]{1,0:T(8,128)(2,1)S(1)} %collective-permute-done.1.refs_0_.refs_4_, ...), custom_call_target="tpu_custom_call", output_to_operand_aliasing={{0}: (9, {}), {1}: (10, {}), {2}: (11, {})} | custom-call | flops 1610612736 | bytes 6291456 | tf_op jit(solution)/shard_map/pallas_call | solution.py:245
  58.9 3.5 %shard_map.120 = (bf16[512,512]{1,0:T(8,128)(2,1)S(1)}, bf16[512,128]{1,0:T(8,128)(2,1)S(1)}, f32[8,512]{1,0:T(8,128)S(1)}, bf16[16,640]{1,0:T(8,128)(2,1)S(1)}) custom-call(s32[16]{0:T(128)S(1)} %compare_select_fusion.9.i.idx, ...), custom_call_target="tpu_custom_call", output_to_operand_aliasing={{0}: (8, {}), {1}: (9, {}), {2}: (10, {})} | custom-call | flops 805306368 | bytes 6291456 | tf_op jit(solution)/shard_map/pallas_call | solution.py:245
  65.3 3.6 %collective-permute-start.22 = (bf16[256,128]{1,0:T(8,128)(2,1)S(1)}, bf16[256,128]{1,0:T(8,128)(2,1)S(1)}, u32[]{:S(2)}, u32[]{:S(2)}) collective-permute-start(bf16[256,128]{1,0:T(8,128)(2,1)S(1)} %conv_states.1), channel_id=1, source_target_pairs={{0,4},{1,5},{2,6},{3,7},{4,0},{5,1},{6,2},{7,3},{8,12},{9,13},{10,... | collective-permute-start | bytes 196616 | tf_op jit(solution)/shard_map/ppermute | solution.py:33
  69.4 4.5 %collective-permute-done.22 = bf16[256,128]{1,0:T(8,128)(2,1)S(1)} collective-permute-done((bf16[256,128]{1,0:T(8,128)(2,1)S(1)}, bf16[256,128]{1,0:T(8,128)(2,1)S(1)}, u32[]{:S(2)}, u32[]{:S(2)}) %collective-permute-start.22) | collective-permute-done | bytes 65568 | tf_op jit(solution)/shard_map/ppermute | solution.py:33
  74.1 3.4 %inputs_stage.1 = (bf16[512,512]{1,0:T(8,128)(2,1)S(1)}, bf16[512,512]{1,0:T(8,128)(2,1)S(1)}, bf16[512,512]{1,0:T(8,128)(2,1)S(1)}, f32[8,512]{1,0:T(8,128)S(1)}, f32[8,512]{1,0:T(8,128)S(1)}) custom-call(f32[24]{0:T(128)S(1)} %pad_maximum_fusion.5.par_ref, bf16[512,512]{1,0:T(8,128)(2,1)S(1)} %get-tuple-element.49.rows_ref, ...), custom_call_target="tpu_custom_call" | custom-call | flops 10000000 | bytes 2000000 | tf_op jit(solution)/shard_map/inputs_stage/pallas_call | solution.py:353
  77.6 5.1 %shard_map.121.gate_ref = bf16[512,512]{1,0:T(8,128)(2,1)S(1)} custom-call(s32[16]{0:T(128)S(1)} %compare_select_fusion.9.i.idx, bf16[32,4096]{1,0:T(8,128)(2,1)S(1)} %constant_dynamic-update-slice_fusion.refs_0_, bf16[32,4096]{1,0:T(8,128)(2,1)S(1)} %constant_dynamic-update-slice_fusion.2.refs_1_, bf16[32,4096]{1,0:T(8,128)(2,1)S(1)} %collective-permute-done.5.refs_2_, ...), custom_call_target="tpu_custom_call" | custom-call | flops 2147483648 | bytes 4194304 | tf_op jit(solution)/shard_map/pallas_call | solution.py:160
  84.1 4.6 %collective-permute-start.27 = (f16[272,128]{1,0:T(8,128)(2,1)S(1)}, f16[272,128]{1,0:T(8,128)(2,1)S(1)}, u32[]{:S(2)}, u32[]{:S(2)}) collective-permute-start(f16[272,128]{1,0:T(8,128)(2,1)S(1)} %get-tuple-element.86), channel_id=1, source_target_pairs={{0,96},{32,64},{64,32},{96,0},{128,224},{160,192},{192,160},{224,1... | collective-permute-start | bytes 208904 | tf_op jit(solution)/shard_map/ppermute | solution.py:33
  92.4 8.1 %collective-permute-start.28 = (f16[272,128]{1,0:T(8,128)(2,1)S(1)}, f16[272,128]{1,0:T(8,128)(2,1)S(1)}, u32[]{:S(2)}, u32[]{:S(2)}) collective-permute-start(f16[272,128]{1,0:T(8,128)(2,1)S(1)} %convert_element_type.201), channel_id=1, source_target_pairs={{0,128},{32,160},{64,192},{96,224},{128,0},{160,32},{192,64},{224,... | collective-permute-start | bytes 208904 | tf_op jit(solution)/shard_map/ppermute | solution.py:33
  100.5 4.2 %scan_stage.1 = (f32[512,512]{1,0:T(8,128)S(1)}, bf16[512,256]{1,0:T(8,128)(2,1)S(1)}) custom-call(s32[16]{0:T(128)S(1)} %compare_select_fusion.9.i.idx, f32[24]{0:T(128)S(1)} %pad_maximum_fusion.5.par_ref, bf16[4,256,128]{2,1,0:T(8,128)(2,1)S(1)} %pad_maximum_fusion.2.own_ref, bf16[4,256,128]{2,1,0:T(8,128)(2,1)S(1)} %collective-permute-done.24.oth_ref, ...), custom_call_target="tpu_custom_call" | custom-call | flops 6000000000 | bytes 3000000 | tf_op jit(solution)/shard_map/scan_stage/pallas_call | solution.py:538
  105.6 2.1 %collective-permute-start.30 = (f16[272,128]{1,0:T(8,128)(2,1)S(1)}, f16[272,128]{1,0:T(8,128)(2,1)S(1)}, u32[]{:S(2)}, u32[]{:S(2)}) collective-permute-start(f16[272,128]{1,0:T(8,128)(2,1)S(1)} %get-tuple-element.84), channel_id=1, source_target_pairs={{0,64},{32,96},{64,0},{96,32},{128,192},{160,224},{192,128},{224,1... | collective-permute-start | bytes 208904 | tf_op jit(solution)/shard_map/ppermute | solution.py:33
  107.7 2.6 %collective-permute-start.31 = (f16[272,128]{1,0:T(8,128)(2,1)S(1)}, f16[272,128]{1,0:T(8,128)(2,1)S(1)}, u32[]{:S(2)}, u32[]{:S(2)}) collective-permute-start(f16[272,128]{1,0:T(8,128)(2,1)S(1)} %get-tuple-element.83), channel_id=1, source_target_pairs={{0,96},{32,64},{64,32},{96,0},{128,224},{160,192},{192,160},{224,1... | collective-permute-start | bytes 208904 | tf_op jit(solution)/shard_map/ppermute | solution.py:33
  113.2 3.0 %gate_stage.1 = (f32[512,512]{1,0:T(8,128)S(1)}, f32[4,128]{1,0:T(4,128)S(1)}) custom-call(s32[16]{0:T(128)S(1)} %compare_select_fusion.9.i.idx, f32[512,512]{1,0:T(8,128)S(1)} %get-tuple-element.54.y_ref, bf16[512,256]{1,0:T(8,128)(2,1)S(1)} %get-tuple-element.55.read_ref, f32[272,128]{1,0:T(8,128)S(1)} %slice_bitcast_fusion.q0, ...), custom_call_target="tpu_custom_call" | custom-call | flops 200000000 | bytes 3000000 | tf_op jit(solution)/shard_map/gate_stage/pallas_call | solution.py:580
  117.9 3.2 %collective-permute-done.33 = f32[4,128]{1,0:T(4,128)S(1)} collective-permute-done((f32[4,128]{1,0:T(4,128)S(1)}, f32[4,128]{1,0:T(4,128)S(1)}, u32[]{:S(2)}, u32[]{:S(2)}) %collective-permute-start.33) | collective-permute-done | bytes 2080 | tf_op jit(solution)/shard_map/ppermute | solution.py:33
  122.2 3.4 %collective-permute-done.34 = f32[4,128]{1,0:T(4,128)S(1)} collective-permute-done((f32[4,128]{1,0:T(4,128)S(1)}, f32[4,128]{1,0:T(4,128)S(1)}, u32[]{:S(2)}, u32[]{:S(2)}) %collective-permute-start.34) | collective-permute-done | bytes 2080 | tf_op jit(solution)/shard_map/ppermute | solution.py:33
  125.6 2.6 %out_block.3 = (f32[64,4096]{1,0:T(8,128)S(1)}, bf16[64,4096]{1,0:T(8,128)(2,1)S(1)}) custom-call(s32[16]{0:T(128)S(1)} %compare_select_fusion.9.i.idx, f32[512,512]{1,0:T(8,128)S(1)} %get-tuple-element.61.u_ref, f32[4,128]{1,0:T(4,128)S(1)} %add.206.ss_ref, f32[1,512]{1,0:T(1,128)S(1)} %bitcast.26, bf16[512,4096]{1,0:T(8,128)(2,1)S(1)} %load.1.w_ref), custom_call_target="tpu_custom_call" | custom-call | flops 536870912 | bytes 6000000 | tf_op jit(solution)/shard_map/out_block/pallas_call | solution.py:637
  128.3 3.7 %out_block.2 = (f32[192,4096]{1,0:T(8,128)S(1)}, bf16[192,4096]{1,0:T(8,128)(2,1)S(1)}) custom-call(s32[16]{0:T(128)S(1)} %compare_select_fusion.9.i.idx, f32[512,512]{1,0:T(8,128)S(1)} %get-tuple-element.61.u_ref, f32[4,128]{1,0:T(4,128)S(1)} %add.206.ss_ref, f32[1,512]{1,0:T(1,128)S(1)} %bitcast.27, bf16[512,4096]{1,0:T(8,128)(2,1)S(1)} %load.1.w_ref), custom_call_target="tpu_custom_call" | custom-call | flops 1610612736 | bytes 6000000 | tf_op jit(solution)/shard_map/out_block/pallas_call | solution.py:637
  133.5 2.7 %collective-permute-start.39 = (f16[32,4096]{1,0:T(8,128)(2,1)S(1)}, f16[32,4096]{1,0:T(8,128)(2,1)S(1)}, u32[]{:S(2)}, u32[]{:S(2)}) collective-permute-start(f16[32,4096]{1,0:T(8,128)(2,1)S(1)} %get-tuple-element.80), channel_id=1, source_target_pairs={{0,24},{1,25},{2,26},{3,27},{4,28},{5,29},{6,30},{7,31},{8,0},{9,1... | collective-permute-start | bytes 786440 | tf_op jit(solution)/shard_map/ppermute | solution.py:33
  136.1 6.2 %collective-permute-done.37 = f16[32,4096]{1,0:T(8,128)(2,1)S(1)} collective-permute-done((f16[32,4096]{1,0:T(8,128)(2,1)S(1)}, f16[32,4096]{1,0:T(8,128)(2,1)S(1)}, u32[]{:S(2)}, u32[]{:S(2)}) %collective-permute-start.37) | collective-permute-done | bytes 262176 | tf_op jit(solution)/shard_map/ppermute | solution.py:33
  143.2 3.0 %collective-permute-start.45 = (f16[64,2048]{1,0:T(8,128)(2,1)S(1)}, f16[64,2048]{1,0:T(8,128)(2,1)S(1)}, u32[]{:S(2)}, u32[]{:S(2)}) collective-permute-start(f16[64,2048]{1,0:T(8,128)(2,1)S(1)} %get-tuple-element.68), channel_id=1, source_target_pairs={{0,24},{1,25},{2,26},{3,27},{4,28},{5,29},{6,30},{7,31},{8,0},{9,1... | collective-permute-start | bytes 786440 | tf_op jit(solution)/shard_map/ppermute | solution.py:33
  146.1 3.2 %collective-permute-start.40 = (f16[64,2048]{1,0:T(8,128)(2,1)S(1)}, f16[64,2048]{1,0:T(8,128)(2,1)S(1)}, u32[]{:S(2)}, u32[]{:S(2)}) collective-permute-start(f16[64,2048]{1,0:T(8,128)(2,1)S(1)} %get-tuple-element.71), channel_id=1, source_target_pairs={{0,24},{1,25},{2,26},{3,27},{4,28},{5,29},{6,30},{7,31},{8,0},{9,1... | collective-permute-start | bytes 786440 | tf_op jit(solution)/shard_map/ppermute | solution.py:33
  149.4 3.5 %collective-permute-done.45 = f16[64,2048]{1,0:T(8,128)(2,1)S(1)} collective-permute-done((f16[64,2048]{1,0:T(8,128)(2,1)S(1)}, f16[64,2048]{1,0:T(8,128)(2,1)S(1)}, u32[]{:S(2)}, u32[]{:S(2)}) %collective-permute-start.45) | collective-permute-done | bytes 262176 | tf_op jit(solution)/shard_map/ppermute | solution.py:33
  152.8 3.7 %collective-permute-done.44 = f16[64,2048]{1,0:T(8,128)(2,1)S(1)} collective-permute-done((f16[64,2048]{1,0:T(8,128)(2,1)S(1)}, f16[64,2048]{1,0:T(8,128)(2,1)S(1)}, u32[]{:S(2)}, u32[]{:S(2)}) %collective-permute-start.44) | collective-permute-done | bytes 262176 | tf_op jit(solution)/shard_map/ppermute | solution.py:33
  158.6 2.5 %collective-permute-start.46 = (f16[16,2048]{1,0:T(8,128)(2,1)S(1)}, f16[16,2048]{1,0:T(8,128)(2,1)S(1)}, u32[]{:S(2)}, u32[]{:S(2)}) collective-permute-start(f16[16,2048]{1,0:T(8,128)(2,1)S(1)} %get-tuple-element.76), channel_id=1, source_target_pairs={{0,2},{1,3},{2,0},{3,1},{4,6},{5,7},{6,4},{7,5},{8,10},{9,11},{10,... | collective-permute-start | bytes 196616 | tf_op jit(solution)/shard_map/ppermute | solution.py:33
  (145 shorter events, 44.4 us)
Async XLA Ops:
  0.0 6.8 %collective-permute-start = (bf16[16,4096]{1,0:T(8,128)(2,1)}, bf16[16,4096]{1,0:T(8,128)(2,1)S(1)}, u32[]{:S(2)}, u32[]{:S(2)}) collective-permute-start(bf16[16,4096]{1,0:T(8,128)(2,1)} %param.12), channel_id=1, source_target_pairs={{0,2},{1,3},{2,0},{3,1},{4,6},{5,7},{6,4},{7,5},{8,10},{9,11},{10,... | collective-permute-start | bytes 393224 | tf_op jit(solution)/shard_map/ppermute | solution.py:33
  1.9 13.5 %collective-permute-start.3 = (bf16[16,4096]{1,0:T(8,128)(2,1)}, bf16[16,4096]{1,0:T(8,128)(2,1)S(1)}, u32[]{:S(2)}, u32[]{:S(2)}) collective-permute-start(bf16[16,4096]{1,0:T(8,128)(2,1)} %param.12), channel_id=1, source_target_pairs={{0,4},{1,5},{2,6},{3,7},{4,0},{5,1},{6,2},{7,3},{8,12},{9,13},{10,... | collective-permute-start | bytes 393224 | tf_op jit(solution)/shard_map/ppermute | solution.py:33
  5.2 10.2 %collective-permute-start.4 = (bf16[16,4096]{1,0:T(8,128)(2,1)}, bf16[16,4096]{1,0:T(8,128)(2,1)S(1)}, u32[]{:S(2)}, u32[]{:S(2)}) collective-permute-start(bf16[16,4096]{1,0:T(8,128)(2,1)} %param.12), channel_id=1, source_target_pairs={{0,6},{1,7},{2,4},{3,5},{4,2},{5,3},{6,0},{7,1},{8,14},{9,15},{10,... | collective-permute-start | bytes 393224 | tf_op jit(solution)/shard_map/ppermute | solution.py:33
  5.2 31.7 %collective-permute-start.14 = (bf16[64,4096]{1,0:T(8,128)(2,1)}, bf16[64,4096]{1,0:T(8,128)(2,1)S(1)}, u32[]{:S(2)}, u32[]{:S(2)}) collective-permute-start(bf16[64,4096]{1,0:T(8,128)(2,1)} %bitcast.28), channel_id=1, source_target_pairs={{0,1},{1,0},{2,3},{3,2},{4,5},{5,4},{6,7},{7,6},{8,9},{9,8},{10,11... | collective-permute-start | bytes 1572872 | tf_op jit(solution)/shard_map/ppermute | solution.py:33
  5.2 12.7 %collective-permute-start.20 = (f32[5,64]{1,0:T(8,128)}, f32[5,64]{1,0:T(8,128)S(1)}, u32[]{:S(2)}, u32[]{:S(2)}) collective-permute-start(f32[5,64]{1,0:T(8,128)} %param.18), channel_id=1, source_target_pairs={{0,1},{1,0},{2,3},{3,2},{4,5},{5,4},{6,7},{7,6},{8,9},{9,8},{10,11... | collective-permute-start | bytes 3848 | tf_op jit(solution)/shard_map/ppermute | solution.py:33
  17.0 13.7 %collective-permute-start.5 = (bf16[32,4096]{1,0:T(8,128)(2,1)S(1)}, bf16[32,4096]{1,0:T(8,128)(2,1)S(1)}, u32[]{:S(2)}, u32[]{:S(2)}) collective-permute-start(bf16[32,4096]{1,0:T(8,128)(2,1)S(1)} %constant_dynamic-update-slice_fusion.refs_0_), channel_id=1, source_target_pairs={{0,1},{1,0},{2,3},{3,2},{4,5},{5,4},{6,7},{7,6},{8,9},{9,8},{10,11... | collective-permute-start | bytes 786440 | tf_op jit(solution)/shard_map/ppermute | solution.py:33
  18.9 11.7 %collective-permute-start.9 = (bf16[8,4096]{1,0:T(8,128)(2,1)S(1)}, bf16[8,4096]{1,0:T(8,128)(2,1)S(1)}, u32[]{:S(2)}, u32[]{:S(2)}) collective-permute-start(bf16[8,4096]{1,0:T(8,128)(2,1)S(1)} %add.201), channel_id=1, source_target_pairs={{24,0},{25,1},{26,2},{27,3},{28,4},{29,5},{30,6},{31,7},{56,32},{5... | collective-permute-start | bytes 196616 | tf_op jit(solution)/shard_map/ppermute | solution.py:39
  20.3 15.9 %collective-permute-start.1 = (bf16[32,4096]{1,0:T(8,128)(2,1)S(1)}, bf16[32,4096]{1,0:T(8,128)(2,1)S(1)}, u32[]{:S(2)}, u32[]{:S(2)}) collective-permute-start(bf16[32,4096]{1,0:T(8,128)(2,1)S(1)} %constant_dynamic-update-slice_fusion.refs_0_), channel_id=1, source_target_pairs={{0,8},{1,9},{2,10},{3,11},{4,12},{5,13},{6,14},{7,15},{8,16},{9,17... | collective-permute-start | bytes 786440 | tf_op jit(solution)/shard_map/ppermute | solution.py:33
  21.2 15.1 %collective-permute-start.16 = (bf16[32,4096]{1,0:T(8,128)(2,1)S(1)}, bf16[32,4096]{1,0:T(8,128)(2,1)S(1)}, u32[]{:S(2)}, u32[]{:S(2)}) collective-permute-start(bf16[32,4096]{1,0:T(8,128)(2,1)S(1)} %constant_dynamic-update-slice_fusion.refs_0_), channel_id=1, source_target_pairs={{0,24},{1,25},{2,26},{3,27},{4,28},{5,29},{6,30},{7,31},{8,0},{9,1... | collective-permute-start | bytes 786440 | tf_op jit(solution)/shard_map/ppermute | solution.py:33
  30.7 8.7 %collective-permute-start.6 = (bf16[32,4096]{1,0:T(8,128)(2,1)S(1)}, bf16[32,4096]{1,0:T(8,128)(2,1)S(1)}, u32[]{:S(2)}, u32[]{:S(2)}) collective-permute-start(bf16[32,4096]{1,0:T(8,128)(2,1)S(1)} %constant_dynamic-update-slice_fusion.2.refs_1_), channel_id=1, source_target_pairs={{0,24},{1,25},{2,26},{3,27},{4,28},{5,29},{6,30},{7,31},{8,0},{9,1... | collective-permute-start | bytes 786440 | tf_op jit(solution)/shard_map/ppermute | solution.py:33
  30.8 12.3 %collective-permute-start.15 = (bf16[32,4096]{1,0:T(8,128)(2,1)S(1)}, bf16[32,4096]{1,0:T(8,128)(2,1)S(1)}, u32[]{:S(2)}, u32[]{:S(2)}) collective-permute-start(bf16[32,4096]{1,0:T(8,128)(2,1)S(1)} %constant_dynamic-update-slice_fusion.2.refs_1_), channel_id=1, source_target_pairs={{0,8},{1,9},{2,10},{3,11},{4,12},{5,13},{6,14},{7,15},{8,16},{9,17... | collective-permute-start | bytes 786440 | tf_op jit(solution)/shard_map/ppermute | solution.py:33
  36.2 12.2 %collective-permute-start.19 = (bf16[32,4096]{1,0:T(8,128)(2,1)S(1)}, bf16[32,4096]{1,0:T(8,128)(2,1)S(1)}, u32[]{:S(2)}, u32[]{:S(2)}) collective-permute-start(bf16[32,4096]{1,0:T(8,128)(2,1)S(1)} %constant_dynamic-update-slice_fusion.2.refs_1_), channel_id=1, source_target_pairs={{0,1},{1,0},{2,3},{3,2},{4,5},{5,4},{6,7},{7,6},{8,9},{9,8},{10,11... | collective-permute-start | bytes 786440 | tf_op jit(solution)/shard_map/ppermute | solution.py:33
  36.3 18.3 %collective-permute-start.17 = (bf16[64,4096]{1,0:T(8,128)(2,1)S(1)}, bf16[64,4096]{1,0:T(8,128)(2,1)S(1)}, u32[]{:S(2)}, u32[]{:S(2)}) collective-permute-start(bf16[64,4096]{1,0:T(8,128)(2,1)S(1)} %pad_maximum_fusion), channel_id=1, source_target_pairs={{0,1},{1,0},{2,3},{3,2},{4,5},{5,4},{6,7},{7,6},{8,9},{9,8},{10,11... | collective-permute-start | bytes 1572872 | tf_op jit(solution)/shard_map/ppermute | solution.py:33
  36.9 10.1 %collective-permute-start.2 = (bf16[32,4096]{1,0:T(8,128)(2,1)S(1)}, bf16[32,4096]{1,0:T(8,128)(2,1)S(1)}, u32[]{:S(2)}, u32[]{:S(2)}) collective-permute-start(bf16[32,4096]{1,0:T(8,128)(2,1)S(1)} %collective-permute-done.1.refs_0_.refs_4_), channel_id=1, source_target_pairs={{0,8},{1,9},{2,10},{3,11},{4,12},{5,13},{6,14},{7,15},{8,16},{9,17... | collective-permute-start | bytes 786440 | tf_op jit(solution)/shard_map/ppermute | solution.py:33
  39.4 8.7 %collective-permute-start.10 = (bf16[32,4096]{1,0:T(8,128)(2,1)S(1)}, bf16[32,4096]{1,0:T(8,128)(2,1)S(1)}, u32[]{:S(2)}, u32[]{:S(2)}) collective-permute-start(bf16[32,4096]{1,0:T(8,128)(2,1)S(1)} %collective-permute-done.6.refs_5_.refs_9_), channel_id=1, source_target_pairs={{0,24},{1,25},{2,26},{3,27},{4,28},{5,29},{6,30},{7,31},{8,0},{9,1... | collective-permute-start | bytes 786440 | tf_op jit(solution)/shard_map/ppermute | solution.py:33
  43.1 11.5 %collective-permute-start.18 = (bf16[64,4096]{1,0:T(8,128)(2,1)S(1)}, bf16[64,4096]{1,0:T(8,128)(2,1)S(1)}, u32[]{:S(2)}, u32[]{:S(2)}) collective-permute-start(bf16[64,4096]{1,0:T(8,128)(2,1)S(1)} %pad_maximum_fusion.1), channel_id=1, source_target_pairs={{0,1},{1,0},{2,3},{3,2},{4,5},{5,4},{6,7},{7,6},{8,9},{9,8},{10,11... | collective-permute-start | bytes 1572872 | tf_op jit(solution)/shard_map/ppermute | solution.py:33
  46.9 11.9 %collective-permute-start.11 = (bf16[32,4096]{1,0:T(8,128)(2,1)S(1)}, bf16[32,4096]{1,0:T(8,128)(2,1)S(1)}, u32[]{:S(2)}, u32[]{:S(2)}) collective-permute-start(bf16[32,4096]{1,0:T(8,128)(2,1)S(1)} %collective-permute-done.2.refs_0_.refs_12_), channel_id=1, source_target_pairs={{0,1},{1,0},{2,3},{3,2},{4,5},{5,4},{6,7},{7,6},{8,9},{9,8},{10,11... | collective-permute-start | bytes 786440 | tf_op jit(solution)/shard_map/ppermute | solution.py:33
  48.1 10.8 %collective-permute-start.12 = (bf16[32,4096]{1,0:T(8,128)(2,1)S(1)}, bf16[32,4096]{1,0:T(8,128)(2,1)S(1)}, u32[]{:S(2)}, u32[]{:S(2)}) collective-permute-start(bf16[32,4096]{1,0:T(8,128)(2,1)S(1)} %collective-permute-done.10.refs_1_.refs_13_), channel_id=1, source_target_pairs={{0,1},{1,0},{2,3},{3,2},{4,5},{5,4},{6,7},{7,6},{8,9},{9,8},{10,11... | collective-permute-start | bytes 786440 | tf_op jit(solution)/shard_map/ppermute | solution.py:33
  65.3 8.6 %collective-permute-start.22 = (bf16[256,128]{1,0:T(8,128)(2,1)S(1)}, bf16[256,128]{1,0:T(8,128)(2,1)S(1)}, u32[]{:S(2)}, u32[]{:S(2)}) collective-permute-start(bf16[256,128]{1,0:T(8,128)(2,1)S(1)} %conv_states.1), channel_id=1, source_target_pairs={{0,4},{1,5},{2,6},{3,7},{4,0},{5,1},{6,2},{7,3},{8,12},{9,13},{10,... | collective-permute-start | bytes 196616 | tf_op jit(solution)/shard_map/ppermute | solution.py:33
  73.9 8.8 %collective-permute-start.24 = (bf16[4,256,128]{2,1,0:T(8,128)(2,1)S(1)}, bf16[4,256,128]{2,1,0:T(8,128)(2,1)S(1)}, u32[]{:S(2)}, u32[]{:S(2)}) collective-permute-start(bf16[4,256,128]{2,1,0:T(8,128)(2,1)S(1)} %pad_maximum_fusion.2.own_ref), channel_id=1, source_target_pairs={{0,1},{1,0},{2,3},{3,2},{4,5},{5,4},{6,7},{7,6},{8,9},{9,8},{10,11... | collective-permute-start | bytes 786440 | tf_op jit(solution)/shard_map/ppermute | solution.py:33
  84.1 7.5 %collective-permute-start.27 = (f16[272,128]{1,0:T(8,128)(2,1)S(1)}, f16[272,128]{1,0:T(8,128)(2,1)S(1)}, u32[]{:S(2)}, u32[]{:S(2)}) collective-permute-start(f16[272,128]{1,0:T(8,128)(2,1)S(1)} %get-tuple-element.86), channel_id=1, source_target_pairs={{0,96},{32,64},{64,32},{96,0},{128,224},{160,192},{192,160},{224,1... | collective-permute-start | bytes 208904 | tf_op jit(solution)/shard_map/ppermute | solution.py:33
  92.4 12.2 %collective-permute-start.28 = (f16[272,128]{1,0:T(8,128)(2,1)S(1)}, f16[272,128]{1,0:T(8,128)(2,1)S(1)}, u32[]{:S(2)}, u32[]{:S(2)}) collective-permute-start(f16[272,128]{1,0:T(8,128)(2,1)S(1)} %convert_element_type.201), channel_id=1, source_target_pairs={{0,128},{32,160},{64,192},{96,224},{128,0},{160,32},{192,64},{224,... | collective-permute-start | bytes 208904 | tf_op jit(solution)/shard_map/ppermute | solution.py:33
  132.0 10.5 %collective-permute-start.35 = (bf16[192,4096]{1,0:T(8,128)(2,1)S(1)}, bf16[192,4096]{1,0:T(8,128)(2,1)S(1)}, u32[]{:S(2)}, u32[]{:S(2)}) collective-permute-start(bf16[192,4096]{1,0:T(8,128)(2,1)S(1)} %get-tuple-element.64), channel_id=1, source_target_pairs={{0,1},{1,0},{2,3},{3,2},{4,5},{5,4},{6,7},{7,6},{8,9},{9,8},{10,11... | collective-permute-start | bytes 4718600 | tf_op jit(solution)/shard_map/ppermute | solution.py:33
  132.8 9.5 %collective-permute-start.37 = (f16[32,4096]{1,0:T(8,128)(2,1)S(1)}, f16[32,4096]{1,0:T(8,128)(2,1)S(1)}, u32[]{:S(2)}, u32[]{:S(2)}) collective-permute-start(f16[32,4096]{1,0:T(8,128)(2,1)S(1)} %get-tuple-element.79), channel_id=1, source_target_pairs={{0,8},{1,9},{2,10},{3,11},{4,12},{5,13},{6,14},{7,15},{8,16},{9,17... | collective-permute-start | bytes 786440 | tf_op jit(solution)/shard_map/ppermute | solution.py:33
  133.5 8.9 %collective-permute-start.39 = (f16[32,4096]{1,0:T(8,128)(2,1)S(1)}, f16[32,4096]{1,0:T(8,128)(2,1)S(1)}, u32[]{:S(2)}, u32[]{:S(2)}) collective-permute-start(f16[32,4096]{1,0:T(8,128)(2,1)S(1)} %get-tuple-element.80), channel_id=1, source_target_pairs={{0,24},{1,25},{2,26},{3,27},{4,28},{5,29},{6,30},{7,31},{8,0},{9,1... | collective-permute-start | bytes 786440 | tf_op jit(solution)/shard_map/ppermute | solution.py:33
  143.2 9.7 %collective-permute-start.45 = (f16[64,2048]{1,0:T(8,128)(2,1)S(1)}, f16[64,2048]{1,0:T(8,128)(2,1)S(1)}, u32[]{:S(2)}, u32[]{:S(2)}) collective-permute-start(f16[64,2048]{1,0:T(8,128)(2,1)S(1)} %get-tuple-element.68), channel_id=1, source_target_pairs={{0,24},{1,25},{2,26},{3,27},{4,28},{5,29},{6,30},{7,31},{8,0},{9,1... | collective-permute-start | bytes 786440 | tf_op jit(solution)/shard_map/ppermute | solution.py:33
  146.1 10.4 %collective-permute-start.44 = (f16[64,2048]{1,0:T(8,128)(2,1)S(1)}, f16[64,2048]{1,0:T(8,128)(2,1)S(1)}, u32[]{:S(2)}, u32[]{:S(2)}) collective-permute-start(f16[64,2048]{1,0:T(8,128)(2,1)S(1)} %get-tuple-element.69), channel_id=1, source_target_pairs={{0,8},{1,9},{2,10},{3,11},{4,12},{5,13},{6,14},{7,15},{8,16},{9,17... | collective-permute-start | bytes 786440 | tf_op jit(solution)/shard_map/ppermute | solution.py:33
  146.1 15.0 %collective-permute-start.40 = (f16[64,2048]{1,0:T(8,128)(2,1)S(1)}, f16[64,2048]{1,0:T(8,128)(2,1)S(1)}, u32[]{:S(2)}, u32[]{:S(2)}) collective-permute-start(f16[64,2048]{1,0:T(8,128)(2,1)S(1)} %get-tuple-element.71), channel_id=1, source_target_pairs={{0,24},{1,25},{2,26},{3,27},{4,28},{5,29},{6,30},{7,31},{8,0},{9,1... | collective-permute-start | bytes 786440 | tf_op jit(solution)/shard_map/ppermute | solution.py:33
  149.4 11.8 %collective-permute-start.38 = (f16[64,2048]{1,0:T(8,128)(2,1)S(1)}, f16[64,2048]{1,0:T(8,128)(2,1)S(1)}, u32[]{:S(2)}, u32[]{:S(2)}) collective-permute-start(f16[64,2048]{1,0:T(8,128)(2,1)S(1)} %get-tuple-element.67), channel_id=1, source_target_pairs={{0,8},{1,9},{2,10},{3,11},{4,12},{5,13},{6,14},{7,15},{8,16},{9,17... | collective-permute-start | bytes 786440 | tf_op jit(solution)/shard_map/ppermute | solution.py:33
  156.6 7.0 %collective-permute-start.48 = (f16[16,2048]{1,0:T(8,128)(2,1)S(1)}, f16[16,2048]{1,0:T(8,128)(2,1)S(1)}, u32[]{:S(2)}, u32[]{:S(2)}) collective-permute-start(f16[16,2048]{1,0:T(8,128)(2,1)S(1)} %get-tuple-element.77), channel_id=1, source_target_pairs={{0,6},{1,7},{2,4},{3,5},{4,2},{5,3},{6,0},{7,1},{8,14},{9,15},{10,... | collective-permute-start | bytes 196616 | tf_op jit(solution)/shard_map/ppermute | solution.py:33
  158.6 7.7 %collective-permute-start.47 = (f16[16,2048]{1,0:T(8,128)(2,1)S(1)}, f16[16,2048]{1,0:T(8,128)(2,1)S(1)}, u32[]{:S(2)}, u32[]{:S(2)}) collective-permute-start(f16[16,2048]{1,0:T(8,128)(2,1)S(1)} %get-tuple-element.78), channel_id=1, source_target_pairs={{0,4},{1,5},{2,6},{3,7},{4,0},{5,1},{6,2},{7,3},{8,12},{9,13},{10,... | collective-permute-start | bytes 196616 | tf_op jit(solution)/shard_map/ppermute | solution.py:33
  158.6 7.7 %collective-permute-start.46 = (f16[16,2048]{1,0:T(8,128)(2,1)S(1)}, f16[16,2048]{1,0:T(8,128)(2,1)S(1)}, u32[]{:S(2)}, u32[]{:S(2)}) collective-permute-start(f16[16,2048]{1,0:T(8,128)(2,1)S(1)} %get-tuple-element.76), channel_id=1, source_target_pairs={{0,2},{1,3},{2,0},{3,1},{4,6},{5,7},{6,4},{7,5},{8,10},{9,11},{10,... | collective-permute-start | bytes 196616 | tf_op jit(solution)/shard_map/ppermute | solution.py:33
  (26 other events, 262.4 us)

commit v3 on v2

--- a/solution.py
+++ b/solution.py
@@ -176,7 +176,7 @@
 
 def project_resident(parts, halo, slots, idx, input_w, small_w, bufs):
     depth = parts[0][0].shape[1]
-    kb = 512
+    kb = 1024 if halo is not None else 512
     count = len(slots)
     rows = 128 * count
     extra = 0 if halo is None else 16
@@ -311,24 +311,21 @@
     taps = taps_ref[...]
     rate = jnp.exp(column(par_ref, 0))
     bias = column(par_ref, 8)
-    lane = lax.broadcasted_iota(jnp.int32, (8, 128), 1)
-    dts, cums = [], []
-    for k in range(4):
-        raw = step_ref[:, 128 * k : 128 * k + 128] + bias
-        dt = jnp.maximum(raw, 0.0) + jnp.log1p(jnp.exp(-jnp.abs(raw)))
-        cum = -dt * rate
-        for b in range(7):
-            moved = pltpu.roll(cum, 1 << b, 1)
-            cum = cum + jnp.where(lane >= (1 << b), moved, 0.0)
-        dts.append(dt)
-        cums.append(cum)
-        dt_ref[:, 128 * k : 128 * k + 128] = dt
-        cum_ref[:, 128 * k : 128 * k + 128] = cum
+    lane = lax.bitwise_and(lax.broadcasted_iota(jnp.int32, (8, 512), 1), 127)
+    raw = step_ref[...] + jnp.concatenate([bias] * 4, axis=1)
+    dt = jnp.maximum(raw, 0.0) + jnp.log1p(jnp.exp(-jnp.abs(raw)))
+    cum = -dt * jnp.concatenate([rate] * 4, axis=1)
+    for b in range(7):
+        cum = cum + jnp.where(lane >= (1 << b), pltpu.roll(cum, 1 << b, 1), 0.0)
+    dt_ref[...] = dt
+    cum_ref[...] = cum
     after = jnp.zeros((8, 1), F32)
+    gaps = []
     for k in reversed(range(4)):
-        total = cums[k][:, 127:128]
-        weight_ref[:, 128 * k : 128 * k + 128] = jnp.exp(total - cums[k] + after) * dts[k]
+        total = cum[:, 128 * k + 127 : 128 * k + 128]
+        gaps.insert(0, jnp.broadcast_to(total + after, (8, 128)))
         after = after + total
+    weight_ref[...] = jnp.exp(jnp.concatenate(gaps, axis=1) - cum) * dt
     longer[0:16, :] = halo_ref[:, 0:512]
     longer[16:528, :] = rows_ref[...]
 
@@ -610,6 +607,7 @@
 def out_block(idx, slots, u, ss, gain, out_w):
     count = len(slots)
     rows = 64 * count
+    wide = 1024 if count == 1 else 512
 
     def kernel(i, u_ref, ss_ref, gain_ref, w_ref, own_ref, oth_ref, lhs):
         for s in range(count):
@@ -626,13 +624,13 @@
                     lhs[pl.ds(pl.multiple_of(at, 16), 16), ch] = normed[t * 16 : t * 16 + 16, :]
 
         def one(n, carry):
-            here = pl.ds(pl.multiple_of(n * 512, 512), 512)
+            here = pl.ds(pl.multiple_of(n * wide, wide), wide)
             part = dot(lhs[...], w_ref[:, here])
             own_ref[:, here] = part[0:rows, :]
             oth_ref[:, here] = part[rows : 2 * rows, :].astype(BF16)
             return carry
 
-        lax.fori_loop(0, 8, one, 0)
+        lax.fori_loop(0, 4096 // wide, one, 0)
 
     return pl.pallas_call(
         kernel,
@@ -711,7 +709,6 @@
     side1 = flip(jnp.concatenate([right1, left1], axis=0), "tp", 1)
     rim = rim + hop(rim, to["hc"])
     rim = rim + hop(rim, to["h1"])
-    left2, rim = lax.optimization_barrier((left2, rim))
     far_b = along_x(left2, -1)
     side2 = flip(jnp.concatenate([right2, left2], axis=0), "tp", 1)
     rim = rim + hop(rim, to["h2"])

time: 171 us -> 170 us (level)
  waiting for transfers between devices: 56.7 us -> 58.7 us
    ppermute x45, waiting for transfers between devices: 54 us -> 56 us  [send(): return lax.ppermute(array, axis, pairs)]
where the time goes in v3:
time: 170 us; the launch traced here: 169 us
  starting transfers between devices  67 us (39%)
  waiting for transfers between devices  58.7 us (35%)
  Pallas kernels  35.5 us (21%)
  other arithmetic  5.52 us (3%)
    ppermute x45, starting transfers between devices, send(): return lax.ppermute(array, axis, pairs)  62.8 us
    ppermute x45, waiting for transfers between devices, send(): return lax.ppermute(array, axis, pairs)  56 us
    pallas_call x3, Pallas kernels, project_resident(): pl.pallas_call(kernel, out_shape=outs, in_specs=[SM] + [VM] * (nl + 2) +...  10.5 us
    pallas_call x2, Pallas kernels, out_block(): pl.pallas_call(kernel, out_shape=[sds((rows, 4096), F32), sds((rows, 4096...  5.7 us
    pallas_call x1, Pallas kernels, project(): pl.pallas_call(kernel, out_shape=outs, grid_spec=pltpu.PrefetchScalarGrid...  5.1 us
    ppermute x4, starting transfers between devices, hop(): return lax.ppermute(array, ('ctx', 'tp'), pairs)  4.18 us
    pallas_call x1, Pallas kernels, scan_stage(): pl.pallas_call(scan_kernel, out_shape=[sds((512, 512), F32), sds((512, 25...  4.15 us
    pallas_call x1, Pallas kernels, inputs_stage(): pl.pallas_call(inputs_kernel, out_shape=[sds((512, 512), BF16)] * 3 + [sd...  3.45 us
  transfers between devices with their start and end apart: 49, of which 23 were waited for; matrix products, arithmetic and copies ran while one was open for 3% of the time, Pallas kernels for 14%

profile of v3, /device:TPU:24, one launch (start us, length us, event | category | flops | bytes accessed | tf_op | source)
XLA Modules:
  0.0 168.7 jit_solution(16021682911128563573)
XLA Ops:
  1.9 3.3 %collective-permute-start.3 = (bf16[16,4096]{1,0:T(8,128)(2,1)}, bf16[16,4096]{1,0:T(8,128)(2,1)S(1)}, u32[]{:S(2)}, u32[]{:S(2)}) collective-permute-start(bf16[16,4096]{1,0:T(8,128)(2,1)} %param.12), channel_id=1, source_target_pairs={{0,4},{1,5},{2,6},{3,7},{4,0},{5,1},{6,2},{7,3},{8,12},{9,13},{10,... | collective-permute-start | bytes 393224 | tf_op jit(solution)/shard_map/ppermute | solution.py:33
  6.8 8.6 %collective-permute-done.3 = bf16[16,4096]{1,0:T(8,128)(2,1)S(1)} collective-permute-done((bf16[16,4096]{1,0:T(8,128)(2,1)}, bf16[16,4096]{1,0:T(8,128)(2,1)S(1)}, u32[]{:S(2)}, u32[]{:S(2)}) %collective-permute-start.3) | collective-permute-done | bytes 131104 | tf_op jit(solution)/shard_map/ppermute | solution.py:33
  20.7 7.2 %collective-permute-start.16 = (bf16[32,4096]{1,0:T(8,128)(2,1)S(1)}, bf16[32,4096]{1,0:T(8,128)(2,1)S(1)}, u32[]{:S(2)}, u32[]{:S(2)}) collective-permute-start(bf16[32,4096]{1,0:T(8,128)(2,1)S(1)} %constant_dynamic-update-slice_fusion.refs_0_), channel_id=1, source_target_pairs={{0,24},{1,25},{2,26},{3,27},{4,28},{5,29},{6,30},{7,31},{8,0},{9,1... | collective-permute-start | bytes 786440 | tf_op jit(solution)/shard_map/ppermute | solution.py:33
  27.9 2.7 %collective-permute-done.12 = bf16[8,4096]{1,0:T(8,128)(2,1)S(1)} collective-permute-done((bf16[8,4096]{1,0:T(8,128)(2,1)S(1)}, bf16[8,4096]{1,0:T(8,128)(2,1)S(1)}, u32[]{:S(2)}, u32[]{:S(2)}) %collective-permute-start.12) | collective-permute-done | bytes 65568 | tf_op jit(solution)/shard_map/ppermute | solution.py:39
  32.4 3.3 %collective-permute-done.1.refs_0_.refs_4_ = bf16[32,4096]{1,0:T(8,128)(2,1)S(1)} collective-permute-done((bf16[32,4096]{1,0:T(8,128)(2,1)S(1)}, bf16[32,4096]{1,0:T(8,128)(2,1)S(1)}, u32[]{:S(2)}, u32[]{:S(2)}) %collective-permute-start.1) | collective-permute-done | bytes 262176 | tf_op jit(solution)/shard_map/ppermute | solution.py:33
  39.6 3.5 %collective-permute-start.7 = (bf16[32,4096]{1,0:T(8,128)(2,1)S(1)}, bf16[32,4096]{1,0:T(8,128)(2,1)S(1)}, u32[]{:S(2)}, u32[]{:S(2)}) collective-permute-start(bf16[32,4096]{1,0:T(8,128)(2,1)S(1)} %collective-permute-done.6.refs_5_.refs_9_), channel_id=1, source_target_pairs={{0,24},{1,25},{2,26},{3,27},{4,28},{5,29},{6,30},{7,31},{8,0},{9,1... | collective-permute-start | bytes 786440 | tf_op jit(solution)/shard_map/ppermute | solution.py:33
  43.1 3.0 %collective-permute-done.15.refs_1_.refs_5_ = bf16[32,4096]{1,0:T(8,128)(2,1)S(1)} collective-permute-done((bf16[32,4096]{1,0:T(8,128)(2,1)S(1)}, bf16[32,4096]{1,0:T(8,128)(2,1)S(1)}, u32[]{:S(2)}, u32[]{:S(2)}) %collective-permute-start.15) | collective-permute-done | bytes 262176 | tf_op jit(solution)/shard_map/ppermute | solution.py:33
  46.2 4.1 %collective-permute-done.2.refs_0_.refs_12_ = bf16[32,4096]{1,0:T(8,128)(2,1)S(1)} collective-permute-done((bf16[32,4096]{1,0:T(8,128)(2,1)S(1)}, bf16[32,4096]{1,0:T(8,128)(2,1)S(1)}, u32[]{:S(2)}, u32[]{:S(2)}) %collective-permute-start.2) | collective-permute-done | bytes 262176 | tf_op jit(solution)/shard_map/ppermute | solution.py:33
  51.2 3.4 %shard_map.118 = (bf16[512,512]{1,0:T(8,128)(2,1)S(1)}, bf16[512,128]{1,0:T(8,128)(2,1)S(1)}, f32[8,512]{1,0:T(8,128)S(1)}) custom-call(s32[16]{0:T(128)S(1)} %compare_select_fusion.9.i.idx, bf16[32,4096]{1,0:T(8,128)(2,1)S(1)} %constant_dynamic-update-slice_fusion.refs_0_, bf16[32,4096]{1,0:T(8,128)(2,1)S(1)} %constant_dynamic-update-slice_fusion.2.refs_1_, ...), custom_call_target="tpu_custom_call" | custom-call | flops 805306368 | bytes 6291456 | tf_op jit(solution)/shard_map/pallas_call | solution.py:245
  54.6 4.2 %shard_map.119 = (bf16[512,512]{1,0:T(8,128)(2,1)S(1)}, bf16[512,128]{1,0:T(8,128)(2,1)S(1)}, f32[8,512]{1,0:T(8,128)S(1)}) custom-call(s32[16]{0:T(128)S(1)} %compare_select_fusion.9.i.idx, bf16[32,4096]{1,0:T(8,128)(2,1)S(1)} %collective-permute-done.1.refs_0_.refs_4_, ...), custom_call_target="tpu_custom_call", output_to_operand_aliasing={{0}: (9, {}), {1}: (10, {}), {2}: (11, {})} | custom-call | flops 1610612736 | bytes 6291456 | tf_op jit(solution)/shard_map/pallas_call | solution.py:245
  58.9 2.9 %shard_map.120 = (bf16[512,512]{1,0:T(8,128)(2,1)S(1)}, bf16[512,128]{1,0:T(8,128)(2,1)S(1)}, f32[8,512]{1,0:T(8,128)S(1)}, bf16[16,640]{1,0:T(8,128)(2,1)S(1)}) custom-call(s32[16]{0:T(128)S(1)} %compare_select_fusion.9.i.idx, ...), custom_call_target="tpu_custom_call", output_to_operand_aliasing={{0}: (8, {}), {1}: (9, {}), {2}: (10, {})} | custom-call | flops 805306368 | bytes 6291456 | tf_op jit(solution)/shard_map/pallas_call | solution.py:245
  64.6 3.6 %collective-permute-start.22 = (bf16[256,128]{1,0:T(8,128)(2,1)S(1)}, bf16[256,128]{1,0:T(8,128)(2,1)S(1)}, u32[]{:S(2)}, u32[]{:S(2)}) collective-permute-start(bf16[256,128]{1,0:T(8,128)(2,1)S(1)} %conv_states.1), channel_id=1, source_target_pairs={{0,4},{1,5},{2,6},{3,7},{4,0},{5,1},{6,2},{7,3},{8,12},{9,13},{10,... | collective-permute-start | bytes 196616 | tf_op jit(solution)/shard_map/ppermute | solution.py:33
  68.8 4.3 %collective-permute-done.22 = bf16[256,128]{1,0:T(8,128)(2,1)S(1)} collective-permute-done((bf16[256,128]{1,0:T(8,128)(2,1)S(1)}, bf16[256,128]{1,0:T(8,128)(2,1)S(1)}, u32[]{:S(2)}, u32[]{:S(2)}) %collective-permute-start.22) | collective-permute-done | bytes 65568 | tf_op jit(solution)/shard_map/ppermute | solution.py:33
  73.4 3.4 %inputs_stage.1 = (bf16[512,512]{1,0:T(8,128)(2,1)S(1)}, bf16[512,512]{1,0:T(8,128)(2,1)S(1)}, bf16[512,512]{1,0:T(8,128)(2,1)S(1)}, f32[8,512]{1,0:T(8,128)S(1)}, f32[8,512]{1,0:T(8,128)S(1)}) custom-call(f32[24]{0:T(128)S(1)} %pad_maximum_fusion.5.par_ref, bf16[512,512]{1,0:T(8,128)(2,1)S(1)} %get-tuple-element.45.rows_ref, ...), custom_call_target="tpu_custom_call" | custom-call | flops 10000000 | bytes 2000000 | tf_op jit(solution)/shard_map/inputs_stage/pallas_call | solution.py:350
  76.8 5.1 %shard_map.121.gate_ref = bf16[512,512]{1,0:T(8,128)(2,1)S(1)} custom-call(s32[16]{0:T(128)S(1)} %compare_select_fusion.9.i.idx, bf16[32,4096]{1,0:T(8,128)(2,1)S(1)} %constant_dynamic-update-slice_fusion.refs_0_, bf16[32,4096]{1,0:T(8,128)(2,1)S(1)} %constant_dynamic-update-slice_fusion.2.refs_1_, bf16[32,4096]{1,0:T(8,128)(2,1)S(1)} %collective-permute-done.5.refs_2_, ...), custom_call_target="tpu_custom_call" | custom-call | flops 2147483648 | bytes 4194304 | tf_op jit(solution)/shard_map/pallas_call | solution.py:160
  83.3 4.6 %collective-permute-start.27 = (f16[272,128]{1,0:T(8,128)(2,1)S(1)}, f16[272,128]{1,0:T(8,128)(2,1)S(1)}, u32[]{:S(2)}, u32[]{:S(2)}) collective-permute-start(f16[272,128]{1,0:T(8,128)(2,1)S(1)} %get-tuple-element.82), channel_id=1, source_target_pairs={{0,96},{32,64},{64,32},{96,0},{128,224},{160,192},{192,160},{224,1... | collective-permute-start | bytes 208904 | tf_op jit(solution)/shard_map/ppermute | solution.py:33
  91.7 8.1 %collective-permute-start.28 = (f16[272,128]{1,0:T(8,128)(2,1)S(1)}, f16[272,128]{1,0:T(8,128)(2,1)S(1)}, u32[]{:S(2)}, u32[]{:S(2)}) collective-permute-start(f16[272,128]{1,0:T(8,128)(2,1)S(1)} %convert_element_type.201), channel_id=1, source_target_pairs={{0,128},{32,160},{64,192},{96,224},{128,0},{160,32},{192,64},{224,... | collective-permute-start | bytes 208904 | tf_op jit(solution)/shard_map/ppermute | solution.py:33
  99.7 4.2 %scan_stage.1 = (f32[512,512]{1,0:T(8,128)S(1)}, bf16[512,256]{1,0:T(8,128)(2,1)S(1)}) custom-call(s32[16]{0:T(128)S(1)} %compare_select_fusion.9.i.idx, f32[24]{0:T(128)S(1)} %pad_maximum_fusion.5.par_ref, bf16[4,256,128]{2,1,0:T(8,128)(2,1)S(1)} %pad_maximum_fusion.2.own_ref, bf16[4,256,128]{2,1,0:T(8,128)(2,1)S(1)} %collective-permute-done.24.oth_ref, ...), custom_call_target="tpu_custom_call" | custom-call | flops 6000000000 | bytes 3000000 | tf_op jit(solution)/shard_map/scan_stage/pallas_call | solution.py:535
  104.8 2.1 %collective-permute-start.30 = (f16[272,128]{1,0:T(8,128)(2,1)S(1)}, f16[272,128]{1,0:T(8,128)(2,1)S(1)}, u32[]{:S(2)}, u32[]{:S(2)}) collective-permute-start(f16[272,128]{1,0:T(8,128)(2,1)S(1)} %get-tuple-element.80), channel_id=1, source_target_pairs={{0,64},{32,96},{64,0},{96,32},{128,192},{160,224},{192,128},{224,1... | collective-permute-start | bytes 208904 | tf_op jit(solution)/shard_map/ppermute | solution.py:33
  106.9 2.6 %collective-permute-start.31 = (f16[272,128]{1,0:T(8,128)(2,1)S(1)}, f16[272,128]{1,0:T(8,128)(2,1)S(1)}, u32[]{:S(2)}, u32[]{:S(2)}) collective-permute-start(f16[272,128]{1,0:T(8,128)(2,1)S(1)} %get-tuple-element.79), channel_id=1, source_target_pairs={{0,96},{32,64},{64,32},{96,0},{128,224},{160,192},{192,160},{224,1... | collective-permute-start | bytes 208904 | tf_op jit(solution)/shard_map/ppermute | solution.py:33
  112.4 3.0 %gate_stage.1 = (f32[512,512]{1,0:T(8,128)S(1)}, f32[4,128]{1,0:T(4,128)S(1)}) custom-call(s32[16]{0:T(128)S(1)} %compare_select_fusion.9.i.idx, f32[512,512]{1,0:T(8,128)S(1)} %get-tuple-element.50.y_ref, bf16[512,256]{1,0:T(8,128)(2,1)S(1)} %get-tuple-element.51.read_ref, f32[272,128]{1,0:T(8,128)S(1)} %slice_bitcast_fusion.q0, ...), custom_call_target="tpu_custom_call" | custom-call | flops 200000000 | bytes 3000000 | tf_op jit(solution)/shard_map/gate_stage/pallas_call | solution.py:577
  117.2 3.3 %collective-permute-done.33 = f32[4,128]{1,0:T(4,128)S(1)} collective-permute-done((f32[4,128]{1,0:T(4,128)S(1)}, f32[4,128]{1,0:T(4,128)S(1)}, u32[]{:S(2)}, u32[]{:S(2)}) %collective-permute-start.33) | collective-permute-done | bytes 2080 | tf_op jit(solution)/shard_map/ppermute | solution.py:33
  121.6 3.4 %collective-permute-done.34 = f32[4,128]{1,0:T(4,128)S(1)} collective-permute-done((f32[4,128]{1,0:T(4,128)S(1)}, f32[4,128]{1,0:T(4,128)S(1)}, u32[]{:S(2)}, u32[]{:S(2)}) %collective-permute-start.34) | collective-permute-done | bytes 2080 | tf_op jit(solution)/shard_map/ppermute | solution.py:33
  127.1 3.7 %out_block.2 = (f32[192,4096]{1,0:T(8,128)S(1)}, bf16[192,4096]{1,0:T(8,128)(2,1)S(1)}) custom-call(s32[16]{0:T(128)S(1)} %compare_select_fusion.9.i.idx, f32[512,512]{1,0:T(8,128)S(1)} %get-tuple-element.57.u_ref, f32[4,128]{1,0:T(4,128)S(1)} %add.206.ss_ref, f32[1,512]{1,0:T(1,128)S(1)} %bitcast.27, bf16[512,4096]{1,0:T(8,128)(2,1)S(1)} %load.1.w_ref), custom_call_target="tpu_custom_call" | custom-call | flops 1610612736 | bytes 6000000 | tf_op jit(solution)/shard_map/out_block/pallas_call | solution.py:635
  131.8 3.2 %collective-permute-start.39 = (f16[32,4096]{1,0:T(8,128)(2,1)S(1)}, f16[32,4096]{1,0:T(8,128)(2,1)S(1)}, u32[]{:S(2)}, u32[]{:S(2)}) collective-permute-start(f16[32,4096]{1,0:T(8,128)(2,1)S(1)} %get-tuple-element.76), channel_id=1, source_target_pairs={{0,24},{1,25},{2,26},{3,27},{4,28},{5,29},{6,30},{7,31},{8,0},{9,1... | collective-permute-start | bytes 786440 | tf_op jit(solution)/shard_map/ppermute | solution.py:33
  135.0 6.2 %collective-permute-done.37 = f16[32,4096]{1,0:T(8,128)(2,1)S(1)} collective-permute-done((f16[32,4096]{1,0:T(8,128)(2,1)S(1)}, f16[32,4096]{1,0:T(8,128)(2,1)S(1)}, u32[]{:S(2)}, u32[]{:S(2)}) %collective-permute-start.37) | collective-permute-done | bytes 262176 | tf_op jit(solution)/shard_map/ppermute | solution.py:33
  142.0 3.0 %collective-permute-start.45 = (f16[64,2048]{1,0:T(8,128)(2,1)S(1)}, f16[64,2048]{1,0:T(8,128)(2,1)S(1)}, u32[]{:S(2)}, u32[]{:S(2)}) collective-permute-start(f16[64,2048]{1,0:T(8,128)(2,1)S(1)} %get-tuple-element.64), channel_id=1, source_target_pairs={{0,24},{1,25},{2,26},{3,27},{4,28},{5,29},{6,30},{7,31},{8,0},{9,1... | collective-permute-start | bytes 786440 | tf_op jit(solution)/shard_map/ppermute | solution.py:33
  145.0 3.2 %collective-permute-start.40 = (f16[64,2048]{1,0:T(8,128)(2,1)S(1)}, f16[64,2048]{1,0:T(8,128)(2,1)S(1)}, u32[]{:S(2)}, u32[]{:S(2)}) collective-permute-start(f16[64,2048]{1,0:T(8,128)(2,1)S(1)} %get-tuple-element.67), channel_id=1, source_target_pairs={{0,24},{1,25},{2,26},{3,27},{4,28},{5,29},{6,30},{7,31},{8,0},{9,1... | collective-permute-start | bytes 786440 | tf_op jit(solution)/shard_map/ppermute | solution.py:33
  148.2 3.5 %collective-permute-done.45 = f16[64,2048]{1,0:T(8,128)(2,1)S(1)} collective-permute-done((f16[64,2048]{1,0:T(8,128)(2,1)S(1)}, f16[64,2048]{1,0:T(8,128)(2,1)S(1)}, u32[]{:S(2)}, u32[]{:S(2)}) %collective-permute-start.45) | collective-permute-done | bytes 262176 | tf_op jit(solution)/shard_map/ppermute | solution.py:33
  151.7 3.7 %collective-permute-done.44 = f16[64,2048]{1,0:T(8,128)(2,1)S(1)} collective-permute-done((f16[64,2048]{1,0:T(8,128)(2,1)S(1)}, f16[64,2048]{1,0:T(8,128)(2,1)S(1)}, u32[]{:S(2)}, u32[]{:S(2)}) %collective-permute-start.44) | collective-permute-done | bytes 262176 | tf_op jit(solution)/shard_map/ppermute | solution.py:33
  157.5 2.5 %collective-permute-start.46 = (f16[16,2048]{1,0:T(8,128)(2,1)S(1)}, f16[16,2048]{1,0:T(8,128)(2,1)S(1)}, u32[]{:S(2)}, u32[]{:S(2)}) collective-permute-start(f16[16,2048]{1,0:T(8,128)(2,1)S(1)} %get-tuple-element.72), channel_id=1, source_target_pairs={{0,2},{1,3},{2,0},{3,1},{4,6},{5,7},{6,4},{7,5},{8,10},{9,11},{10,... | collective-permute-start | bytes 196616 | tf_op jit(solution)/shard_map/ppermute | solution.py:33
  162.4 2.1 %collective-permute-start.41 = (f16[16,2048]{1,0:T(8,128)(2,1)S(1)}, f16[16,2048]{1,0:T(8,128)(2,1)S(1)}, u32[]{:S(2)}, u32[]{:S(2)}) collective-permute-start(f16[16,2048]{1,0:T(8,128)(2,1)S(1)} %get-tuple-element.69), channel_id=1, source_target_pairs={{0,2},{1,3},{2,0},{3,1},{4,6},{5,7},{6,4},{7,5},{8,10},{9,11},{10,... | collective-permute-start | bytes 196616 | tf_op jit(solution)/shard_map/ppermute | solution.py:33
  (145 shorter events, 42.9 us)
Async XLA Ops:
  0.0 6.8 %collective-permute-start = (bf16[16,4096]{1,0:T(8,128)(2,1)}, bf16[16,4096]{1,0:T(8,128)(2,1)S(1)}, u32[]{:S(2)}, u32[]{:S(2)}) collective-permute-start(bf16[16,4096]{1,0:T(8,128)(2,1)} %param.12), channel_id=1, source_target_pairs={{0,2},{1,3},{2,0},{3,1},{4,6},{5,7},{6,4},{7,5},{8,10},{9,11},{10,... | collective-permute-start | bytes 393224 | tf_op jit(solution)/shard_map/ppermute | solution.py:33
  1.9 13.5 %collective-permute-start.3 = (bf16[16,4096]{1,0:T(8,128)(2,1)}, bf16[16,4096]{1,0:T(8,128)(2,1)S(1)}, u32[]{:S(2)}, u32[]{:S(2)}) collective-permute-start(bf16[16,4096]{1,0:T(8,128)(2,1)} %param.12), channel_id=1, source_target_pairs={{0,4},{1,5},{2,6},{3,7},{4,0},{5,1},{6,2},{7,3},{8,12},{9,13},{10,... | collective-permute-start | bytes 393224 | tf_op jit(solution)/shard_map/ppermute | solution.py:33
  5.2 10.2 %collective-permute-start.4 = (bf16[16,4096]{1,0:T(8,128)(2,1)}, bf16[16,4096]{1,0:T(8,128)(2,1)S(1)}, u32[]{:S(2)}, u32[]{:S(2)}) collective-permute-start(bf16[16,4096]{1,0:T(8,128)(2,1)} %param.12), channel_id=1, source_target_pairs={{0,6},{1,7},{2,4},{3,5},{4,2},{5,3},{6,0},{7,1},{8,14},{9,15},{10,... | collective-permute-start | bytes 393224 | tf_op jit(solution)/shard_map/ppermute | solution.py:33
  5.2 31.2 %collective-permute-start.14 = (bf16[64,4096]{1,0:T(8,128)(2,1)}, bf16[64,4096]{1,0:T(8,128)(2,1)S(1)}, u32[]{:S(2)}, u32[]{:S(2)}) collective-permute-start(bf16[64,4096]{1,0:T(8,128)(2,1)} %bitcast.28), channel_id=1, source_target_pairs={{0,1},{1,0},{2,3},{3,2},{4,5},{5,4},{6,7},{7,6},{8,9},{9,8},{10,11... | collective-permute-start | bytes 1572872 | tf_op jit(solution)/shard_map/ppermute | solution.py:33
  5.2 12.5 %collective-permute-start.20 = (f32[5,64]{1,0:T(8,128)}, f32[5,64]{1,0:T(8,128)S(1)}, u32[]{:S(2)}, u32[]{:S(2)}) collective-permute-start(f32[5,64]{1,0:T(8,128)} %param.18), channel_id=1, source_target_pairs={{0,1},{1,0},{2,3},{3,2},{4,5},{5,4},{6,7},{7,6},{8,9},{9,8},{10,11... | collective-permute-start | bytes 3848 | tf_op jit(solution)/shard_map/ppermute | solution.py:33
  17.0 15.3 %collective-permute-start.5 = (bf16[32,4096]{1,0:T(8,128)(2,1)S(1)}, bf16[32,4096]{1,0:T(8,128)(2,1)S(1)}, u32[]{:S(2)}, u32[]{:S(2)}) collective-permute-start(bf16[32,4096]{1,0:T(8,128)(2,1)S(1)} %constant_dynamic-update-slice_fusion.refs_0_), channel_id=1, source_target_pairs={{0,1},{1,0},{2,3},{3,2},{4,5},{5,4},{6,7},{7,6},{8,9},{9,8},{10,11... | collective-permute-start | bytes 786440 | tf_op jit(solution)/shard_map/ppermute | solution.py:33
  18.5 12.2 %collective-permute-start.12 = (bf16[8,4096]{1,0:T(8,128)(2,1)S(1)}, bf16[8,4096]{1,0:T(8,128)(2,1)S(1)}, u32[]{:S(2)}, u32[]{:S(2)}) collective-permute-start(bf16[8,4096]{1,0:T(8,128)(2,1)S(1)} %add.201), channel_id=1, source_target_pairs={{24,0},{25,1},{26,2},{27,3},{28,4},{29,5},{30,6},{31,7},{56,32},{5... | collective-permute-start | bytes 196616 | tf_op jit(solution)/shard_map/ppermute | solution.py:39
  19.8 15.9 %collective-permute-start.1 = (bf16[32,4096]{1,0:T(8,128)(2,1)S(1)}, bf16[32,4096]{1,0:T(8,128)(2,1)S(1)}, u32[]{:S(2)}, u32[]{:S(2)}) collective-permute-start(bf16[32,4096]{1,0:T(8,128)(2,1)S(1)} %constant_dynamic-update-slice_fusion.refs_0_), channel_id=1, source_target_pairs={{0,8},{1,9},{2,10},{3,11},{4,12},{5,13},{6,14},{7,15},{8,16},{9,17... | collective-permute-start | bytes 786440 | tf_op jit(solution)/shard_map/ppermute | solution.py:33
  20.7 15.0 %collective-permute-start.16 = (bf16[32,4096]{1,0:T(8,128)(2,1)S(1)}, bf16[32,4096]{1,0:T(8,128)(2,1)S(1)}, u32[]{:S(2)}, u32[]{:S(2)}) collective-permute-start(bf16[32,4096]{1,0:T(8,128)(2,1)S(1)} %constant_dynamic-update-slice_fusion.refs_0_), channel_id=1, source_target_pairs={{0,24},{1,25},{2,26},{3,27},{4,28},{5,29},{6,30},{7,31},{8,0},{9,1... | collective-permute-start | bytes 786440 | tf_op jit(solution)/shard_map/ppermute | solution.py:33
  32.3 7.3 %collective-permute-start.6 = (bf16[32,4096]{1,0:T(8,128)(2,1)S(1)}, bf16[32,4096]{1,0:T(8,128)(2,1)S(1)}, u32[]{:S(2)}, u32[]{:S(2)}) collective-permute-start(bf16[32,4096]{1,0:T(8,128)(2,1)S(1)} %constant_dynamic-update-slice_fusion.2.refs_1_), channel_id=1, source_target_pairs={{0,24},{1,25},{2,26},{3,27},{4,28},{5,29},{6,30},{7,31},{8,0},{9,1... | collective-permute-start | bytes 786440 | tf_op jit(solution)/shard_map/ppermute | solution.py:33
  35.7 10.4 %collective-permute-start.15 = (bf16[32,4096]{1,0:T(8,128)(2,1)S(1)}, bf16[32,4096]{1,0:T(8,128)(2,1)S(1)}, u32[]{:S(2)}, u32[]{:S(2)}) collective-permute-start(bf16[32,4096]{1,0:T(8,128)(2,1)S(1)} %constant_dynamic-update-slice_fusion.2.refs_1_), channel_id=1, source_target_pairs={{0,8},{1,9},{2,10},{3,11},{4,12},{5,13},{6,14},{7,15},{8,16},{9,17... | collective-permute-start | bytes 786440 | tf_op jit(solution)/shard_map/ppermute | solution.py:33
  35.7 15.5 %collective-permute-start.19 = (bf16[32,4096]{1,0:T(8,128)(2,1)S(1)}, bf16[32,4096]{1,0:T(8,128)(2,1)S(1)}, u32[]{:S(2)}, u32[]{:S(2)}) collective-permute-start(bf16[32,4096]{1,0:T(8,128)(2,1)S(1)} %constant_dynamic-update-slice_fusion.2.refs_1_), channel_id=1, source_target_pairs={{0,1},{1,0},{2,3},{3,2},{4,5},{5,4},{6,7},{7,6},{8,9},{9,8},{10,11... | collective-permute-start | bytes 786440 | tf_op jit(solution)/shard_map/ppermute | solution.py:33
  35.8 18.8 %collective-permute-start.17 = (bf16[64,4096]{1,0:T(8,128)(2,1)S(1)}, bf16[64,4096]{1,0:T(8,128)(2,1)S(1)}, u32[]{:S(2)}, u32[]{:S(2)}) collective-permute-start(bf16[64,4096]{1,0:T(8,128)(2,1)S(1)} %pad_maximum_fusion), channel_id=1, source_target_pairs={{0,1},{1,0},{2,3},{3,2},{4,5},{5,4},{6,7},{7,6},{8,9},{9,8},{10,11... | collective-permute-start | bytes 1572872 | tf_op jit(solution)/shard_map/ppermute | solution.py:33
  36.4 13.9 %collective-permute-start.2 = (bf16[32,4096]{1,0:T(8,128)(2,1)S(1)}, bf16[32,4096]{1,0:T(8,128)(2,1)S(1)}, u32[]{:S(2)}, u32[]{:S(2)}) collective-permute-start(bf16[32,4096]{1,0:T(8,128)(2,1)S(1)} %collective-permute-done.1.refs_0_.refs_4_), channel_id=1, source_target_pairs={{0,8},{1,9},{2,10},{3,11},{4,12},{5,13},{6,14},{7,15},{8,16},{9,17... | collective-permute-start | bytes 786440 | tf_op jit(solution)/shard_map/ppermute | solution.py:33
  39.6 10.7 %collective-permute-start.7 = (bf16[32,4096]{1,0:T(8,128)(2,1)S(1)}, bf16[32,4096]{1,0:T(8,128)(2,1)S(1)}, u32[]{:S(2)}, u32[]{:S(2)}) collective-permute-start(bf16[32,4096]{1,0:T(8,128)(2,1)S(1)} %collective-permute-done.6.refs_5_.refs_9_), channel_id=1, source_target_pairs={{0,24},{1,25},{2,26},{3,27},{4,28},{5,29},{6,30},{7,31},{8,0},{9,1... | collective-permute-start | bytes 786440 | tf_op jit(solution)/shard_map/ppermute | solution.py:33
  46.1 8.5 %collective-permute-start.18 = (bf16[64,4096]{1,0:T(8,128)(2,1)S(1)}, bf16[64,4096]{1,0:T(8,128)(2,1)S(1)}, u32[]{:S(2)}, u32[]{:S(2)}) collective-permute-start(bf16[64,4096]{1,0:T(8,128)(2,1)S(1)} %pad_maximum_fusion.1), channel_id=1, source_target_pairs={{0,1},{1,0},{2,3},{3,2},{4,5},{5,4},{6,7},{7,6},{8,9},{9,8},{10,11... | collective-permute-start | bytes 1572872 | tf_op jit(solution)/shard_map/ppermute | solution.py:33
  50.3 8.5 %collective-permute-start.8 = (bf16[32,4096]{1,0:T(8,128)(2,1)S(1)}, bf16[32,4096]{1,0:T(8,128)(2,1)S(1)}, u32[]{:S(2)}, u32[]{:S(2)}) collective-permute-start(bf16[32,4096]{1,0:T(8,128)(2,1)S(1)} %collective-permute-done.2.refs_0_.refs_12_), channel_id=1, source_target_pairs={{0,1},{1,0},{2,3},{3,2},{4,5},{5,4},{6,7},{7,6},{8,9},{9,8},{10,11... | collective-permute-start | bytes 786440 | tf_op jit(solution)/shard_map/ppermute | solution.py:33
  50.3 8.5 %collective-permute-start.9 = (bf16[32,4096]{1,0:T(8,128)(2,1)S(1)}, bf16[32,4096]{1,0:T(8,128)(2,1)S(1)}, u32[]{:S(2)}, u32[]{:S(2)}) collective-permute-start(bf16[32,4096]{1,0:T(8,128)(2,1)S(1)} %collective-permute-done.7.refs_1_.refs_13_), channel_id=1, source_target_pairs={{0,1},{1,0},{2,3},{3,2},{4,5},{5,4},{6,7},{7,6},{8,9},{9,8},{10,11... | collective-permute-start | bytes 786440 | tf_op jit(solution)/shard_map/ppermute | solution.py:33
  64.6 8.5 %collective-permute-start.22 = (bf16[256,128]{1,0:T(8,128)(2,1)S(1)}, bf16[256,128]{1,0:T(8,128)(2,1)S(1)}, u32[]{:S(2)}, u32[]{:S(2)}) collective-permute-start(bf16[256,128]{1,0:T(8,128)(2,1)S(1)} %conv_states.1), channel_id=1, source_target_pairs={{0,4},{1,5},{2,6},{3,7},{4,0},{5,1},{6,2},{7,3},{8,12},{9,13},{10,... | collective-permute-start | bytes 196616 | tf_op jit(solution)/shard_map/ppermute | solution.py:33
  73.1 8.8 %collective-permute-start.24 = (bf16[4,256,128]{2,1,0:T(8,128)(2,1)S(1)}, bf16[4,256,128]{2,1,0:T(8,128)(2,1)S(1)}, u32[]{:S(2)}, u32[]{:S(2)}) collective-permute-start(bf16[4,256,128]{2,1,0:T(8,128)(2,1)S(1)} %pad_maximum_fusion.2.own_ref), channel_id=1, source_target_pairs={{0,1},{1,0},{2,3},{3,2},{4,5},{5,4},{6,7},{7,6},{8,9},{9,8},{10,11... | collective-permute-start | bytes 786440 | tf_op jit(solution)/shard_map/ppermute | solution.py:33
  83.3 7.5 %collective-permute-start.27 = (f16[272,128]{1,0:T(8,128)(2,1)S(1)}, f16[272,128]{1,0:T(8,128)(2,1)S(1)}, u32[]{:S(2)}, u32[]{:S(2)}) collective-permute-start(f16[272,128]{1,0:T(8,128)(2,1)S(1)} %get-tuple-element.82), channel_id=1, source_target_pairs={{0,96},{32,64},{64,32},{96,0},{128,224},{160,192},{192,160},{224,1... | collective-permute-start | bytes 208904 | tf_op jit(solution)/shard_map/ppermute | solution.py:33
  91.7 12.2 %collective-permute-start.28 = (f16[272,128]{1,0:T(8,128)(2,1)S(1)}, f16[272,128]{1,0:T(8,128)(2,1)S(1)}, u32[]{:S(2)}, u32[]{:S(2)}) collective-permute-start(f16[272,128]{1,0:T(8,128)(2,1)S(1)} %convert_element_type.201), channel_id=1, source_target_pairs={{0,128},{32,160},{64,192},{96,224},{128,0},{160,32},{192,64},{224,... | collective-permute-start | bytes 208904 | tf_op jit(solution)/shard_map/ppermute | solution.py:33
  130.9 10.5 %collective-permute-start.35 = (bf16[192,4096]{1,0:T(8,128)(2,1)S(1)}, bf16[192,4096]{1,0:T(8,128)(2,1)S(1)}, u32[]{:S(2)}, u32[]{:S(2)}) collective-permute-start(bf16[192,4096]{1,0:T(8,128)(2,1)S(1)} %get-tuple-element.60), channel_id=1, source_target_pairs={{0,1},{1,0},{2,3},{3,2},{4,5},{5,4},{6,7},{7,6},{8,9},{9,8},{10,11... | collective-permute-start | bytes 4718600 | tf_op jit(solution)/shard_map/ppermute | solution.py:33
  131.7 9.5 %collective-permute-start.37 = (f16[32,4096]{1,0:T(8,128)(2,1)S(1)}, f16[32,4096]{1,0:T(8,128)(2,1)S(1)}, u32[]{:S(2)}, u32[]{:S(2)}) collective-permute-start(f16[32,4096]{1,0:T(8,128)(2,1)S(1)} %get-tuple-element.75), channel_id=1, source_target_pairs={{0,8},{1,9},{2,10},{3,11},{4,12},{5,13},{6,14},{7,15},{8,16},{9,17... | collective-permute-start | bytes 786440 | tf_op jit(solution)/shard_map/ppermute | solution.py:33
  131.8 9.5 %collective-permute-start.39 = (f16[32,4096]{1,0:T(8,128)(2,1)S(1)}, f16[32,4096]{1,0:T(8,128)(2,1)S(1)}, u32[]{:S(2)}, u32[]{:S(2)}) collective-permute-start(f16[32,4096]{1,0:T(8,128)(2,1)S(1)} %get-tuple-element.76), channel_id=1, source_target_pairs={{0,24},{1,25},{2,26},{3,27},{4,28},{5,29},{6,30},{7,31},{8,0},{9,1... | collective-permute-start | bytes 786440 | tf_op jit(solution)/shard_map/ppermute | solution.py:33
  142.0 9.7 %collective-permute-start.45 = (f16[64,2048]{1,0:T(8,128)(2,1)S(1)}, f16[64,2048]{1,0:T(8,128)(2,1)S(1)}, u32[]{:S(2)}, u32[]{:S(2)}) collective-permute-start(f16[64,2048]{1,0:T(8,128)(2,1)S(1)} %get-tuple-element.64), channel_id=1, source_target_pairs={{0,24},{1,25},{2,26},{3,27},{4,28},{5,29},{6,30},{7,31},{8,0},{9,1... | collective-permute-start | bytes 786440 | tf_op jit(solution)/shard_map/ppermute | solution.py:33
  145.0 10.4 %collective-permute-start.44 = (f16[64,2048]{1,0:T(8,128)(2,1)S(1)}, f16[64,2048]{1,0:T(8,128)(2,1)S(1)}, u32[]{:S(2)}, u32[]{:S(2)}) collective-permute-start(f16[64,2048]{1,0:T(8,128)(2,1)S(1)} %get-tuple-element.65), channel_id=1, source_target_pairs={{0,8},{1,9},{2,10},{3,11},{4,12},{5,13},{6,14},{7,15},{8,16},{9,17... | collective-permute-start | bytes 786440 | tf_op jit(solution)/shard_map/ppermute | solution.py:33
  145.0 15.0 %collective-permute-start.40 = (f16[64,2048]{1,0:T(8,128)(2,1)S(1)}, f16[64,2048]{1,0:T(8,128)(2,1)S(1)}, u32[]{:S(2)}, u32[]{:S(2)}) collective-permute-start(f16[64,2048]{1,0:T(8,128)(2,1)S(1)} %get-tuple-element.67), channel_id=1, source_target_pairs={{0,24},{1,25},{2,26},{3,27},{4,28},{5,29},{6,30},{7,31},{8,0},{9,1... | collective-permute-start | bytes 786440 | tf_op jit(solution)/shard_map/ppermute | solution.py:33
  148.2 11.8 %collective-permute-start.38 = (f16[64,2048]{1,0:T(8,128)(2,1)S(1)}, f16[64,2048]{1,0:T(8,128)(2,1)S(1)}, u32[]{:S(2)}, u32[]{:S(2)}) collective-permute-start(f16[64,2048]{1,0:T(8,128)(2,1)S(1)} %get-tuple-element.63), channel_id=1, source_target_pairs={{0,8},{1,9},{2,10},{3,11},{4,12},{5,13},{6,14},{7,15},{8,16},{9,17... | collective-permute-start | bytes 786440 | tf_op jit(solution)/shard_map/ppermute | solution.py:33
  155.5 7.0 %collective-permute-start.48 = (f16[16,2048]{1,0:T(8,128)(2,1)S(1)}, f16[16,2048]{1,0:T(8,128)(2,1)S(1)}, u32[]{:S(2)}, u32[]{:S(2)}) collective-permute-start(f16[16,2048]{1,0:T(8,128)(2,1)S(1)} %get-tuple-element.73), channel_id=1, source_target_pairs={{0,6},{1,7},{2,4},{3,5},{4,2},{5,3},{6,0},{7,1},{8,14},{9,15},{10,... | collective-permute-start | bytes 196616 | tf_op jit(solution)/shard_map/ppermute | solution.py:33
  157.5 7.6 %collective-permute-start.47 = (f16[16,2048]{1,0:T(8,128)(2,1)S(1)}, f16[16,2048]{1,0:T(8,128)(2,1)S(1)}, u32[]{:S(2)}, u32[]{:S(2)}) collective-permute-start(f16[16,2048]{1,0:T(8,128)(2,1)S(1)} %get-tuple-element.74), channel_id=1, source_target_pairs={{0,4},{1,5},{2,6},{3,7},{4,0},{5,1},{6,2},{7,3},{8,12},{9,13},{10,... | collective-permute-start | bytes 196616 | tf_op jit(solution)/shard_map/ppermute | solution.py:33
  157.5 7.6 %collective-permute-start.46 = (f16[16,2048]{1,0:T(8,128)(2,1)S(1)}, f16[16,2048]{1,0:T(8,128)(2,1)S(1)}, u32[]{:S(2)}, u32[]{:S(2)}) collective-permute-start(f16[16,2048]{1,0:T(8,128)(2,1)S(1)} %get-tuple-element.72), channel_id=1, source_target_pairs={{0,2},{1,3},{2,0},{3,1},{4,6},{5,7},{6,4},{7,5},{8,10},{9,11},{10,... | collective-permute-start | bytes 196616 | tf_op jit(solution)/shard_map/ppermute | solution.py:33
  (26 other events, 246.3 us)

commit v4 on v3

--- a/solution.py
+++ b/solution.py
@@ -675,7 +675,9 @@
     low = core == 0
     first = jnp.where(low, state_rows_w, state_pair)
     second = jnp.where(low, state_pair, state_rows_w)
-    small_w = jnp.concatenate([first, second, step_weight.T, jnp.zeros((120, tokens.shape[1]), BF16)], axis=0)
+    small_w = jnp.concatenate(
+        [first, second, step_weight.T, jnp.zeros((120, tokens.shape[1]), BF16)], axis=0
+    )
     state_taps = jnp.concatenate(
         [jnp.where(low, state_conv, taps_pair), jnp.where(low, taps_pair, state_conv)], axis=1
     )
@@ -704,7 +706,6 @@
         "h2": lambda c, t: (c, t - 8) if t >= 24 else ((c, t + 8) if t < 8 else None),
     }
     rim = hop(last, to["h0"])
-    bufs = project_resident(own_parts, None, [0], idx, input_weight, small_w, None)
     far_a = along_x(right1, 1)
     side1 = flip(jnp.concatenate([right1, left1], axis=0), "tp", 1)
     rim = rim + hop(rim, to["hc"])
@@ -714,7 +715,9 @@
     rim = rim + hop(rim, to["h2"])
     rights = [(right1, 0), (right2, 0), (side1, 0), (side2, 0)]
     lefts = [(left1, 0), (left2, 0), (side1, 1), (side2, 1)]
-    bufs = project_resident(rights + lefts, None, [1, 2], idx, input_weight, small_w, bufs)
+    bufs = project_resident(
+        own_parts + rights + lefts, None, [0, 1, 2], idx, input_weight, small_w, None
+    )
     rim = jnp.concatenate([jnp.zeros_like(rim), rim], axis=0)
     far_a_other = flip(far_a, "tp", 1)
     far_b_other = flip(far_b, "tp", 1)

time: 170 us -> 169 us (level)
  Pallas kernels: 35.5 us -> 33.2 us
    pallas_call x3 -> x2, Pallas kernels: 10.5 us -> 8.19 us  [project_resident(): pl.pallas_call(kernel, out_shape=outs, in_specs=[SM] + [VM] * (nl + 2) +...]
  transfers between devices with their start and end apart: 49 -> 49, of which waited for: 23 -> 22; matrix products, arithmetic and copies ran while one was open for 3% -> 3% of each run, Pallas kernels for 14% -> 13%
where the time goes in v4:
time: 169 us; the launch traced here: 167 us
  starting transfers between devices  68.2 us (40%)
  waiting for transfers between devices  58.4 us (35%)
  Pallas kernels  33.2 us (20%)
  other arithmetic  5.51 us (3%)
    ppermute x45, starting transfers between devices, send(): return lax.ppermute(array, axis, pairs)  64.1 us
    ppermute x45, waiting for transfers between devices, send(): return lax.ppermute(array, axis, pairs)  55.7 us
    pallas_call x2, Pallas kernels, project_resident(): pl.pallas_call(kernel, out_shape=outs, in_specs=[SM] + [VM] * (nl + 2) +...  8.19 us
    pallas_call x2, Pallas kernels, out_block(): pl.pallas_call(kernel, out_shape=[sds((rows, 4096), F32), sds((rows, 4096...  5.7 us
    pallas_call x1, Pallas kernels, project(): pl.pallas_call(kernel, out_shape=outs, grid_spec=pltpu.PrefetchScalarGrid...  5.1 us
    ppermute x4, starting transfers between devices, hop(): return lax.ppermute(array, ('ctx', 'tp'), pairs)  4.18 us
    pallas_call x1, Pallas kernels, scan_stage(): pl.pallas_call(scan_kernel, out_shape=[sds((512, 512), F32), sds((512, 25...  4.13 us
    pallas_call x1, Pallas kernels, inputs_stage(): pl.pallas_call(inputs_kernel, out_shape=[sds((512, 512), BF16)] * 3 + [sd...  3.45 us
  transfers between devices with their start and end apart: 49, of which 22 were waited for; matrix products, arithmetic and copies ran while one was open for 3% of the time, Pallas kernels for 13%

profile of v4, /device:TPU:24, one launch (start us, length us, event | category | flops | bytes accessed | tf_op | source)
XLA Modules:
  0.0 167.3 jit_solution(4121386306357817420)
XLA Ops:
  1.9 3.3 %collective-permute-start.3 = (bf16[16,4096]{1,0:T(8,128)(2,1)}, bf16[16,4096]{1,0:T(8,128)(2,1)S(1)}, u32[]{:S(2)}, u32[]{:S(2)}) collective-permute-start(bf16[16,4096]{1,0:T(8,128)(2,1)} %param.12), channel_id=1, source_target_pairs={{0,4},{1,5},{2,6},{3,7},{4,0},{5,1},{6,2},{7,3},{8,12},{9,13},{10,... | collective-permute-start | bytes 393224 | tf_op jit(solution)/shard_map/ppermute | solution.py:33
  6.8 8.6 %collective-permute-done.3 = bf16[16,4096]{1,0:T(8,128)(2,1)S(1)} collective-permute-done((bf16[16,4096]{1,0:T(8,128)(2,1)}, bf16[16,4096]{1,0:T(8,128)(2,1)S(1)}, u32[]{:S(2)}, u32[]{:S(2)}) %collective-permute-start.3) | collective-permute-done | bytes 131104 | tf_op jit(solution)/shard_map/ppermute | solution.py:33
  20.7 7.2 %collective-permute-start.17 = (bf16[32,4096]{1,0:T(8,128)(2,1)S(1)}, bf16[32,4096]{1,0:T(8,128)(2,1)S(1)}, u32[]{:S(2)}, u32[]{:S(2)}) collective-permute-start(bf16[32,4096]{1,0:T(8,128)(2,1)S(1)} %constant_dynamic-update-slice_fusion.refs_0_), channel_id=1, source_target_pairs={{0,24},{1,25},{2,26},{3,27},{4,28},{5,29},{6,30},{7,31},{8,0},{9,1... | collective-permute-start | bytes 786440 | tf_op jit(solution)/shard_map/ppermute | solution.py:33
  27.9 2.7 %collective-permute-done.12 = bf16[8,4096]{1,0:T(8,128)(2,1)S(1)} collective-permute-done((bf16[8,4096]{1,0:T(8,128)(2,1)S(1)}, bf16[8,4096]{1,0:T(8,128)(2,1)S(1)}, u32[]{:S(2)}, u32[]{:S(2)}) %collective-permute-start.12) | collective-permute-done | bytes 65568 | tf_op jit(solution)/shard_map/ppermute | solution.py:39
  32.4 3.3 %collective-permute-done.1.refs_4_ = bf16[32,4096]{1,0:T(8,128)(2,1)S(1)} collective-permute-done((bf16[32,4096]{1,0:T(8,128)(2,1)S(1)}, bf16[32,4096]{1,0:T(8,128)(2,1)S(1)}, u32[]{:S(2)}, u32[]{:S(2)}) %collective-permute-start.1) | collective-permute-done | bytes 262176 | tf_op jit(solution)/shard_map/ppermute | solution.py:33
  36.6 2.1 %collective-permute-start.2 = (bf16[32,4096]{1,0:T(8,128)(2,1)S(1)}, bf16[32,4096]{1,0:T(8,128)(2,1)S(1)}, u32[]{:S(2)}, u32[]{:S(2)}) collective-permute-start(bf16[32,4096]{1,0:T(8,128)(2,1)S(1)} %collective-permute-done.1.refs_4_), channel_id=1, source_target_pairs={{0,8},{1,9},{2,10},{3,11},{4,12},{5,13},{6,14},{7,15},{8,16},{9,17... | collective-permute-start | bytes 786440 | tf_op jit(solution)/shard_map/ppermute | solution.py:33
  39.8 3.3 %collective-permute-start.7 = (bf16[32,4096]{1,0:T(8,128)(2,1)S(1)}, bf16[32,4096]{1,0:T(8,128)(2,1)S(1)}, u32[]{:S(2)}, u32[]{:S(2)}) collective-permute-start(bf16[32,4096]{1,0:T(8,128)(2,1)S(1)} %collective-permute-done.6.refs_9_), channel_id=1, source_target_pairs={{0,24},{1,25},{2,26},{3,27},{4,28},{5,29},{6,30},{7,31},{8,0},{9,1... | collective-permute-start | bytes 786440 | tf_op jit(solution)/shard_map/ppermute | solution.py:33
  43.1 3.0 %collective-permute-done.16.refs_5_ = bf16[32,4096]{1,0:T(8,128)(2,1)S(1)} collective-permute-done((bf16[32,4096]{1,0:T(8,128)(2,1)S(1)}, bf16[32,4096]{1,0:T(8,128)(2,1)S(1)}, u32[]{:S(2)}, u32[]{:S(2)}) %collective-permute-start.16) | collective-permute-done | bytes 262176 | tf_op jit(solution)/shard_map/ppermute | solution.py:33
  46.2 5.0 %collective-permute-done.2.refs_0_.refs_12_ = bf16[32,4096]{1,0:T(8,128)(2,1)S(1)} collective-permute-done((bf16[32,4096]{1,0:T(8,128)(2,1)S(1)}, bf16[32,4096]{1,0:T(8,128)(2,1)S(1)}, u32[]{:S(2)}, u32[]{:S(2)}) %collective-permute-start.2) | collective-permute-done | bytes 262176 | tf_op jit(solution)/shard_map/ppermute | solution.py:33
  52.1 5.3 %shard_map.118 = (bf16[512,512]{1,0:T(8,128)(2,1)S(1)}, bf16[512,128]{1,0:T(8,128)(2,1)S(1)}, f32[8,512]{1,0:T(8,128)S(1)}) custom-call(s32[16]{0:T(128)S(1)} %compare_select_fusion.9.i.idx, bf16[32,4096]{1,0:T(8,128)(2,1)S(1)} %constant_dynamic-update-slice_fusion.refs_0_, bf16[32,4096]{1,0:T(8,128)(2,1)S(1)} %constant_dynamic-update-slice_fusion.2.refs_1_, ...), custom_call_target="tpu_custom_call" | custom-call | flops 2415919104 | bytes 6291456 | tf_op jit(solution)/shard_map/pallas_call | solution.py:245
  57.6 2.9 %shard_map.119 = (bf16[512,512]{1,0:T(8,128)(2,1)S(1)}, bf16[512,128]{1,0:T(8,128)(2,1)S(1)}, f32[8,512]{1,0:T(8,128)S(1)}, bf16[16,640]{1,0:T(8,128)(2,1)S(1)}) custom-call(s32[16]{0:T(128)S(1)} %compare_select_fusion.9.i.idx, ...), custom_call_target="tpu_custom_call", output_to_operand_aliasing={{0}: (8, {}), {1}: (9, {}), {2}: (10, {})} | custom-call | flops 805306368 | bytes 6291456 | tf_op jit(solution)/shard_map/pallas_call | solution.py:245
  63.2 3.6 %collective-permute-start.22 = (bf16[256,128]{1,0:T(8,128)(2,1)S(1)}, bf16[256,128]{1,0:T(8,128)(2,1)S(1)}, u32[]{:S(2)}, u32[]{:S(2)}) collective-permute-start(bf16[256,128]{1,0:T(8,128)(2,1)S(1)} %conv_states.1), channel_id=1, source_target_pairs={{0,4},{1,5},{2,6},{3,7},{4,0},{5,1},{6,2},{7,3},{8,12},{9,13},{10,... | collective-permute-start | bytes 196616 | tf_op jit(solution)/shard_map/ppermute | solution.py:33
  67.4 4.3 %collective-permute-done.22 = bf16[256,128]{1,0:T(8,128)(2,1)S(1)} collective-permute-done((bf16[256,128]{1,0:T(8,128)(2,1)S(1)}, bf16[256,128]{1,0:T(8,128)(2,1)S(1)}, u32[]{:S(2)}, u32[]{:S(2)}) %collective-permute-start.22) | collective-permute-done | bytes 65568 | tf_op jit(solution)/shard_map/ppermute | solution.py:33
  72.0 3.4 %inputs_stage.1 = (bf16[512,512]{1,0:T(8,128)(2,1)S(1)}, bf16[512,512]{1,0:T(8,128)(2,1)S(1)}, bf16[512,512]{1,0:T(8,128)(2,1)S(1)}, f32[8,512]{1,0:T(8,128)S(1)}, f32[8,512]{1,0:T(8,128)S(1)}) custom-call(f32[24]{0:T(128)S(1)} %pad_maximum_fusion.5.par_ref, bf16[512,512]{1,0:T(8,128)(2,1)S(1)} %get-tuple-element.39.rows_ref, ...), custom_call_target="tpu_custom_call" | custom-call | flops 10000000 | bytes 2000000 | tf_op jit(solution)/shard_map/inputs_stage/pallas_call | solution.py:350
  75.4 5.1 %shard_map.120.gate_ref = bf16[512,512]{1,0:T(8,128)(2,1)S(1)} custom-call(s32[16]{0:T(128)S(1)} %compare_select_fusion.9.i.idx, bf16[32,4096]{1,0:T(8,128)(2,1)S(1)} %constant_dynamic-update-slice_fusion.refs_0_, bf16[32,4096]{1,0:T(8,128)(2,1)S(1)} %constant_dynamic-update-slice_fusion.2.refs_1_, bf16[32,4096]{1,0:T(8,128)(2,1)S(1)} %collective-permute-done.5.refs_2_, ...), custom_call_target="tpu_custom_call" | custom-call | flops 2147483648 | bytes 4194304 | tf_op jit(solution)/shard_map/pallas_call | solution.py:160
  81.9 4.6 %collective-permute-start.27 = (f16[272,128]{1,0:T(8,128)(2,1)S(1)}, f16[272,128]{1,0:T(8,128)(2,1)S(1)}, u32[]{:S(2)}, u32[]{:S(2)}) collective-permute-start(f16[272,128]{1,0:T(8,128)(2,1)S(1)} %get-tuple-element.76), channel_id=1, source_target_pairs={{0,96},{32,64},{64,32},{96,0},{128,224},{160,192},{192,160},{224,1... | collective-permute-start | bytes 208904 | tf_op jit(solution)/shard_map/ppermute | solution.py:33
  90.3 8.1 %collective-permute-start.28 = (f16[272,128]{1,0:T(8,128)(2,1)S(1)}, f16[272,128]{1,0:T(8,128)(2,1)S(1)}, u32[]{:S(2)}, u32[]{:S(2)}) collective-permute-start(f16[272,128]{1,0:T(8,128)(2,1)S(1)} %convert_element_type.201), channel_id=1, source_target_pairs={{0,128},{32,160},{64,192},{96,224},{128,0},{160,32},{192,64},{224,... | collective-permute-start | bytes 208904 | tf_op jit(solution)/shard_map/ppermute | solution.py:33
  98.3 4.1 %scan_stage.1 = (f32[512,512]{1,0:T(8,128)S(1)}, bf16[512,256]{1,0:T(8,128)(2,1)S(1)}) custom-call(s32[16]{0:T(128)S(1)} %compare_select_fusion.9.i.idx, f32[24]{0:T(128)S(1)} %pad_maximum_fusion.5.par_ref, bf16[4,256,128]{2,1,0:T(8,128)(2,1)S(1)} %pad_maximum_fusion.2.own_ref, bf16[4,256,128]{2,1,0:T(8,128)(2,1)S(1)} %collective-permute-done.24.oth_ref, ...), custom_call_target="tpu_custom_call" | custom-call | flops 6000000000 | bytes 3000000 | tf_op jit(solution)/shard_map/scan_stage/pallas_call | solution.py:535
  103.4 2.1 %collective-permute-start.30 = (f16[272,128]{1,0:T(8,128)(2,1)S(1)}, f16[272,128]{1,0:T(8,128)(2,1)S(1)}, u32[]{:S(2)}, u32[]{:S(2)}) collective-permute-start(f16[272,128]{1,0:T(8,128)(2,1)S(1)} %get-tuple-element.74), channel_id=1, source_target_pairs={{0,64},{32,96},{64,0},{96,32},{128,192},{160,224},{192,128},{224,1... | collective-permute-start | bytes 208904 | tf_op jit(solution)/shard_map/ppermute | solution.py:33
  105.5 2.6 %collective-permute-start.31 = (f16[272,128]{1,0:T(8,128)(2,1)S(1)}, f16[272,128]{1,0:T(8,128)(2,1)S(1)}, u32[]{:S(2)}, u32[]{:S(2)}) collective-permute-start(f16[272,128]{1,0:T(8,128)(2,1)S(1)} %get-tuple-element.73), channel_id=1, source_target_pairs={{0,96},{32,64},{64,32},{96,0},{128,224},{160,192},{192,160},{224,1... | collective-permute-start | bytes 208904 | tf_op jit(solution)/shard_map/ppermute | solution.py:33
  111.0 3.0 %gate_stage.1 = (f32[512,512]{1,0:T(8,128)S(1)}, f32[4,128]{1,0:T(4,128)S(1)}) custom-call(s32[16]{0:T(128)S(1)} %compare_select_fusion.9.i.idx, f32[512,512]{1,0:T(8,128)S(1)} %get-tuple-element.44.y_ref, bf16[512,256]{1,0:T(8,128)(2,1)S(1)} %get-tuple-element.45.read_ref, f32[272,128]{1,0:T(8,128)S(1)} %slice_bitcast_fusion.q0, ...), custom_call_target="tpu_custom_call" | custom-call | flops 200000000 | bytes 3000000 | tf_op jit(solution)/shard_map/gate_stage/pallas_call | solution.py:577
  115.8 3.3 %collective-permute-done.33 = f32[4,128]{1,0:T(4,128)S(1)} collective-permute-done((f32[4,128]{1,0:T(4,128)S(1)}, f32[4,128]{1,0:T(4,128)S(1)}, u32[]{:S(2)}, u32[]{:S(2)}) %collective-permute-start.33) | collective-permute-done | bytes 2080 | tf_op jit(solution)/shard_map/ppermute | solution.py:33
  120.2 3.5 %collective-permute-done.34 = f32[4,128]{1,0:T(4,128)S(1)} collective-permute-done((f32[4,128]{1,0:T(4,128)S(1)}, f32[4,128]{1,0:T(4,128)S(1)}, u32[]{:S(2)}, u32[]{:S(2)}) %collective-permute-start.34) | collective-permute-done | bytes 2080 | tf_op jit(solution)/shard_map/ppermute | solution.py:33
  125.7 3.7 %out_block.2 = (f32[192,4096]{1,0:T(8,128)S(1)}, bf16[192,4096]{1,0:T(8,128)(2,1)S(1)}) custom-call(s32[16]{0:T(128)S(1)} %compare_select_fusion.9.i.idx, f32[512,512]{1,0:T(8,128)S(1)} %get-tuple-element.51.u_ref, f32[4,128]{1,0:T(4,128)S(1)} %add.206.ss_ref, f32[1,512]{1,0:T(1,128)S(1)} %bitcast.27, bf16[512,4096]{1,0:T(8,128)(2,1)S(1)} %load.1.w_ref), custom_call_target="tpu_custom_call" | custom-call | flops 1610612736 | bytes 6000000 | tf_op jit(solution)/shard_map/out_block/pallas_call | solution.py:635
  130.3 3.2 %collective-permute-start.39 = (f16[32,4096]{1,0:T(8,128)(2,1)S(1)}, f16[32,4096]{1,0:T(8,128)(2,1)S(1)}, u32[]{:S(2)}, u32[]{:S(2)}) collective-permute-start(f16[32,4096]{1,0:T(8,128)(2,1)S(1)} %get-tuple-element.70), channel_id=1, source_target_pairs={{0,24},{1,25},{2,26},{3,27},{4,28},{5,29},{6,30},{7,31},{8,0},{9,1... | collective-permute-start | bytes 786440 | tf_op jit(solution)/shard_map/ppermute | solution.py:33
  133.6 6.2 %collective-permute-done.37 = f16[32,4096]{1,0:T(8,128)(2,1)S(1)} collective-permute-done((f16[32,4096]{1,0:T(8,128)(2,1)S(1)}, f16[32,4096]{1,0:T(8,128)(2,1)S(1)}, u32[]{:S(2)}, u32[]{:S(2)}) %collective-permute-start.37) | collective-permute-done | bytes 262176 | tf_op jit(solution)/shard_map/ppermute | solution.py:33
  140.6 3.0 %collective-permute-start.45 = (f16[64,2048]{1,0:T(8,128)(2,1)S(1)}, f16[64,2048]{1,0:T(8,128)(2,1)S(1)}, u32[]{:S(2)}, u32[]{:S(2)}) collective-permute-start(f16[64,2048]{1,0:T(8,128)(2,1)S(1)} %get-tuple-element.58), channel_id=1, source_target_pairs={{0,24},{1,25},{2,26},{3,27},{4,28},{5,29},{6,30},{7,31},{8,0},{9,1... | collective-permute-start | bytes 786440 | tf_op jit(solution)/shard_map/ppermute | solution.py:33
  143.6 3.2 %collective-permute-start.40 = (f16[64,2048]{1,0:T(8,128)(2,1)S(1)}, f16[64,2048]{1,0:T(8,128)(2,1)S(1)}, u32[]{:S(2)}, u32[]{:S(2)}) collective-permute-start(f16[64,2048]{1,0:T(8,128)(2,1)S(1)} %get-tuple-element.61), channel_id=1, source_target_pairs={{0,24},{1,25},{2,26},{3,27},{4,28},{5,29},{6,30},{7,31},{8,0},{9,1... | collective-permute-start | bytes 786440 | tf_op jit(solution)/shard_map/ppermute | solution.py:33
  146.8 3.5 %collective-permute-done.45 = f16[64,2048]{1,0:T(8,128)(2,1)S(1)} collective-permute-done((f16[64,2048]{1,0:T(8,128)(2,1)S(1)}, f16[64,2048]{1,0:T(8,128)(2,1)S(1)}, u32[]{:S(2)}, u32[]{:S(2)}) %collective-permute-start.45) | collective-permute-done | bytes 262176 | tf_op jit(solution)/shard_map/ppermute | solution.py:33
  150.2 3.7 %collective-permute-done.44 = f16[64,2048]{1,0:T(8,128)(2,1)S(1)} collective-permute-done((f16[64,2048]{1,0:T(8,128)(2,1)S(1)}, f16[64,2048]{1,0:T(8,128)(2,1)S(1)}, u32[]{:S(2)}, u32[]{:S(2)}) %collective-permute-start.44) | collective-permute-done | bytes 262176 | tf_op jit(solution)/shard_map/ppermute | solution.py:33
  156.0 2.5 %collective-permute-start.46 = (f16[16,2048]{1,0:T(8,128)(2,1)S(1)}, f16[16,2048]{1,0:T(8,128)(2,1)S(1)}, u32[]{:S(2)}, u32[]{:S(2)}) collective-permute-start(f16[16,2048]{1,0:T(8,128)(2,1)S(1)} %get-tuple-element.66), channel_id=1, source_target_pairs={{0,2},{1,3},{2,0},{3,1},{4,6},{5,7},{6,4},{7,5},{8,10},{9,11},{10,... | collective-permute-start | bytes 196616 | tf_op jit(solution)/shard_map/ppermute | solution.py:33
  161.0 2.1 %collective-permute-start.41 = (f16[16,2048]{1,0:T(8,128)(2,1)S(1)}, f16[16,2048]{1,0:T(8,128)(2,1)S(1)}, u32[]{:S(2)}, u32[]{:S(2)}) collective-permute-start(f16[16,2048]{1,0:T(8,128)(2,1)S(1)} %get-tuple-element.63), channel_id=1, source_target_pairs={{0,2},{1,3},{2,0},{3,1},{4,6},{5,7},{6,4},{7,5},{8,10},{9,11},{10,... | collective-permute-start | bytes 196616 | tf_op jit(solution)/shard_map/ppermute | solution.py:33
  (144 shorter events, 40.9 us)
Async XLA Ops:
  0.0 6.8 %collective-permute-start = (bf16[16,4096]{1,0:T(8,128)(2,1)}, bf16[16,4096]{1,0:T(8,128)(2,1)S(1)}, u32[]{:S(2)}, u32[]{:S(2)}) collective-permute-start(bf16[16,4096]{1,0:T(8,128)(2,1)} %param.12), channel_id=1, source_target_pairs={{0,2},{1,3},{2,0},{3,1},{4,6},{5,7},{6,4},{7,5},{8,10},{9,11},{10,... | collective-permute-start | bytes 393224 | tf_op jit(solution)/shard_map/ppermute | solution.py:33
  1.9 13.5 %collective-permute-start.3 = (bf16[16,4096]{1,0:T(8,128)(2,1)}, bf16[16,4096]{1,0:T(8,128)(2,1)S(1)}, u32[]{:S(2)}, u32[]{:S(2)}) collective-permute-start(bf16[16,4096]{1,0:T(8,128)(2,1)} %param.12), channel_id=1, source_target_pairs={{0,4},{1,5},{2,6},{3,7},{4,0},{5,1},{6,2},{7,3},{8,12},{9,13},{10,... | collective-permute-start | bytes 393224 | tf_op jit(solution)/shard_map/ppermute | solution.py:33
  5.2 10.2 %collective-permute-start.4 = (bf16[16,4096]{1,0:T(8,128)(2,1)}, bf16[16,4096]{1,0:T(8,128)(2,1)S(1)}, u32[]{:S(2)}, u32[]{:S(2)}) collective-permute-start(bf16[16,4096]{1,0:T(8,128)(2,1)} %param.12), channel_id=1, source_target_pairs={{0,6},{1,7},{2,4},{3,5},{4,2},{5,3},{6,0},{7,1},{8,14},{9,15},{10,... | collective-permute-start | bytes 393224 | tf_op jit(solution)/shard_map/ppermute | solution.py:33
  5.2 31.4 %collective-permute-start.14 = (bf16[64,4096]{1,0:T(8,128)(2,1)}, bf16[64,4096]{1,0:T(8,128)(2,1)S(1)}, u32[]{:S(2)}, u32[]{:S(2)}) collective-permute-start(bf16[64,4096]{1,0:T(8,128)(2,1)} %bitcast.28), channel_id=1, source_target_pairs={{0,1},{1,0},{2,3},{3,2},{4,5},{5,4},{6,7},{7,6},{8,9},{9,8},{10,11... | collective-permute-start | bytes 1572872 | tf_op jit(solution)/shard_map/ppermute | solution.py:33
  5.2 12.5 %collective-permute-start.20 = (f32[5,64]{1,0:T(8,128)}, f32[5,64]{1,0:T(8,128)S(1)}, u32[]{:S(2)}, u32[]{:S(2)}) collective-permute-start(f32[5,64]{1,0:T(8,128)} %param.18), channel_id=1, source_target_pairs={{0,1},{1,0},{2,3},{3,2},{4,5},{5,4},{6,7},{7,6},{8,9},{9,8},{10,11... | collective-permute-start | bytes 3848 | tf_op jit(solution)/shard_map/ppermute | solution.py:33
  17.0 15.3 %collective-permute-start.5 = (bf16[32,4096]{1,0:T(8,128)(2,1)S(1)}, bf16[32,4096]{1,0:T(8,128)(2,1)S(1)}, u32[]{:S(2)}, u32[]{:S(2)}) collective-permute-start(bf16[32,4096]{1,0:T(8,128)(2,1)S(1)} %constant_dynamic-update-slice_fusion.refs_0_), channel_id=1, source_target_pairs={{0,1},{1,0},{2,3},{3,2},{4,5},{5,4},{6,7},{7,6},{8,9},{9,8},{10,11... | collective-permute-start | bytes 786440 | tf_op jit(solution)/shard_map/ppermute | solution.py:33
  18.5 12.2 %collective-permute-start.12 = (bf16[8,4096]{1,0:T(8,128)(2,1)S(1)}, bf16[8,4096]{1,0:T(8,128)(2,1)S(1)}, u32[]{:S(2)}, u32[]{:S(2)}) collective-permute-start(bf16[8,4096]{1,0:T(8,128)(2,1)S(1)} %add.201), channel_id=1, source_target_pairs={{24,0},{25,1},{26,2},{27,3},{28,4},{29,5},{30,6},{31,7},{56,32},{5... | collective-permute-start | bytes 196616 | tf_op jit(solution)/shard_map/ppermute | solution.py:39
  19.8 15.9 %collective-permute-start.1 = (bf16[32,4096]{1,0:T(8,128)(2,1)S(1)}, bf16[32,4096]{1,0:T(8,128)(2,1)S(1)}, u32[]{:S(2)}, u32[]{:S(2)}) collective-permute-start(bf16[32,4096]{1,0:T(8,128)(2,1)S(1)} %constant_dynamic-update-slice_fusion.refs_0_), channel_id=1, source_target_pairs={{0,8},{1,9},{2,10},{3,11},{4,12},{5,13},{6,14},{7,15},{8,16},{9,17... | collective-permute-start | bytes 786440 | tf_op jit(solution)/shard_map/ppermute | solution.py:33
  20.7 15.0 %collective-permute-start.17 = (bf16[32,4096]{1,0:T(8,128)(2,1)S(1)}, bf16[32,4096]{1,0:T(8,128)(2,1)S(1)}, u32[]{:S(2)}, u32[]{:S(2)}) collective-permute-start(bf16[32,4096]{1,0:T(8,128)(2,1)S(1)} %constant_dynamic-update-slice_fusion.refs_0_), channel_id=1, source_target_pairs={{0,24},{1,25},{2,26},{3,27},{4,28},{5,29},{6,30},{7,31},{8,0},{9,1... | collective-permute-start | bytes 786440 | tf_op jit(solution)/shard_map/ppermute | solution.py:33
  32.3 7.5 %collective-permute-start.6 = (bf16[32,4096]{1,0:T(8,128)(2,1)S(1)}, bf16[32,4096]{1,0:T(8,128)(2,1)S(1)}, u32[]{:S(2)}, u32[]{:S(2)}) collective-permute-start(bf16[32,4096]{1,0:T(8,128)(2,1)S(1)} %constant_dynamic-update-slice_fusion.2.refs_1_), channel_id=1, source_target_pairs={{0,24},{1,25},{2,26},{3,27},{4,28},{5,29},{6,30},{7,31},{8,0},{9,1... | collective-permute-start | bytes 786440 | tf_op jit(solution)/shard_map/ppermute | solution.py:33
  35.7 16.4 %collective-permute-start.15 = (bf16[32,4096]{1,0:T(8,128)(2,1)S(1)}, bf16[32,4096]{1,0:T(8,128)(2,1)S(1)}, u32[]{:S(2)}, u32[]{:S(2)}) collective-permute-start(bf16[32,4096]{1,0:T(8,128)(2,1)S(1)} %constant_dynamic-update-slice_fusion.2.refs_1_), channel_id=1, source_target_pairs={{0,1},{1,0},{2,3},{3,2},{4,5},{5,4},{6,7},{7,6},{8,9},{9,8},{10,11... | collective-permute-start | bytes 786440 | tf_op jit(solution)/shard_map/ppermute | solution.py:33
  35.7 10.4 %collective-permute-start.16 = (bf16[32,4096]{1,0:T(8,128)(2,1)S(1)}, bf16[32,4096]{1,0:T(8,128)(2,1)S(1)}, u32[]{:S(2)}, u32[]{:S(2)}) collective-permute-start(bf16[32,4096]{1,0:T(8,128)(2,1)S(1)} %constant_dynamic-update-slice_fusion.2.refs_1_), channel_id=1, source_target_pairs={{0,8},{1,9},{2,10},{3,11},{4,12},{5,13},{6,14},{7,15},{8,16},{9,17... | collective-permute-start | bytes 786440 | tf_op jit(solution)/shard_map/ppermute | solution.py:33
  36.4 15.7 %collective-permute-start.18 = (bf16[64,4096]{1,0:T(8,128)(2,1)S(1)}, bf16[64,4096]{1,0:T(8,128)(2,1)S(1)}, u32[]{:S(2)}, u32[]{:S(2)}) collective-permute-start(bf16[64,4096]{1,0:T(8,128)(2,1)S(1)} %pad_maximum_fusion), channel_id=1, source_target_pairs={{0,1},{1,0},{2,3},{3,2},{4,5},{5,4},{6,7},{7,6},{8,9},{9,8},{10,11... | collective-permute-start | bytes 1572872 | tf_op jit(solution)/shard_map/ppermute | solution.py:33
  36.6 14.7 %collective-permute-start.2 = (bf16[32,4096]{1,0:T(8,128)(2,1)S(1)}, bf16[32,4096]{1,0:T(8,128)(2,1)S(1)}, u32[]{:S(2)}, u32[]{:S(2)}) collective-permute-start(bf16[32,4096]{1,0:T(8,128)(2,1)S(1)} %collective-permute-done.1.refs_4_), channel_id=1, source_target_pairs={{0,8},{1,9},{2,10},{3,11},{4,12},{5,13},{6,14},{7,15},{8,16},{9,17... | collective-permute-start | bytes 786440 | tf_op jit(solution)/shard_map/ppermute | solution.py:33
  39.8 11.5 %collective-permute-start.7 = (bf16[32,4096]{1,0:T(8,128)(2,1)S(1)}, bf16[32,4096]{1,0:T(8,128)(2,1)S(1)}, u32[]{:S(2)}, u32[]{:S(2)}) collective-permute-start(bf16[32,4096]{1,0:T(8,128)(2,1)S(1)} %collective-permute-done.6.refs_9_), channel_id=1, source_target_pairs={{0,24},{1,25},{2,26},{3,27},{4,28},{5,29},{6,30},{7,31},{8,0},{9,1... | collective-permute-start | bytes 786440 | tf_op jit(solution)/shard_map/ppermute | solution.py:33
  51.3 6.2 %collective-permute-start.8 = (bf16[32,4096]{1,0:T(8,128)(2,1)S(1)}, bf16[32,4096]{1,0:T(8,128)(2,1)S(1)}, u32[]{:S(2)}, u32[]{:S(2)}) collective-permute-start(bf16[32,4096]{1,0:T(8,128)(2,1)S(1)} %collective-permute-done.2.refs_0_.refs_12_), channel_id=1, source_target_pairs={{0,1},{1,0},{2,3},{3,2},{4,5},{5,4},{6,7},{7,6},{8,9},{9,8},{10,11... | collective-permute-start | bytes 786440 | tf_op jit(solution)/shard_map/ppermute | solution.py:33
  51.3 6.2 %collective-permute-start.9 = (bf16[32,4096]{1,0:T(8,128)(2,1)S(1)}, bf16[32,4096]{1,0:T(8,128)(2,1)S(1)}, u32[]{:S(2)}, u32[]{:S(2)}) collective-permute-start(bf16[32,4096]{1,0:T(8,128)(2,1)S(1)} %collective-permute-done.7.refs_1_.refs_13_), channel_id=1, source_target_pairs={{0,1},{1,0},{2,3},{3,2},{4,5},{5,4},{6,7},{7,6},{8,9},{9,8},{10,11... | collective-permute-start | bytes 786440 | tf_op jit(solution)/shard_map/ppermute | solution.py:33
  63.2 8.5 %collective-permute-start.22 = (bf16[256,128]{1,0:T(8,128)(2,1)S(1)}, bf16[256,128]{1,0:T(8,128)(2,1)S(1)}, u32[]{:S(2)}, u32[]{:S(2)}) collective-permute-start(bf16[256,128]{1,0:T(8,128)(2,1)S(1)} %conv_states.1), channel_id=1, source_target_pairs={{0,4},{1,5},{2,6},{3,7},{4,0},{5,1},{6,2},{7,3},{8,12},{9,13},{10,... | collective-permute-start | bytes 196616 | tf_op jit(solution)/shard_map/ppermute | solution.py:33
  71.8 8.8 %collective-permute-start.24 = (bf16[4,256,128]{2,1,0:T(8,128)(2,1)S(1)}, bf16[4,256,128]{2,1,0:T(8,128)(2,1)S(1)}, u32[]{:S(2)}, u32[]{:S(2)}) collective-permute-start(bf16[4,256,128]{2,1,0:T(8,128)(2,1)S(1)} %pad_maximum_fusion.2.own_ref), channel_id=1, source_target_pairs={{0,1},{1,0},{2,3},{3,2},{4,5},{5,4},{6,7},{7,6},{8,9},{9,8},{10,11... | collective-permute-start | bytes 786440 | tf_op jit(solution)/shard_map/ppermute | solution.py:33
  81.9 7.5 %collective-permute-start.27 = (f16[272,128]{1,0:T(8,128)(2,1)S(1)}, f16[272,128]{1,0:T(8,128)(2,1)S(1)}, u32[]{:S(2)}, u32[]{:S(2)}) collective-permute-start(f16[272,128]{1,0:T(8,128)(2,1)S(1)} %get-tuple-element.76), channel_id=1, source_target_pairs={{0,96},{32,64},{64,32},{96,0},{128,224},{160,192},{192,160},{224,1... | collective-permute-start | bytes 208904 | tf_op jit(solution)/shard_map/ppermute | solution.py:33
  90.3 12.2 %collective-permute-start.28 = (f16[272,128]{1,0:T(8,128)(2,1)S(1)}, f16[272,128]{1,0:T(8,128)(2,1)S(1)}, u32[]{:S(2)}, u32[]{:S(2)}) collective-permute-start(f16[272,128]{1,0:T(8,128)(2,1)S(1)} %convert_element_type.201), channel_id=1, source_target_pairs={{0,128},{32,160},{64,192},{96,224},{128,0},{160,32},{192,64},{224,... | collective-permute-start | bytes 208904 | tf_op jit(solution)/shard_map/ppermute | solution.py:33
  129.4 10.5 %collective-permute-start.35 = (bf16[192,4096]{1,0:T(8,128)(2,1)S(1)}, bf16[192,4096]{1,0:T(8,128)(2,1)S(1)}, u32[]{:S(2)}, u32[]{:S(2)}) collective-permute-start(bf16[192,4096]{1,0:T(8,128)(2,1)S(1)} %get-tuple-element.54), channel_id=1, source_target_pairs={{0,1},{1,0},{2,3},{3,2},{4,5},{5,4},{6,7},{7,6},{8,9},{9,8},{10,11... | collective-permute-start | bytes 4718600 | tf_op jit(solution)/shard_map/ppermute | solution.py:33
  130.2 9.5 %collective-permute-start.37 = (f16[32,4096]{1,0:T(8,128)(2,1)S(1)}, f16[32,4096]{1,0:T(8,128)(2,1)S(1)}, u32[]{:S(2)}, u32[]{:S(2)}) collective-permute-start(f16[32,4096]{1,0:T(8,128)(2,1)S(1)} %get-tuple-element.69), channel_id=1, source_target_pairs={{0,8},{1,9},{2,10},{3,11},{4,12},{5,13},{6,14},{7,15},{8,16},{9,17... | collective-permute-start | bytes 786440 | tf_op jit(solution)/shard_map/ppermute | solution.py:33
  130.3 9.5 %collective-permute-start.39 = (f16[32,4096]{1,0:T(8,128)(2,1)S(1)}, f16[32,4096]{1,0:T(8,128)(2,1)S(1)}, u32[]{:S(2)}, u32[]{:S(2)}) collective-permute-start(f16[32,4096]{1,0:T(8,128)(2,1)S(1)} %get-tuple-element.70), channel_id=1, source_target_pairs={{0,24},{1,25},{2,26},{3,27},{4,28},{5,29},{6,30},{7,31},{8,0},{9,1... | collective-permute-start | bytes 786440 | tf_op jit(solution)/shard_map/ppermute | solution.py:33
  140.6 9.7 %collective-permute-start.45 = (f16[64,2048]{1,0:T(8,128)(2,1)S(1)}, f16[64,2048]{1,0:T(8,128)(2,1)S(1)}, u32[]{:S(2)}, u32[]{:S(2)}) collective-permute-start(f16[64,2048]{1,0:T(8,128)(2,1)S(1)} %get-tuple-element.58), channel_id=1, source_target_pairs={{0,24},{1,25},{2,26},{3,27},{4,28},{5,29},{6,30},{7,31},{8,0},{9,1... | collective-permute-start | bytes 786440 | tf_op jit(solution)/shard_map/ppermute | solution.py:33
  143.5 10.4 %collective-permute-start.44 = (f16[64,2048]{1,0:T(8,128)(2,1)S(1)}, f16[64,2048]{1,0:T(8,128)(2,1)S(1)}, u32[]{:S(2)}, u32[]{:S(2)}) collective-permute-start(f16[64,2048]{1,0:T(8,128)(2,1)S(1)} %get-tuple-element.59), channel_id=1, source_target_pairs={{0,8},{1,9},{2,10},{3,11},{4,12},{5,13},{6,14},{7,15},{8,16},{9,17... | collective-permute-start | bytes 786440 | tf_op jit(solution)/shard_map/ppermute | solution.py:33
  143.6 15.0 %collective-permute-start.40 = (f16[64,2048]{1,0:T(8,128)(2,1)S(1)}, f16[64,2048]{1,0:T(8,128)(2,1)S(1)}, u32[]{:S(2)}, u32[]{:S(2)}) collective-permute-start(f16[64,2048]{1,0:T(8,128)(2,1)S(1)} %get-tuple-element.61), channel_id=1, source_target_pairs={{0,24},{1,25},{2,26},{3,27},{4,28},{5,29},{6,30},{7,31},{8,0},{9,1... | collective-permute-start | bytes 786440 | tf_op jit(solution)/shard_map/ppermute | solution.py:33
  146.8 11.8 %collective-permute-start.38 = (f16[64,2048]{1,0:T(8,128)(2,1)S(1)}, f16[64,2048]{1,0:T(8,128)(2,1)S(1)}, u32[]{:S(2)}, u32[]{:S(2)}) collective-permute-start(f16[64,2048]{1,0:T(8,128)(2,1)S(1)} %get-tuple-element.57), channel_id=1, source_target_pairs={{0,8},{1,9},{2,10},{3,11},{4,12},{5,13},{6,14},{7,15},{8,16},{9,17... | collective-permute-start | bytes 786440 | tf_op jit(solution)/shard_map/ppermute | solution.py:33
  154.1 7.0 %collective-permute-start.48 = (f16[16,2048]{1,0:T(8,128)(2,1)S(1)}, f16[16,2048]{1,0:T(8,128)(2,1)S(1)}, u32[]{:S(2)}, u32[]{:S(2)}) collective-permute-start(f16[16,2048]{1,0:T(8,128)(2,1)S(1)} %get-tuple-element.67), channel_id=1, source_target_pairs={{0,6},{1,7},{2,4},{3,5},{4,2},{5,3},{6,0},{7,1},{8,14},{9,15},{10,... | collective-permute-start | bytes 196616 | tf_op jit(solution)/shard_map/ppermute | solution.py:33
  156.0 7.7 %collective-permute-start.47 = (f16[16,2048]{1,0:T(8,128)(2,1)S(1)}, f16[16,2048]{1,0:T(8,128)(2,1)S(1)}, u32[]{:S(2)}, u32[]{:S(2)}) collective-permute-start(f16[16,2048]{1,0:T(8,128)(2,1)S(1)} %get-tuple-element.68), channel_id=1, source_target_pairs={{0,4},{1,5},{2,6},{3,7},{4,0},{5,1},{6,2},{7,3},{8,12},{9,13},{10,... | collective-permute-start | bytes 196616 | tf_op jit(solution)/shard_map/ppermute | solution.py:33
  156.0 7.7 %collective-permute-start.46 = (f16[16,2048]{1,0:T(8,128)(2,1)S(1)}, f16[16,2048]{1,0:T(8,128)(2,1)S(1)}, u32[]{:S(2)}, u32[]{:S(2)}) collective-permute-start(f16[16,2048]{1,0:T(8,128)(2,1)S(1)} %get-tuple-element.66), channel_id=1, source_target_pairs={{0,2},{1,3},{2,0},{3,1},{4,6},{5,7},{6,4},{7,5},{8,10},{9,11},{10,... | collective-permute-start | bytes 196616 | tf_op jit(solution)/shard_map/ppermute | solution.py:33
  158.7 6.3 %collective-permute-start.43 = (f16[16,2048]{1,0:T(8,128)(2,1)S(1)}, f16[16,2048]{1,0:T(8,128)(2,1)S(1)}, u32[]{:S(2)}, u32[]{:S(2)}) collective-permute-start(f16[16,2048]{1,0:T(8,128)(2,1)S(1)} %get-tuple-element.64), channel_id=1, source_target_pairs={{0,6},{1,7},{2,4},{3,5},{4,2},{5,3},{6,0},{7,1},{8,14},{9,15},{10,... | collective-permute-start | bytes 196616 | tf_op jit(solution)/shard_map/ppermute | solution.py:33
  (26 other events, 248.4 us)

commit v5 on v4

--- a/solution.py
+++ b/solution.py
@@ -76,102 +76,66 @@
     return high, (value - high.astype(F32)).astype(BF16)
 
 
-def project(parts, slots, idx, gate_w, input_w, small_w, bufs):
+def gate_of(parts, slots, idx, gate_w):
     depth = parts[0][0].shape[1]
     steps = 4
     kb = depth // steps
     count = len(slots)
     rows = 128 * count
-    weights, wspecs, outs, accs = [], [], [], []
-    if gate_w is not None:
-        weights.append(gate_w)
-        wspecs.append(pl.BlockSpec((kb, 512), lambda k, i: (k, 0)))
-        outs.append(sds((512, 512), BF16))
-        accs.append(pltpu.VMEM((rows, 512), F32))
-    if input_w is not None:
-        weights += [input_w, small_w]
-        wspecs += [
-            pl.BlockSpec((kb, 512), lambda k, i: (k, 0)),
-            pl.BlockSpec((256, kb), lambda k, i: (0, k)),
-        ]
-        outs += [sds((512, 512), BF16), sds((512, 128), BF16), sds((8, 512), F32)]
-        accs += [pltpu.VMEM((rows, 512), F32), pltpu.VMEM((rows, 256), F32)]
-    nw, no, na = len(weights), len(outs), len(accs)
-    aliased = [] if bufs is None else list(bufs)
-    ready = [pltpu.VMEM((rows, 512), BF16)] if gate_w is not None else []
-    if input_w is not None:
-        ready += [pltpu.VMEM((rows, 512), BF16), pltpu.VMEM((rows, 128), BF16), pltpu.VMEM((8, rows), F32)]
-        ready += [pltpu.VMEM((rows, 128), F32)]
     nl = len(parts)
 
     def kernel(i, *refs):
-        lrefs, refs = refs[:nl], refs[nl:]
-        wrefs, refs = refs[:nw], refs[nw + len(aliased) :]
-        orefs, refs = refs[:no], refs[no:]
-        arefs, refs = refs[:na], refs[na:]
-        rrefs, sem = refs[:-1], refs[-1]
+        lrefs, w_ref, out_ref, acc, ready, sem = refs[:nl], *refs[nl:]
         k = pl.program_id(0)
-        lhs = jnp.concatenate([r[...] for r in lrefs], axis=0)
-        for n, w in enumerate(wrefs):
-            nt = input_w is not None and n == nw - 1
-            part = dot_nt(lhs, w[...]) if nt else dot(lhs, w[...])
-
-            @pl.when(k == 0)
-            def _():
-                arefs[n][...] = part
-
-            @pl.when(k > 0)
-            def _():
-                arefs[n][...] += part
+        part = dot(jnp.concatenate([r[...] for r in lrefs], axis=0), w_ref[...])
+
+        @pl.when(k == 0)
+        def _():
+            acc[...] = part
+
+        @pl.when(k > 0)
+        def _():
+            acc[...] += part
 
         @pl.when(k == steps - 1)
         def _():
+            def tile(n, carry):
+                at = pl.ds(pl.multiple_of(n * 16, 16), 16)
+                to = i[4 + lax.rem(n, 8)] * 16 + lax.div(n, 8) * 128
+                rounded = acc[at, :].astype(BF16).astype(F32)
+                ready[pl.ds(pl.multiple_of(to, 16), 16), :] = silu(rounded)
+                return carry
+
+            lax.fori_loop(0, 8 * count, tile, 0, unroll=2)
             copies = []
             for s in range(count):
-                for t in range(8):
-                    at = slice(s * 128 + t * 16, s * 128 + t * 16 + 16)
-                    dst = pl.ds(pl.multiple_of(i[4 + t] * 16, 16) + s * 128, 16)
-                    n = 0
-                    if gate_w is not None:
-                        rrefs[n][dst, :] = arefs[n][at, :].astype(BF16)
-                        n += 1
-                    if input_w is not None:
-                        rrefs[n][dst, :] = arefs[n][at, :].astype(BF16)
-                        rrefs[n + 1][dst, :] = arefs[n + 1][at, 0:128].astype(BF16)
-                        rrefs[n + 3][dst, :] = arefs[n + 1][at, 128:256]
-                here = slice(s * 128, s * 128 + 128)
-                if input_w is not None:
-                    rrefs[n + 2][:, here] = jnp.transpose(rrefs[n + 3][here, :])[0:8, :]
                 there = pl.ds(pl.multiple_of(i[slots[s]] * 128, 128), 128)
-                for n in range(no):
-                    if n == no - 1 and input_w is not None:
-                        source, target = rrefs[n].at[:, here], orefs[n].at[:, there]
-                    else:
-                        source, target = rrefs[n].at[here, :], orefs[n].at[there, :]
-                    copies.append(pltpu.make_async_copy(source, target, sem.at[len(copies)]))
+                copies.append(
+                    pltpu.make_async_copy(ready.at[s * 128 : s * 128 + 128, :], out_ref.at[there, :], sem.at[s])
+                )
             for copy in copies:
                 copy.start()
             for copy in copies:
                 copy.wait()
 
-    cols = (512 if gate_w is not None else 0) + (768 if input_w is not None else 0)
-    first = 1 + nl + nw
-    lspecs = [pl.BlockSpec((32, kb), lambda k, i, b=b: (b, k)) for _, b in parts]
-    out = pl.pallas_call(
+    return pl.pallas_call(
         kernel,
-        out_shape=outs,
+        out_shape=sds((512, 512), F32),
         grid_spec=pltpu.PrefetchScalarGridSpec(
             num_scalar_prefetch=1,
             grid=(steps,),
-            in_specs=lspecs + wspecs + [pl.BlockSpec(memory_space=pl.ANY)] * len(aliased),
-            out_specs=[pl.BlockSpec(memory_space=pl.ANY)] * no,
-            scratch_shapes=accs + ready + [pltpu.SemaphoreType.DMA((no * count,))],
+            in_specs=[pl.BlockSpec((32, kb), lambda k, i, b=b: (b, k)) for _, b in parts]
+            + [pl.BlockSpec((kb, 512), lambda k, i: (k, 0))],
+            out_specs=pl.BlockSpec(memory_space=pl.ANY),
+            scratch_shapes=[
+                pltpu.VMEM((rows, 512), F32),
+                pltpu.VMEM((rows, 512), F32),
+                pltpu.SemaphoreType.DMA((count,)),
+            ],
         ),
-        input_output_aliases={first + n: n for n in range(len(aliased))},
-        compiler_params=pltpu.CompilerParams(vmem_limit_bytes=14 * MIB),
-        cost_estimate=cost(2 * rows * depth * cols, 2 * depth * cols),
-    )(idx, *[p for p, _ in parts], *weights, *aliased)
-    return list(out)
+        compiler_params=pltpu.CompilerParams(vmem_limit_bytes=14 * MIB),
+        cost_estimate=cost(2 * rows * depth * 512, 2 * depth * 512),
+    )(idx, *[p for p, _ in parts], gate_w)
 
 
 def project_resident(parts, halo, slots, idx, input_w, small_w, bufs):
@@ -564,7 +528,7 @@
             ch = slice(128 * p, 128 * p + 128)
             carried = dot(read, halves[p][0]) + dot(read, halves[p][1])
             y = y_ref[here, ch] + pair_scale(cols, p) * carried
-            u = y * silu(gate_ref[here, ch].astype(F32))
+            u = y * gate_ref[here, ch]
             u_ref[here, ch] = u
             squares = squares + u * u
         ss_ref[pl.ds(k, 1), :] = jnp.sum(jnp.transpose(squares), axis=0, keepdims=True)
@@ -737,10 +701,10 @@
     inc, pre, total = prefix_stage(idx, *ends)
     before = half_flip(total, 4)
     everything = own_parts + rights + lefts + fars
-    (gate_rows,) = project(everything, [0, 1, 2, 3], idx, gate_weight, None, None, None)
+    gate = gate_of(everything, [0, 1, 2, 3], idx, gate_weight)
     spread = spread_stage(idx, inc, pre, before)
     quarters = [spread[0]] + [half_flip(spread[s], s) for s in (1, 2, 3)]
-    u, squares = gate_stage(idx, y_local, read_vec, quarters, cum, gate_rows)
+    u, squares = gate_stage(idx, y_local, read_vec, quarters, cum, gate)
 
     squares = squares + flip(squares, "tp", 1)
     squares = squares + flip(squares, "tp", 2)

time: 169 us -> 169 us (level)
  no operation moved by 1% of the time
where the time goes in v5:
time: 169 us; the launch traced here: 167 us
  starting transfers between devices  68.2 us (40%)
  waiting for transfers between devices  58.4 us (35%)
  Pallas kernels  33 us (20%)
  other arithmetic  5.44 us (3%)
    ppermute x45, starting transfers between devices, send(): return lax.ppermute(array, axis, pairs)  64.1 us
    ppermute x45, waiting for transfers between devices, send(): return lax.ppermute(array, axis, pairs)  55.6 us
    pallas_call x2, Pallas kernels, project_resident(): pl.pallas_call(kernel, out_shape=outs, in_specs=[SM] + [VM] * (nl + 2) +...  8.19 us
    pallas_call x2, Pallas kernels, out_block(): pl.pallas_call(kernel, out_shape=[sds((rows, 4096), F32), sds((rows, 4096...  5.7 us
    pallas_call x1, Pallas kernels, gate_of(): pl.pallas_call(kernel, out_shape=sds((512, 512), F32), grid_spec=pltpu.Pr...  4.87 us
    ppermute x4, starting transfers between devices, hop(): return lax.ppermute(array, ('ctx', 'tp'), pairs)  4.18 us
    pallas_call x1, Pallas kernels, scan_stage(): pl.pallas_call(scan_kernel, out_shape=[sds((512, 512), F32), sds((512, 25...  4.16 us
    pallas_call x1, Pallas kernels, inputs_stage(): pl.pallas_call(inputs_kernel, out_shape=[sds((512, 512), BF16)] * 3 + [sd...  3.45 us
  transfers between devices with their start and end apart: 49, of which 22 were waited for; matrix products, arithmetic and copies ran while one was open for 3% of the time, Pallas kernels for 13%

profile of v5, /device:TPU:24, one launch (start us, length us, event | category | flops | bytes accessed | tf_op | source)
XLA Modules:
  0.0 167.0 jit_solution(5830544826068397797)
XLA Ops:
  1.9 3.3 %collective-permute-start.3 = (bf16[16,4096]{1,0:T(8,128)(2,1)}, bf16[16,4096]{1,0:T(8,128)(2,1)S(1)}, u32[]{:S(2)}, u32[]{:S(2)}) collective-permute-start(bf16[16,4096]{1,0:T(8,128)(2,1)} %param.12), channel_id=1, source_target_pairs={{0,4},{1,5},{2,6},{3,7},{4,0},{5,1},{6,2},{7,3},{8,12},{9,13},{10,... | collective-permute-start | bytes 393224 | tf_op jit(solution)/shard_map/ppermute | solution.py:33
  6.8 8.6 %collective-permute-done.3 = bf16[16,4096]{1,0:T(8,128)(2,1)S(1)} collective-permute-done((bf16[16,4096]{1,0:T(8,128)(2,1)}, bf16[16,4096]{1,0:T(8,128)(2,1)S(1)}, u32[]{:S(2)}, u32[]{:S(2)}) %collective-permute-start.3) | collective-permute-done | bytes 131104 | tf_op jit(solution)/shard_map/ppermute | solution.py:33
  20.7 7.2 %collective-permute-start.17 = (bf16[32,4096]{1,0:T(8,128)(2,1)S(1)}, bf16[32,4096]{1,0:T(8,128)(2,1)S(1)}, u32[]{:S(2)}, u32[]{:S(2)}) collective-permute-start(bf16[32,4096]{1,0:T(8,128)(2,1)S(1)} %constant_dynamic-update-slice_fusion.refs_0_), channel_id=1, source_target_pairs={{0,24},{1,25},{2,26},{3,27},{4,28},{5,29},{6,30},{7,31},{8,0},{9,1... | collective-permute-start | bytes 786440 | tf_op jit(solution)/shard_map/ppermute | solution.py:33
  27.9 2.7 %collective-permute-done.12 = bf16[8,4096]{1,0:T(8,128)(2,1)S(1)} collective-permute-done((bf16[8,4096]{1,0:T(8,128)(2,1)S(1)}, bf16[8,4096]{1,0:T(8,128)(2,1)S(1)}, u32[]{:S(2)}, u32[]{:S(2)}) %collective-permute-start.12) | collective-permute-done | bytes 65568 | tf_op jit(solution)/shard_map/ppermute | solution.py:39
  32.4 3.3 %collective-permute-done.1.refs_4_ = bf16[32,4096]{1,0:T(8,128)(2,1)S(1)} collective-permute-done((bf16[32,4096]{1,0:T(8,128)(2,1)S(1)}, bf16[32,4096]{1,0:T(8,128)(2,1)S(1)}, u32[]{:S(2)}, u32[]{:S(2)}) %collective-permute-start.1) | collective-permute-done | bytes 262176 | tf_op jit(solution)/shard_map/ppermute | solution.py:33
  36.6 2.1 %collective-permute-start.2 = (bf16[32,4096]{1,0:T(8,128)(2,1)S(1)}, bf16[32,4096]{1,0:T(8,128)(2,1)S(1)}, u32[]{:S(2)}, u32[]{:S(2)}) collective-permute-start(bf16[32,4096]{1,0:T(8,128)(2,1)S(1)} %collective-permute-done.1.refs_4_), channel_id=1, source_target_pairs={{0,8},{1,9},{2,10},{3,11},{4,12},{5,13},{6,14},{7,15},{8,16},{9,17... | collective-permute-start | bytes 786440 | tf_op jit(solution)/shard_map/ppermute | solution.py:33
  39.8 3.3 %collective-permute-start.7 = (bf16[32,4096]{1,0:T(8,128)(2,1)S(1)}, bf16[32,4096]{1,0:T(8,128)(2,1)S(1)}, u32[]{:S(2)}, u32[]{:S(2)}) collective-permute-start(bf16[32,4096]{1,0:T(8,128)(2,1)S(1)} %collective-permute-done.6.refs_9_), channel_id=1, source_target_pairs={{0,24},{1,25},{2,26},{3,27},{4,28},{5,29},{6,30},{7,31},{8,0},{9,1... | collective-permute-start | bytes 786440 | tf_op jit(solution)/shard_map/ppermute | solution.py:33
  43.1 3.0 %collective-permute-done.16.refs_5_ = bf16[32,4096]{1,0:T(8,128)(2,1)S(1)} collective-permute-done((bf16[32,4096]{1,0:T(8,128)(2,1)S(1)}, bf16[32,4096]{1,0:T(8,128)(2,1)S(1)}, u32[]{:S(2)}, u32[]{:S(2)}) %collective-permute-start.16) | collective-permute-done | bytes 262176 | tf_op jit(solution)/shard_map/ppermute | solution.py:33
  46.2 5.0 %collective-permute-done.2.refs_0_.refs_12_ = bf16[32,4096]{1,0:T(8,128)(2,1)S(1)} collective-permute-done((bf16[32,4096]{1,0:T(8,128)(2,1)S(1)}, bf16[32,4096]{1,0:T(8,128)(2,1)S(1)}, u32[]{:S(2)}, u32[]{:S(2)}) %collective-permute-start.2) | collective-permute-done | bytes 262176 | tf_op jit(solution)/shard_map/ppermute | solution.py:33
  52.1 5.3 %shard_map.118 = (bf16[512,512]{1,0:T(8,128)(2,1)S(1)}, bf16[512,128]{1,0:T(8,128)(2,1)S(1)}, f32[8,512]{1,0:T(8,128)S(1)}) custom-call(s32[16]{0:T(128)S(1)} %compare_select_fusion.9.i.idx, bf16[32,4096]{1,0:T(8,128)(2,1)S(1)} %constant_dynamic-update-slice_fusion.refs_0_, bf16[32,4096]{1,0:T(8,128)(2,1)S(1)} %constant_dynamic-update-slice_fusion.2.refs_1_, ...), custom_call_target="tpu_custom_call" | custom-call | flops 2415919104 | bytes 6291456 | tf_op jit(solution)/shard_map/pallas_call | solution.py:209
  57.6 2.9 %shard_map.119 = (bf16[512,512]{1,0:T(8,128)(2,1)S(1)}, bf16[512,128]{1,0:T(8,128)(2,1)S(1)}, f32[8,512]{1,0:T(8,128)S(1)}, bf16[16,640]{1,0:T(8,128)(2,1)S(1)}) custom-call(s32[16]{0:T(128)S(1)} %compare_select_fusion.9.i.idx, ...), custom_call_target="tpu_custom_call", output_to_operand_aliasing={{0}: (8, {}), {1}: (9, {}), {2}: (10, {})} | custom-call | flops 805306368 | bytes 6291456 | tf_op jit(solution)/shard_map/pallas_call | solution.py:209
  63.2 3.6 %collective-permute-start.22 = (bf16[256,128]{1,0:T(8,128)(2,1)S(1)}, bf16[256,128]{1,0:T(8,128)(2,1)S(1)}, u32[]{:S(2)}, u32[]{:S(2)}) collective-permute-start(bf16[256,128]{1,0:T(8,128)(2,1)S(1)} %conv_states.1), channel_id=1, source_target_pairs={{0,4},{1,5},{2,6},{3,7},{4,0},{5,1},{6,2},{7,3},{8,12},{9,13},{10,... | collective-permute-start | bytes 196616 | tf_op jit(solution)/shard_map/ppermute | solution.py:33
  67.4 4.3 %collective-permute-done.22 = bf16[256,128]{1,0:T(8,128)(2,1)S(1)} collective-permute-done((bf16[256,128]{1,0:T(8,128)(2,1)S(1)}, bf16[256,128]{1,0:T(8,128)(2,1)S(1)}, u32[]{:S(2)}, u32[]{:S(2)}) %collective-permute-start.22) | collective-permute-done | bytes 65568 | tf_op jit(solution)/shard_map/ppermute | solution.py:33
  72.0 3.4 %inputs_stage.1 = (bf16[512,512]{1,0:T(8,128)(2,1)S(1)}, bf16[512,512]{1,0:T(8,128)(2,1)S(1)}, bf16[512,512]{1,0:T(8,128)(2,1)S(1)}, f32[8,512]{1,0:T(8,128)S(1)}, f32[8,512]{1,0:T(8,128)S(1)}) custom-call(f32[24]{0:T(128)S(1)} %pad_maximum_fusion.5.par_ref, bf16[512,512]{1,0:T(8,128)(2,1)S(1)} %get-tuple-element.39.rows_ref, ...), custom_call_target="tpu_custom_call" | custom-call | flops 10000000 | bytes 2000000 | tf_op jit(solution)/shard_map/inputs_stage/pallas_call | solution.py:314
  75.4 4.9 %shard_map.120.gate_ref = f32[512,512]{1,0:T(8,128)S(1)} custom-call(s32[16]{0:T(128)S(1)} %compare_select_fusion.9.i.idx, bf16[32,4096]{1,0:T(8,128)(2,1)S(1)} %constant_dynamic-update-slice_fusion.refs_0_, bf16[32,4096]{1,0:T(8,128)(2,1)S(1)} %constant_dynamic-update-slice_fusion.2.refs_1_, bf16[32,4096]{1,0:T(8,128)(2,1)S(1)} %collective-permute-done.5.refs_2_, ...), custom_call_target="tpu_custom_call" | custom-call | flops 2147483648 | bytes 4194304 | tf_op jit(solution)/shard_map/pallas_call | solution.py:121
  81.7 4.6 %collective-permute-start.27 = (f16[272,128]{1,0:T(8,128)(2,1)S(1)}, f16[272,128]{1,0:T(8,128)(2,1)S(1)}, u32[]{:S(2)}, u32[]{:S(2)}) collective-permute-start(f16[272,128]{1,0:T(8,128)(2,1)S(1)} %get-tuple-element.76), channel_id=1, source_target_pairs={{0,96},{32,64},{64,32},{96,0},{128,224},{160,192},{192,160},{224,1... | collective-permute-start | bytes 208904 | tf_op jit(solution)/shard_map/ppermute | solution.py:33
  90.0 8.1 %collective-permute-start.28 = (f16[272,128]{1,0:T(8,128)(2,1)S(1)}, f16[272,128]{1,0:T(8,128)(2,1)S(1)}, u32[]{:S(2)}, u32[]{:S(2)}) collective-permute-start(f16[272,128]{1,0:T(8,128)(2,1)S(1)} %convert_element_type.201), channel_id=1, source_target_pairs={{0,128},{32,160},{64,192},{96,224},{128,0},{160,32},{192,64},{224,... | collective-permute-start | bytes 208904 | tf_op jit(solution)/shard_map/ppermute | solution.py:33
  98.1 4.2 %scan_stage.1 = (f32[512,512]{1,0:T(8,128)S(1)}, bf16[512,256]{1,0:T(8,128)(2,1)S(1)}) custom-call(s32[16]{0:T(128)S(1)} %compare_select_fusion.9.i.idx, f32[24]{0:T(128)S(1)} %pad_maximum_fusion.5.par_ref, bf16[4,256,128]{2,1,0:T(8,128)(2,1)S(1)} %pad_maximum_fusion.2.own_ref, bf16[4,256,128]{2,1,0:T(8,128)(2,1)S(1)} %collective-permute-done.24.oth_ref, ...), custom_call_target="tpu_custom_call" | custom-call | flops 6000000000 | bytes 3000000 | tf_op jit(solution)/shard_map/scan_stage/pallas_call | solution.py:499
  103.2 2.1 %collective-permute-start.30 = (f16[272,128]{1,0:T(8,128)(2,1)S(1)}, f16[272,128]{1,0:T(8,128)(2,1)S(1)}, u32[]{:S(2)}, u32[]{:S(2)}) collective-permute-start(f16[272,128]{1,0:T(8,128)(2,1)S(1)} %get-tuple-element.74), channel_id=1, source_target_pairs={{0,64},{32,96},{64,0},{96,32},{128,192},{160,224},{192,128},{224,1... | collective-permute-start | bytes 208904 | tf_op jit(solution)/shard_map/ppermute | solution.py:33
  105.3 2.6 %collective-permute-start.31 = (f16[272,128]{1,0:T(8,128)(2,1)S(1)}, f16[272,128]{1,0:T(8,128)(2,1)S(1)}, u32[]{:S(2)}, u32[]{:S(2)}) collective-permute-start(f16[272,128]{1,0:T(8,128)(2,1)S(1)} %get-tuple-element.73), channel_id=1, source_target_pairs={{0,96},{32,64},{64,32},{96,0},{128,224},{160,192},{192,160},{224,1... | collective-permute-start | bytes 208904 | tf_op jit(solution)/shard_map/ppermute | solution.py:33
  110.8 3.0 %gate_stage.1 = (f32[512,512]{1,0:T(8,128)S(1)}, f32[4,128]{1,0:T(4,128)S(1)}) custom-call(s32[16]{0:T(128)S(1)} %compare_select_fusion.9.i.idx, f32[512,512]{1,0:T(8,128)S(1)} %get-tuple-element.44.y_ref, bf16[512,256]{1,0:T(8,128)(2,1)S(1)} %get-tuple-element.45.read_ref, f32[272,128]{1,0:T(8,128)S(1)} %slice_bitcast_fusion.q0, ...), custom_call_target="tpu_custom_call" | custom-call | flops 200000000 | bytes 3000000 | tf_op jit(solution)/shard_map/gate_stage/pallas_call | solution.py:541
  115.6 3.3 %collective-permute-done.33 = f32[4,128]{1,0:T(4,128)S(1)} collective-permute-done((f32[4,128]{1,0:T(4,128)S(1)}, f32[4,128]{1,0:T(4,128)S(1)}, u32[]{:S(2)}, u32[]{:S(2)}) %collective-permute-start.33) | collective-permute-done | bytes 2080 | tf_op jit(solution)/shard_map/ppermute | solution.py:33
  120.0 3.5 %collective-permute-done.34 = f32[4,128]{1,0:T(4,128)S(1)} collective-permute-done((f32[4,128]{1,0:T(4,128)S(1)}, f32[4,128]{1,0:T(4,128)S(1)}, u32[]{:S(2)}, u32[]{:S(2)}) %collective-permute-start.34) | collective-permute-done | bytes 2080 | tf_op jit(solution)/shard_map/ppermute | solution.py:33
  125.5 3.7 %out_block.2 = (f32[192,4096]{1,0:T(8,128)S(1)}, bf16[192,4096]{1,0:T(8,128)(2,1)S(1)}) custom-call(s32[16]{0:T(128)S(1)} %compare_select_fusion.9.i.idx, f32[512,512]{1,0:T(8,128)S(1)} %get-tuple-element.51.u_ref, f32[4,128]{1,0:T(4,128)S(1)} %add.206.ss_ref, f32[1,512]{1,0:T(1,128)S(1)} %bitcast.27, bf16[512,4096]{1,0:T(8,128)(2,1)S(1)} %load.1.w_ref), custom_call_target="tpu_custom_call" | custom-call | flops 1610612736 | bytes 6000000 | tf_op jit(solution)/shard_map/out_block/pallas_call | solution.py:599
  130.1 3.2 %collective-permute-start.39 = (f16[32,4096]{1,0:T(8,128)(2,1)S(1)}, f16[32,4096]{1,0:T(8,128)(2,1)S(1)}, u32[]{:S(2)}, u32[]{:S(2)}) collective-permute-start(f16[32,4096]{1,0:T(8,128)(2,1)S(1)} %get-tuple-element.70), channel_id=1, source_target_pairs={{0,24},{1,25},{2,26},{3,27},{4,28},{5,29},{6,30},{7,31},{8,0},{9,1... | collective-permute-start | bytes 786440 | tf_op jit(solution)/shard_map/ppermute | solution.py:33
  133.4 6.2 %collective-permute-done.37 = f16[32,4096]{1,0:T(8,128)(2,1)S(1)} collective-permute-done((f16[32,4096]{1,0:T(8,128)(2,1)S(1)}, f16[32,4096]{1,0:T(8,128)(2,1)S(1)}, u32[]{:S(2)}, u32[]{:S(2)}) %collective-permute-start.37) | collective-permute-done | bytes 262176 | tf_op jit(solution)/shard_map/ppermute | solution.py:33
  140.3 3.0 %collective-permute-start.45 = (f16[64,2048]{1,0:T(8,128)(2,1)S(1)}, f16[64,2048]{1,0:T(8,128)(2,1)S(1)}, u32[]{:S(2)}, u32[]{:S(2)}) collective-permute-start(f16[64,2048]{1,0:T(8,128)(2,1)S(1)} %get-tuple-element.58), channel_id=1, source_target_pairs={{0,24},{1,25},{2,26},{3,27},{4,28},{5,29},{6,30},{7,31},{8,0},{9,1... | collective-permute-start | bytes 786440 | tf_op jit(solution)/shard_map/ppermute | solution.py:33
  143.3 3.2 %collective-permute-start.40 = (f16[64,2048]{1,0:T(8,128)(2,1)S(1)}, f16[64,2048]{1,0:T(8,128)(2,1)S(1)}, u32[]{:S(2)}, u32[]{:S(2)}) collective-permute-start(f16[64,2048]{1,0:T(8,128)(2,1)S(1)} %get-tuple-element.61), channel_id=1, source_target_pairs={{0,24},{1,25},{2,26},{3,27},{4,28},{5,29},{6,30},{7,31},{8,0},{9,1... | collective-permute-start | bytes 786440 | tf_op jit(solution)/shard_map/ppermute | solution.py:33
  146.5 3.5 %collective-permute-done.45 = f16[64,2048]{1,0:T(8,128)(2,1)S(1)} collective-permute-done((f16[64,2048]{1,0:T(8,128)(2,1)S(1)}, f16[64,2048]{1,0:T(8,128)(2,1)S(1)}, u32[]{:S(2)}, u32[]{:S(2)}) %collective-permute-start.45) | collective-permute-done | bytes 262176 | tf_op jit(solution)/shard_map/ppermute | solution.py:33
  150.0 3.7 %collective-permute-done.44 = f16[64,2048]{1,0:T(8,128)(2,1)S(1)} collective-permute-done((f16[64,2048]{1,0:T(8,128)(2,1)S(1)}, f16[64,2048]{1,0:T(8,128)(2,1)S(1)}, u32[]{:S(2)}, u32[]{:S(2)}) %collective-permute-start.44) | collective-permute-done | bytes 262176 | tf_op jit(solution)/shard_map/ppermute | solution.py:33
  155.8 2.5 %collective-permute-start.46 = (f16[16,2048]{1,0:T(8,128)(2,1)S(1)}, f16[16,2048]{1,0:T(8,128)(2,1)S(1)}, u32[]{:S(2)}, u32[]{:S(2)}) collective-permute-start(f16[16,2048]{1,0:T(8,128)(2,1)S(1)} %get-tuple-element.66), channel_id=1, source_target_pairs={{0,2},{1,3},{2,0},{3,1},{4,6},{5,7},{6,4},{7,5},{8,10},{9,11},{10,... | collective-permute-start | bytes 196616 | tf_op jit(solution)/shard_map/ppermute | solution.py:33
  160.7 2.1 %collective-permute-start.41 = (f16[16,2048]{1,0:T(8,128)(2,1)S(1)}, f16[16,2048]{1,0:T(8,128)(2,1)S(1)}, u32[]{:S(2)}, u32[]{:S(2)}) collective-permute-start(f16[16,2048]{1,0:T(8,128)(2,1)S(1)} %get-tuple-element.63), channel_id=1, source_target_pairs={{0,2},{1,3},{2,0},{3,1},{4,6},{5,7},{6,4},{7,5},{8,10},{9,11},{10,... | collective-permute-start | bytes 196616 | tf_op jit(solution)/shard_map/ppermute | solution.py:33
  (144 shorter events, 40.9 us)
Async XLA Ops:
  0.0 6.8 %collective-permute-start = (bf16[16,4096]{1,0:T(8,128)(2,1)}, bf16[16,4096]{1,0:T(8,128)(2,1)S(1)}, u32[]{:S(2)}, u32[]{:S(2)}) collective-permute-start(bf16[16,4096]{1,0:T(8,128)(2,1)} %param.12), channel_id=1, source_target_pairs={{0,2},{1,3},{2,0},{3,1},{4,6},{5,7},{6,4},{7,5},{8,10},{9,11},{10,... | collective-permute-start | bytes 393224 | tf_op jit(solution)/shard_map/ppermute | solution.py:33
  1.9 13.5 %collective-permute-start.3 = (bf16[16,4096]{1,0:T(8,128)(2,1)}, bf16[16,4096]{1,0:T(8,128)(2,1)S(1)}, u32[]{:S(2)}, u32[]{:S(2)}) collective-permute-start(bf16[16,4096]{1,0:T(8,128)(2,1)} %param.12), channel_id=1, source_target_pairs={{0,4},{1,5},{2,6},{3,7},{4,0},{5,1},{6,2},{7,3},{8,12},{9,13},{10,... | collective-permute-start | bytes 393224 | tf_op jit(solution)/shard_map/ppermute | solution.py:33
  5.2 10.2 %collective-permute-start.4 = (bf16[16,4096]{1,0:T(8,128)(2,1)}, bf16[16,4096]{1,0:T(8,128)(2,1)S(1)}, u32[]{:S(2)}, u32[]{:S(2)}) collective-permute-start(bf16[16,4096]{1,0:T(8,128)(2,1)} %param.12), channel_id=1, source_target_pairs={{0,6},{1,7},{2,4},{3,5},{4,2},{5,3},{6,0},{7,1},{8,14},{9,15},{10,... | collective-permute-start | bytes 393224 | tf_op jit(solution)/shard_map/ppermute | solution.py:33
  5.2 31.4 %collective-permute-start.14 = (bf16[64,4096]{1,0:T(8,128)(2,1)}, bf16[64,4096]{1,0:T(8,128)(2,1)S(1)}, u32[]{:S(2)}, u32[]{:S(2)}) collective-permute-start(bf16[64,4096]{1,0:T(8,128)(2,1)} %bitcast.28), channel_id=1, source_target_pairs={{0,1},{1,0},{2,3},{3,2},{4,5},{5,4},{6,7},{7,6},{8,9},{9,8},{10,11... | collective-permute-start | bytes 1572872 | tf_op jit(solution)/shard_map/ppermute | solution.py:33
  5.2 12.5 %collective-permute-start.20 = (f32[5,64]{1,0:T(8,128)}, f32[5,64]{1,0:T(8,128)S(1)}, u32[]{:S(2)}, u32[]{:S(2)}) collective-permute-start(f32[5,64]{1,0:T(8,128)} %param.18), channel_id=1, source_target_pairs={{0,1},{1,0},{2,3},{3,2},{4,5},{5,4},{6,7},{7,6},{8,9},{9,8},{10,11... | collective-permute-start | bytes 3848 | tf_op jit(solution)/shard_map/ppermute | solution.py:33
  17.0 15.3 %collective-permute-start.5 = (bf16[32,4096]{1,0:T(8,128)(2,1)S(1)}, bf16[32,4096]{1,0:T(8,128)(2,1)S(1)}, u32[]{:S(2)}, u32[]{:S(2)}) collective-permute-start(bf16[32,4096]{1,0:T(8,128)(2,1)S(1)} %constant_dynamic-update-slice_fusion.refs_0_), channel_id=1, source_target_pairs={{0,1},{1,0},{2,3},{3,2},{4,5},{5,4},{6,7},{7,6},{8,9},{9,8},{10,11... | collective-permute-start | bytes 786440 | tf_op jit(solution)/shard_map/ppermute | solution.py:33
  18.5 12.2 %collective-permute-start.12 = (bf16[8,4096]{1,0:T(8,128)(2,1)S(1)}, bf16[8,4096]{1,0:T(8,128)(2,1)S(1)}, u32[]{:S(2)}, u32[]{:S(2)}) collective-permute-start(bf16[8,4096]{1,0:T(8,128)(2,1)S(1)} %add.201), channel_id=1, source_target_pairs={{24,0},{25,1},{26,2},{27,3},{28,4},{29,5},{30,6},{31,7},{56,32},{5... | collective-permute-start | bytes 196616 | tf_op jit(solution)/shard_map/ppermute | solution.py:39
  19.8 15.9 %collective-permute-start.1 = (bf16[32,4096]{1,0:T(8,128)(2,1)S(1)}, bf16[32,4096]{1,0:T(8,128)(2,1)S(1)}, u32[]{:S(2)}, u32[]{:S(2)}) collective-permute-start(bf16[32,4096]{1,0:T(8,128)(2,1)S(1)} %constant_dynamic-update-slice_fusion.refs_0_), channel_id=1, source_target_pairs={{0,8},{1,9},{2,10},{3,11},{4,12},{5,13},{6,14},{7,15},{8,16},{9,17... | collective-permute-start | bytes 786440 | tf_op jit(solution)/shard_map/ppermute | solution.py:33
  20.7 15.0 %collective-permute-start.17 = (bf16[32,4096]{1,0:T(8,128)(2,1)S(1)}, bf16[32,4096]{1,0:T(8,128)(2,1)S(1)}, u32[]{:S(2)}, u32[]{:S(2)}) collective-permute-start(bf16[32,4096]{1,0:T(8,128)(2,1)S(1)} %constant_dynamic-update-slice_fusion.refs_0_), channel_id=1, source_target_pairs={{0,24},{1,25},{2,26},{3,27},{4,28},{5,29},{6,30},{7,31},{8,0},{9,1... | collective-permute-start | bytes 786440 | tf_op jit(solution)/shard_map/ppermute | solution.py:33
  32.3 7.5 %collective-permute-start.6 = (bf16[32,4096]{1,0:T(8,128)(2,1)S(1)}, bf16[32,4096]{1,0:T(8,128)(2,1)S(1)}, u32[]{:S(2)}, u32[]{:S(2)}) collective-permute-start(bf16[32,4096]{1,0:T(8,128)(2,1)S(1)} %constant_dynamic-update-slice_fusion.2.refs_1_), channel_id=1, source_target_pairs={{0,24},{1,25},{2,26},{3,27},{4,28},{5,29},{6,30},{7,31},{8,0},{9,1... | collective-permute-start | bytes 786440 | tf_op jit(solution)/shard_map/ppermute | solution.py:33
  35.7 16.4 %collective-permute-start.15 = (bf16[32,4096]{1,0:T(8,128)(2,1)S(1)}, bf16[32,4096]{1,0:T(8,128)(2,1)S(1)}, u32[]{:S(2)}, u32[]{:S(2)}) collective-permute-start(bf16[32,4096]{1,0:T(8,128)(2,1)S(1)} %constant_dynamic-update-slice_fusion.2.refs_1_), channel_id=1, source_target_pairs={{0,1},{1,0},{2,3},{3,2},{4,5},{5,4},{6,7},{7,6},{8,9},{9,8},{10,11... | collective-permute-start | bytes 786440 | tf_op jit(solution)/shard_map/ppermute | solution.py:33
  35.7 10.4 %collective-permute-start.16 = (bf16[32,4096]{1,0:T(8,128)(2,1)S(1)}, bf16[32,4096]{1,0:T(8,128)(2,1)S(1)}, u32[]{:S(2)}, u32[]{:S(2)}) collective-permute-start(bf16[32,4096]{1,0:T(8,128)(2,1)S(1)} %constant_dynamic-update-slice_fusion.2.refs_1_), channel_id=1, source_target_pairs={{0,8},{1,9},{2,10},{3,11},{4,12},{5,13},{6,14},{7,15},{8,16},{9,17... | collective-permute-start | bytes 786440 | tf_op jit(solution)/shard_map/ppermute | solution.py:33
  36.4 15.7 %collective-permute-start.18 = (bf16[64,4096]{1,0:T(8,128)(2,1)S(1)}, bf16[64,4096]{1,0:T(8,128)(2,1)S(1)}, u32[]{:S(2)}, u32[]{:S(2)}) collective-permute-start(bf16[64,4096]{1,0:T(8,128)(2,1)S(1)} %pad_maximum_fusion), channel_id=1, source_target_pairs={{0,1},{1,0},{2,3},{3,2},{4,5},{5,4},{6,7},{7,6},{8,9},{9,8},{10,11... | collective-permute-start | bytes 1572872 | tf_op jit(solution)/shard_map/ppermute | solution.py:33
  36.6 14.7 %collective-permute-start.2 = (bf16[32,4096]{1,0:T(8,128)(2,1)S(1)}, bf16[32,4096]{1,0:T(8,128)(2,1)S(1)}, u32[]{:S(2)}, u32[]{:S(2)}) collective-permute-start(bf16[32,4096]{1,0:T(8,128)(2,1)S(1)} %collective-permute-done.1.refs_4_), channel_id=1, source_target_pairs={{0,8},{1,9},{2,10},{3,11},{4,12},{5,13},{6,14},{7,15},{8,16},{9,17... | collective-permute-start | bytes 786440 | tf_op jit(solution)/shard_map/ppermute | solution.py:33
  39.8 11.5 %collective-permute-start.7 = (bf16[32,4096]{1,0:T(8,128)(2,1)S(1)}, bf16[32,4096]{1,0:T(8,128)(2,1)S(1)}, u32[]{:S(2)}, u32[]{:S(2)}) collective-permute-start(bf16[32,4096]{1,0:T(8,128)(2,1)S(1)} %collective-permute-done.6.refs_9_), channel_id=1, source_target_pairs={{0,24},{1,25},{2,26},{3,27},{4,28},{5,29},{6,30},{7,31},{8,0},{9,1... | collective-permute-start | bytes 786440 | tf_op jit(solution)/shard_map/ppermute | solution.py:33
  51.3 6.2 %collective-permute-start.8 = (bf16[32,4096]{1,0:T(8,128)(2,1)S(1)}, bf16[32,4096]{1,0:T(8,128)(2,1)S(1)}, u32[]{:S(2)}, u32[]{:S(2)}) collective-permute-start(bf16[32,4096]{1,0:T(8,128)(2,1)S(1)} %collective-permute-done.2.refs_0_.refs_12_), channel_id=1, source_target_pairs={{0,1},{1,0},{2,3},{3,2},{4,5},{5,4},{6,7},{7,6},{8,9},{9,8},{10,11... | collective-permute-start | bytes 786440 | tf_op jit(solution)/shard_map/ppermute | solution.py:33
  51.3 6.2 %collective-permute-start.9 = (bf16[32,4096]{1,0:T(8,128)(2,1)S(1)}, bf16[32,4096]{1,0:T(8,128)(2,1)S(1)}, u32[]{:S(2)}, u32[]{:S(2)}) collective-permute-start(bf16[32,4096]{1,0:T(8,128)(2,1)S(1)} %collective-permute-done.7.refs_1_.refs_13_), channel_id=1, source_target_pairs={{0,1},{1,0},{2,3},{3,2},{4,5},{5,4},{6,7},{7,6},{8,9},{9,8},{10,11... | collective-permute-start | bytes 786440 | tf_op jit(solution)/shard_map/ppermute | solution.py:33
  63.2 8.5 %collective-permute-start.22 = (bf16[256,128]{1,0:T(8,128)(2,1)S(1)}, bf16[256,128]{1,0:T(8,128)(2,1)S(1)}, u32[]{:S(2)}, u32[]{:S(2)}) collective-permute-start(bf16[256,128]{1,0:T(8,128)(2,1)S(1)} %conv_states.1), channel_id=1, source_target_pairs={{0,4},{1,5},{2,6},{3,7},{4,0},{5,1},{6,2},{7,3},{8,12},{9,13},{10,... | collective-permute-start | bytes 196616 | tf_op jit(solution)/shard_map/ppermute | solution.py:33
  71.8 8.6 %collective-permute-start.24 = (bf16[4,256,128]{2,1,0:T(8,128)(2,1)S(1)}, bf16[4,256,128]{2,1,0:T(8,128)(2,1)S(1)}, u32[]{:S(2)}, u32[]{:S(2)}) collective-permute-start(bf16[4,256,128]{2,1,0:T(8,128)(2,1)S(1)} %pad_maximum_fusion.2.own_ref), channel_id=1, source_target_pairs={{0,1},{1,0},{2,3},{3,2},{4,5},{5,4},{6,7},{7,6},{8,9},{9,8},{10,11... | collective-permute-start | bytes 786440 | tf_op jit(solution)/shard_map/ppermute | solution.py:33
  81.7 7.5 %collective-permute-start.27 = (f16[272,128]{1,0:T(8,128)(2,1)S(1)}, f16[272,128]{1,0:T(8,128)(2,1)S(1)}, u32[]{:S(2)}, u32[]{:S(2)}) collective-permute-start(f16[272,128]{1,0:T(8,128)(2,1)S(1)} %get-tuple-element.76), channel_id=1, source_target_pairs={{0,96},{32,64},{64,32},{96,0},{128,224},{160,192},{192,160},{224,1... | collective-permute-start | bytes 208904 | tf_op jit(solution)/shard_map/ppermute | solution.py:33
  90.0 12.2 %collective-permute-start.28 = (f16[272,128]{1,0:T(8,128)(2,1)S(1)}, f16[272,128]{1,0:T(8,128)(2,1)S(1)}, u32[]{:S(2)}, u32[]{:S(2)}) collective-permute-start(f16[272,128]{1,0:T(8,128)(2,1)S(1)} %convert_element_type.201), channel_id=1, source_target_pairs={{0,128},{32,160},{64,192},{96,224},{128,0},{160,32},{192,64},{224,... | collective-permute-start | bytes 208904 | tf_op jit(solution)/shard_map/ppermute | solution.py:33
  129.2 10.4 %collective-permute-start.35 = (bf16[192,4096]{1,0:T(8,128)(2,1)S(1)}, bf16[192,4096]{1,0:T(8,128)(2,1)S(1)}, u32[]{:S(2)}, u32[]{:S(2)}) collective-permute-start(bf16[192,4096]{1,0:T(8,128)(2,1)S(1)} %get-tuple-element.54), channel_id=1, source_target_pairs={{0,1},{1,0},{2,3},{3,2},{4,5},{5,4},{6,7},{7,6},{8,9},{9,8},{10,11... | collective-permute-start | bytes 4718600 | tf_op jit(solution)/shard_map/ppermute | solution.py:33
  130.0 9.5 %collective-permute-start.37 = (f16[32,4096]{1,0:T(8,128)(2,1)S(1)}, f16[32,4096]{1,0:T(8,128)(2,1)S(1)}, u32[]{:S(2)}, u32[]{:S(2)}) collective-permute-start(f16[32,4096]{1,0:T(8,128)(2,1)S(1)} %get-tuple-element.69), channel_id=1, source_target_pairs={{0,8},{1,9},{2,10},{3,11},{4,12},{5,13},{6,14},{7,15},{8,16},{9,17... | collective-permute-start | bytes 786440 | tf_op jit(solution)/shard_map/ppermute | solution.py:33
  130.1 9.5 %collective-permute-start.39 = (f16[32,4096]{1,0:T(8,128)(2,1)S(1)}, f16[32,4096]{1,0:T(8,128)(2,1)S(1)}, u32[]{:S(2)}, u32[]{:S(2)}) collective-permute-start(f16[32,4096]{1,0:T(8,128)(2,1)S(1)} %get-tuple-element.70), channel_id=1, source_target_pairs={{0,24},{1,25},{2,26},{3,27},{4,28},{5,29},{6,30},{7,31},{8,0},{9,1... | collective-permute-start | bytes 786440 | tf_op jit(solution)/shard_map/ppermute | solution.py:33
  140.3 9.7 %collective-permute-start.45 = (f16[64,2048]{1,0:T(8,128)(2,1)S(1)}, f16[64,2048]{1,0:T(8,128)(2,1)S(1)}, u32[]{:S(2)}, u32[]{:S(2)}) collective-permute-start(f16[64,2048]{1,0:T(8,128)(2,1)S(1)} %get-tuple-element.58), channel_id=1, source_target_pairs={{0,24},{1,25},{2,26},{3,27},{4,28},{5,29},{6,30},{7,31},{8,0},{9,1... | collective-permute-start | bytes 786440 | tf_op jit(solution)/shard_map/ppermute | solution.py:33
  143.3 10.4 %collective-permute-start.44 = (f16[64,2048]{1,0:T(8,128)(2,1)S(1)}, f16[64,2048]{1,0:T(8,128)(2,1)S(1)}, u32[]{:S(2)}, u32[]{:S(2)}) collective-permute-start(f16[64,2048]{1,0:T(8,128)(2,1)S(1)} %get-tuple-element.59), channel_id=1, source_target_pairs={{0,8},{1,9},{2,10},{3,11},{4,12},{5,13},{6,14},{7,15},{8,16},{9,17... | collective-permute-start | bytes 786440 | tf_op jit(solution)/shard_map/ppermute | solution.py:33
  143.3 15.0 %collective-permute-start.40 = (f16[64,2048]{1,0:T(8,128)(2,1)S(1)}, f16[64,2048]{1,0:T(8,128)(2,1)S(1)}, u32[]{:S(2)}, u32[]{:S(2)}) collective-permute-start(f16[64,2048]{1,0:T(8,128)(2,1)S(1)} %get-tuple-element.61), channel_id=1, source_target_pairs={{0,24},{1,25},{2,26},{3,27},{4,28},{5,29},{6,30},{7,31},{8,0},{9,1... | collective-permute-start | bytes 786440 | tf_op jit(solution)/shard_map/ppermute | solution.py:33
  146.5 11.8 %collective-permute-start.38 = (f16[64,2048]{1,0:T(8,128)(2,1)S(1)}, f16[64,2048]{1,0:T(8,128)(2,1)S(1)}, u32[]{:S(2)}, u32[]{:S(2)}) collective-permute-start(f16[64,2048]{1,0:T(8,128)(2,1)S(1)} %get-tuple-element.57), channel_id=1, source_target_pairs={{0,8},{1,9},{2,10},{3,11},{4,12},{5,13},{6,14},{7,15},{8,16},{9,17... | collective-permute-start | bytes 786440 | tf_op jit(solution)/shard_map/ppermute | solution.py:33
  153.8 7.0 %collective-permute-start.48 = (f16[16,2048]{1,0:T(8,128)(2,1)S(1)}, f16[16,2048]{1,0:T(8,128)(2,1)S(1)}, u32[]{:S(2)}, u32[]{:S(2)}) collective-permute-start(f16[16,2048]{1,0:T(8,128)(2,1)S(1)} %get-tuple-element.67), channel_id=1, source_target_pairs={{0,6},{1,7},{2,4},{3,5},{4,2},{5,3},{6,0},{7,1},{8,14},{9,15},{10,... | collective-permute-start | bytes 196616 | tf_op jit(solution)/shard_map/ppermute | solution.py:33
  155.8 7.7 %collective-permute-start.47 = (f16[16,2048]{1,0:T(8,128)(2,1)S(1)}, f16[16,2048]{1,0:T(8,128)(2,1)S(1)}, u32[]{:S(2)}, u32[]{:S(2)}) collective-permute-start(f16[16,2048]{1,0:T(8,128)(2,1)S(1)} %get-tuple-element.68), channel_id=1, source_target_pairs={{0,4},{1,5},{2,6},{3,7},{4,0},{5,1},{6,2},{7,3},{8,12},{9,13},{10,... | collective-permute-start | bytes 196616 | tf_op jit(solution)/shard_map/ppermute | solution.py:33
  155.8 7.7 %collective-permute-start.46 = (f16[16,2048]{1,0:T(8,128)(2,1)S(1)}, f16[16,2048]{1,0:T(8,128)(2,1)S(1)}, u32[]{:S(2)}, u32[]{:S(2)}) collective-permute-start(f16[16,2048]{1,0:T(8,128)(2,1)S(1)} %get-tuple-element.66), channel_id=1, source_target_pairs={{0,2},{1,3},{2,0},{3,1},{4,6},{5,7},{6,4},{7,5},{8,10},{9,11},{10,... | collective-permute-start | bytes 196616 | tf_op jit(solution)/shard_map/ppermute | solution.py:33
  158.4 6.3 %collective-permute-start.43 = (f16[16,2048]{1,0:T(8,128)(2,1)S(1)}, f16[16,2048]{1,0:T(8,128)(2,1)S(1)}, u32[]{:S(2)}, u32[]{:S(2)}) collective-permute-start(f16[16,2048]{1,0:T(8,128)(2,1)S(1)} %get-tuple-element.64), channel_id=1, source_target_pairs={{0,6},{1,7},{2,4},{3,5},{4,2},{5,3},{6,0},{7,1},{8,14},{9,15},{10,... | collective-permute-start | bytes 196616 | tf_op jit(solution)/shard_map/ppermute | solution.py:33
  (26 other events, 248.4 us)
